TPU v7x, 32 devices: a whole 2x2x4 slice. The times are simulated.
32 devices in a mesh: band: 16 (over z, y, x), member: 2 (over core).
Axes of the slice: x: 2, y: 2, z: 4, core: 2. Of those that a mesh axis runs over, the one named last changes fastest.
Arguments:
- scaled_atmosphere_field: float32 [80, 4096], P(None, 'band'), may hold values from -6 to 6
- perturbation: bfloat16 [2, 80, 4096], P('member', None, 'band'), may hold values from -6 to 6
- target: bfloat16 [2, 80, 4096], P('member', None, 'band'), may hold values from -6 to 6
- weight_map: bfloat16 [80, 4096], P(None, 'band'), may hold values from 0.01 to 10
- enc_send: int32 [16, 16, 32], P('band'), may hold values from -1 to 255, as said below
- enc_recv: int32 [16, 16, 32], P('band'), may hold values from -1 to 255, as said below
- dec_send: int32 [16, 16, 32], P('band'), may hold values from -1 to 255, as said below
- dec_recv: int32 [16, 16, 32], P('band'), may hold values from -1 to 255, as said below
- lattice_lift_matrix: bfloat16 [80, 512], replicated, may hold values from -0.625 to 0.625
- mixing_rescale_factor: float32 [512], replicated, may hold values from 0.1 to 1.9
- expand_matrix: bfloat16 [512, 512], replicated, may hold values from -0.25 to 0.25
- contract_matrix: bfloat16 [512, 512], replicated, may hold values from -0.25 to 0.25
- readout_matrix: bfloat16 [512, 80], replicated, may hold values from -0.25 to 0.25
Outputs:
- student_outputs: float32 [2, 80, 4096], P('member', None, 'band')
- mesh_grad: bfloat16 [2, 4096, 512], P('member', 'band')
- grad_up: float32 [2, 512, 512], P('member')
- grad_down: float32 [2, 512, 512], P('member')
- grad_dec: float32 [2, 512, 80], P('member')
- grad_gain: float32 [2, 512], P('member')
Inputs may be any that keep to these rules, and one draw needn't show every extreme that they name: enc_send[s, d, k] is a local grid cell of band s (0 to 255) or -1 for an empty slot; in every draw one band fills all its slots and one partition receives full blocks of 32 from every band. enc_recv[d, s, k] is a local mesh node of partition d, and -1 exactly where enc_send[s, d, k] is -1. dec_send[s, d, k] is a local mesh node of partition s or -1 for an empty slot; in every draw one partition fills all its slots and one band receives full blocks of 32 from every partition. dec_recv[d, s, k] is a local grid cell of band d, and -1 exactly where dec_send[s, d, k] is -1.
All inputs are finite; a program needn't handle non-finite values.
Results may differ from a plain program's by a relative error of at most 0.0062.
Values may be sent and summed in bfloat16 or wider, within the bound.
No kernel may reach another device: no remote copies, remote signals or barrier semaphores. Data moves between devices by JAX's collectives and lax.ppermute only.
A program may use at most 64 MiB of HBM per device.

v0:
```python
import math

import jax
import jax.numpy as jnp
from jax import lax
from jax.sharding import PartitionSpec as P

MESH_DEV = 256


smooth_sq = 0.01
norm_eps = 1e-05


def slope(diff):
    return diff * lax.rsqrt(diff * diff + smooth_sq)


def embed_columns(columns, lattice_lift_matrix):
    pre_act = lax.dot_general(
        columns, lattice_lift_matrix, (((0,), (0,)), ((), ())), preferred_element_type=jnp.float32
    )
    return jax.nn.silu(pre_act).astype(jnp.bfloat16)


def body(
    scaled_atmosphere_field,
    perturbation,
    target,
    weight_map,
    enc_send,
    enc_recv,
    dec_send,
    dec_recv,
    lattice_lift_matrix,
    mixing_rescale_factor,
    expand_matrix,
    contract_matrix,
    readout_matrix,
):
    highest = lax.Precision.HIGHEST
    band_count = lax.axis_size("band")
    channels, grid_rows = scaled_atmosphere_field.shape
    width = lattice_lift_matrix.shape[1]
    node_rows = MESH_DEV
    enc_width = enc_send.shape[2]
    dec_width = dec_send.shape[2]
    cell_ids = jnp.arange(grid_rows, dtype=jnp.int32)
    node_ids = jnp.arange(node_rows, dtype=jnp.int32)
    inputs_b = (scaled_atmosphere_field + perturbation[0].astype(jnp.float32)).astype(jnp.bfloat16)
    send_index = enc_send[0].reshape(-1)
    picker = (send_index[:, None] == cell_ids[None, :]).astype(jnp.bfloat16)
    latent = embed_columns(inputs_b, lattice_lift_matrix)
    outgoing = jnp.dot(picker, latent, preferred_element_type=jnp.float32).astype(jnp.bfloat16)
    arrived = lax.all_to_all(
        outgoing.reshape(band_count, enc_width, width),
        "band",
        split_axis=0,
        concat_axis=0,
        tiled=True,
    )
    slot_rows = arrived.reshape(-1, width)
    recv_index = enc_recv[0].reshape(-1)
    landing = (node_ids[:, None] == recv_index[None, :]).astype(jnp.bfloat16)
    summed = jnp.dot(landing, slot_rows, preferred_element_type=jnp.float32)
    edge_count = jnp.sum(landing.astype(jnp.float32), axis=1, keepdims=True)
    mesh_state = summed / jnp.maximum(edge_count, 1.0)
    recip = lax.rsqrt(jnp.mean(mesh_state * mesh_state, axis=1, keepdims=True) + norm_eps)
    normed_b = (mesh_state * recip * mixing_rescale_factor).astype(jnp.bfloat16)
    hidden_pre = jnp.dot(normed_b, expand_matrix, preferred_element_type=jnp.float32)
    hidden_b = jax.nn.silu(hidden_pre).astype(jnp.bfloat16)
    mesh_next = mesh_state + jnp.dot(hidden_b, contract_matrix, preferred_element_type=jnp.float32)
    next_b = mesh_next.astype(jnp.bfloat16)
    dec_index = dec_send[0].reshape(-1)
    mesh_picker = (dec_index[:, None] == node_ids[None, :]).astype(jnp.bfloat16)
    cell_index = dec_recv[0].reshape(-1)
    fill_map = (cell_ids[:, None] == cell_index[None, :]).astype(jnp.bfloat16)
    grid_count = jnp.sum(fill_map.astype(jnp.float32), axis=1)
    inverse = 1.0 / jnp.maximum(grid_count, 1.0)
    projected = lax.dot_general(
        readout_matrix, next_b, (((0,), (1,)), ((), ())), preferred_element_type=jnp.float32
    ).astype(jnp.bfloat16)
    chosen = lax.dot_general(
        projected, mesh_picker, (((1,), (1,)), ((), ())), preferred_element_type=jnp.float32
    ).astype(jnp.bfloat16)
    slot_values = lax.all_to_all(
        chosen.reshape(channels, band_count, dec_width),
        "band",
        split_axis=1,
        concat_axis=1,
        tiled=True,
    ).reshape(channels, -1)
    grid_sum = lax.dot_general(
        slot_values, fill_map, (((1,), (1,)), ((), ())), preferred_element_type=jnp.float32
    )
    student_outputs = scaled_atmosphere_field + grid_sum * inverse[None, :]
    all_pred, all_target = (
        lax.all_gather(student_outputs[None], "member", axis=0, tiled=True),
        lax.all_gather(target.astype(jnp.float32), "member", axis=0, tiled=True),
    )
    teacher_terms = jnp.sum(slope(student_outputs[None] - all_target), axis=0)
    own_terms = jnp.sum(slope(student_outputs[None] - all_pred), axis=0)
    pred_grad = weight_map.astype(jnp.float32) * (teacher_terms - own_terms)
    scaled = pred_grad * inverse[None, :]
    slot_grad = jnp.dot(scaled, fill_map.astype(jnp.float32), precision=highest)
    dec_f32 = readout_matrix.astype(jnp.float32)
    picker_f32 = mesh_picker.astype(jnp.float32)
    returned = lax.all_to_all(
        slot_grad.reshape(channels, band_count, dec_width),
        "band",
        split_axis=1,
        concat_axis=1,
        tiled=True,
    ).reshape(channels, -1)
    node_grad = jnp.dot(returned, picker_f32, precision=highest)
    next_grad = lax.dot_general(node_grad, dec_f32, (((0,), (1,)), ((), ())), precision=highest)
    dec_part = lax.dot_general(
        next_b.astype(jnp.float32), node_grad, (((0,), (1,)), ((), ())), precision=highest
    )
    down_part = lax.dot_general(
        hidden_b.astype(jnp.float32), next_grad, (((0,), (0,)), ((), ())), precision=highest
    )
    hidden_grad = lax.dot_general(
        next_grad, contract_matrix.astype(jnp.float32), (((1,), (1,)), ((), ())), precision=highest
    )
    sigma = jax.nn.sigmoid(hidden_pre)
    pre_grad = hidden_grad * sigma * (1.0 + hidden_pre * (1.0 - sigma))
    up_part = lax.dot_general(
        normed_b.astype(jnp.float32), pre_grad, (((0,), (0,)), ((), ())), precision=highest
    )
    normed_grad = lax.dot_general(
        pre_grad, expand_matrix.astype(jnp.float32), (((1,), (1,)), ((), ())), precision=highest
    )
    gain_part = jnp.sum(normed_grad * mesh_state * recip, axis=0)
    gained = normed_grad * mixing_rescale_factor
    state_grad = (
        next_grad
        + recip * gained
        - mesh_state
        * (recip * recip * recip)
        * jnp.mean(gained * mesh_state, axis=1, keepdims=True)
    )
    up_sum, down_sum, dec_sum, gain_sum = lax.psum(
        (up_part, down_part, dec_part, gain_part), "band"
    )
    factor = 1.0 / math.sqrt(band_count * node_rows)
    return (
        student_outputs[None],
        state_grad.astype(jnp.bfloat16)[None],
        (up_sum * factor)[None],
        (down_sum * factor)[None],
        (dec_sum * factor)[None],
        (gain_sum * factor)[None],
    )


def solution(mesh):
    return jax.shard_map(
        body,
        mesh=mesh,
        in_specs=(
            P(None, "band"),
            P("member", None, "band"),
            P("member", None, "band"),
            P(None, "band"),
            P("band", None, None),
            P("band", None, None),
            P("band", None, None),
            P("band", None, None),
            P(),
            P(),
            P(),
            P(),
            P(),
        ),
        out_specs=(
            P("member", None, "band"),
            P("member", "band", None),
            P("member", None, None),
            P("member", None, None),
            P("member", None, None),
            P("member", None),
        ),
        check_vma=False,
    )
```

profile of v0, /device:TPU:0, one launch (start us, length us, event | category | flops | bytes accessed | tf_op | source)
XLA Modules:
  0.0 213.1 jit_solution(13352040407852293177)
XLA Ops:
  7.2 0.8 eq.64
  8.0 2.4 %convolution_convert_fusion = bf16[512,512]{1,0:T(8,128)(2,1)} fusion(bf16[80,512]{1,0:T(8,128)(2,1)} %param.21, s32[512]{0:T(512)S(1)} %eq.64, f32[80,256]{1,0:T(8,128)} %param.13, bf16[1,80,256]{2,1,0:T(8,128)(2,1)} %param.14), kind=kOutput, calls=%fused_computation | convolution fusion | flops 156299264 | bytes 731136 | tf_op jit(solution)/shard_map/dot_general | solution.py:54
  10.4 8.5 %all-to-all-start = ((bf16[16,32,512]{2,1,0:T(8,128)(2,1)}), bf16[16,32,512]{2,1,0:T(8,128)(2,1)S(1)}, u32[]{:S(2)}, u32[]{:S(2)}) async-start(bf16[16,32,512]{2,1,0:T(8,128)(2,1)} %bitcast.1), calls=%async_computation | async-start | bytes 1048576 | tf_op jit(solution)/shard_map/all_to_all | solution.py:55
  19.7 1.9 all_gather.6
  21.9 12.0 %all-to-all-done = bf16[16,32,512]{2,1,0:T(8,128)(2,1)S(1)} async-done(((bf16[16,32,512]{2,1,0:T(8,128)(2,1)}), bf16[16,32,512]{2,1,0:T(8,128)(2,1)S(1)}, u32[]{:S(2)}, u32[]{:S(2)}) %all-to-all-start) | async-done | bytes 524320 | tf_op jit(solution)/shard_map/all_to_all | solution.py:55
  34.4 0.7 copy-done.5
  35.4 0.7 copy-done.9
  37.4 0.8 copy.23
  38.2 4.1 %all-to-all-start.1 = ((bf16[80,16,32]{0,2,1:T(8,128)(2,1)}), bf16[80,16,32]{0,2,1:T(8,128)(2,1)S(1)}, u32[]{:S(2)}, u32[]{:S(2)}) async-start(bf16[80,16,32]{0,2,1:T(8,128)(2,1)} %bitcast.3), calls=%async_computation.1 | async-start | bytes 262144 | tf_op jit(solution)/shard_map/all_to_all | solution.py:86
  42.3 7.7 %all-to-all-done.1 = bf16[80,16,32]{0,2,1:T(8,128)(2,1)S(1)} async-done(((bf16[80,16,32]{0,2,1:T(8,128)(2,1)}), bf16[80,16,32]{0,2,1:T(8,128)(2,1)S(1)}, u32[]{:S(2)}, u32[]{:S(2)}) %all-to-all-start.1) | async-done | bytes 81952 | tf_op jit(solution)/shard_map/all_to_all | solution.py:86
  50.3 1.9 all-gather
  52.3 0.7 copy-done.3
  53.0 0.6 fusion.3
  53.6 13.0 %all_to_all.15 = f32[80,16,32]{0,2,1:T(8,128)S(1)} all-to-all(f32[80,16,32]{0,2,1:T(8,128)S(1)} %bitcast.42), channel_id=1, replica_groups=mesh['band'=16,'member'=2] {'band'}, dimensions={1} | all-to-all | bytes 327680 | tf_op jit(solution)/shard_map/all_to_all | solution.py:108
  67.2 0.9 fusion.30
  68.5 0.7 fusion
  69.2 1.7 fusion.28
  70.9 1.7 fusion.26
  72.7 0.7 multiply_reduce_fusion
  73.4 40.0 %psum.31 = f32[512]{0:T(512)S(1)} all-reduce(f32[512]{0:T(512)S(1)} %get-tuple-element.6), channel_id=1, replica_groups=mesh['band'=16,'member'=2] {'band'}, use_global_device_ids=true, to_apply=%region_10.11 | all-reduce | flops 512 | bytes 4096 | tf_op jit(solution)/shard_map/psum | solution.py:143
  114.0 0.9 fusion.7
  114.8 86.7 %all-reduce.3.cloned.1.call-done = (f32[512,512]{1,0:T(8,128)}, f32[512,512]{1,0:T(8,128)}, f32[512,80]{0,1:T(8,128)}) async-done(((f32[512,512]{1,0:T(8,128)}, f32[512,512]{1,0:T(8,128)}, f32[512,80]{0,1:T(8,128)}), (f32[512,512]{1,0:T(8,128)}, f32[512,512]{1,0:T(8,128)}, f32[512,80]{0,1:T(8,128)})) %all-reduce.3.cloned.1.call-update) | async-done | bytes 2261008 | tf_op jit(solution)/shard_map/psum | solution.py:143
  201.6 1.6 multiply_bitcast_fusion.2
  203.2 3.1 %multiply_bitcast_fusion = (f32[1,512,512]{2,1,0:T(8,128)}, f32[1,512,512]{2,1,0:T(8,128)}) fusion(f32[512,512]{1,0:T(8,128)} %get-tuple-element.11, f32[512,512]{1,0:T(8,128)} %get-tuple-element.10), kind=kLoop, calls=%fused_computation.10 | loop fusion | flops 524288 | bytes 4194304 | tf_op jit(solution)/shard_map/broadcast_in_dim | solution.py:151
  (40 shorter events, 5.0 us)
Async XLA Ops:
  7.2 27.2 %copy-start = (bf16[512,512]{1,0:T(8,128)(2,1)S(1)}, bf16[512,512]{1,0:T(8,128)(2,1)}, u32[]{:S(2)}) copy-start(bf16[512,512]{1,0:T(8,128)(2,1)} %param.23) | copy-start | bytes 1572868
  10.4 8.5 %copy-start.6 = (s32[1,16,32]{2,1,0:T(8,128)S(1)}, s32[1,16,32]{2,1,0:T(8,128)}, u32[]{:S(2)}) copy-start(s32[1,16,32]{2,1,0:T(8,128)} %param.20) | copy-start | bytes 6148
  10.4 9.3 %copy-start.4 = (bf16[1,80,256]{2,1,0:T(8,128)(2,1)S(1)}, bf16[1,80,256]{2,1,0:T(8,128)(2,1)}, u32[]{:S(2)}) copy-start(bf16[1,80,256]{2,1,0:T(8,128)(2,1)} %param.15) | copy-start | bytes 122884
  10.4 23.6 %all-to-all-start = ((bf16[16,32,512]{2,1,0:T(8,128)(2,1)}), bf16[16,32,512]{2,1,0:T(8,128)(2,1)S(1)}, u32[]{:S(2)}, u32[]{:S(2)}) async-start(bf16[16,32,512]{2,1,0:T(8,128)(2,1)} %bitcast.1), calls=%async_computation | async-start | bytes 1048576 | tf_op jit(solution)/shard_map/all_to_all | solution.py:55
  18.9 0.7 copy-start.7
  18.9 0.8 copy-start.8
  34.3 0.7 copy-start.5
  35.0 1.0 copy-start.9
  36.1 0.9 copy-start.2
  38.2 11.9 %copy-start.10 = (f32[80,256]{1,0:T(8,128)S(1)}, f32[80,256]{1,0:T(8,128)}, u32[]{:S(2)}) copy-start(f32[80,256]{1,0:T(8,128)} %param.13) | copy-start | bytes 245764
  38.2 11.9 %all-to-all-start.1 = ((bf16[80,16,32]{0,2,1:T(8,128)(2,1)}), bf16[80,16,32]{0,2,1:T(8,128)(2,1)S(1)}, u32[]{:S(2)}, u32[]{:S(2)}) async-start(bf16[80,16,32]{0,2,1:T(8,128)(2,1)} %bitcast.3), calls=%async_computation.1 | async-start | bytes 262144 | tf_op jit(solution)/shard_map/all_to_all | solution.py:86
  42.3 159.3 %all-reduce.3.cloned.1.call-start = ((), (), s32[]{:S(2)}) async-start(), calls=%async_computation.3 | async-start | bytes 4521984 | tf_op jit(solution)/shard_map/psum | solution.py:143
  50.3 1.9 copy-start.1
  52.2 0.8 copy-start.3
Sparse Core Ops, SparseCore 0:
  72.8 128.7 all-reduce.2
where the time goes:
time: 214 us; the launch traced here: 213 us
  waiting for transfers between devices  106 us (50%)
  blocking collectives  56.9 us (27%)
  between operations  14.2 us (7%)
  starting transfers between devices  12.6 us (6%)
  matrix products  11.4 us (5%)
  other arithmetic  6.51 us (3%)
  local copies, waits for them, and re-layouts  5.08 us (2%)
    psum x1, waiting for transfers between devices, body(): lax.psum((up_part, down_part, dec_part, gain_part), 'band')  86.7 us
    psum x1, blocking collectives, body(): lax.psum((up_part, down_part, dec_part, gain_part), 'band')  40 us
    all_to_all x1, blocking collectives, body(): lax.all_to_all(slot_grad.reshape(channels, band_count, dec_width), 'band'...  13 us
    all_to_all x1, waiting for transfers between devices, body(): lax.all_to_all(outgoing.reshape(band_count, enc_width, width), 'band', sp...  12 us
    all_to_all x1, starting transfers between devices, body(): lax.all_to_all(outgoing.reshape(band_count, enc_width, width), 'band', sp...  8.47 us
    all_to_all x1, waiting for transfers between devices, body(): lax.all_to_all(chosen.reshape(channels, band_count, dec_width), 'band', s...  7.73 us
  transfers between devices with their start and end apart: 3, of which 3 were waited for; matrix products, arithmetic and copies ran while one was open for 1% of the time, Pallas kernels for 0%

commit v1 on v0

v1 whole, which is shorter than its diff:
```python
import math

import jax
import jax.numpy as jnp
from jax import lax
from jax.sharding import PartitionSpec as P

MESH_DEV = 256


smooth_sq = 0.01
norm_eps = 1e-05

bf16 = jnp.bfloat16
f32 = jnp.float32


def slope(diff):
    return diff * lax.rsqrt(diff * diff + smooth_sq)


def mm(a, b, ca, cb):
    return lax.dot_general(a, b, (((ca,), (cb,)), ((), ())), preferred_element_type=f32)


def split3(x):
    hi = x.astype(bf16)
    return hi, (x - hi.astype(f32)).astype(bf16)


def mm2(a, b, ca, cb):
    hi, lo = split3(a)
    return mm(hi, b, ca, cb) + mm(lo, b, ca, cb)


def exchange(x, band_count):
    rows, width = x.shape
    y = lax.all_to_all(
        x.reshape(band_count, rows // band_count, width), "band", split_axis=0, concat_axis=0, tiled=True
    )
    return y.reshape(rows, width)


def sum_over_bands(x, band_count):
    rows, width = x.shape
    parts = lax.all_to_all(
        x.astype(bf16).reshape(band_count, rows // band_count, width),
        "band",
        split_axis=0,
        concat_axis=0,
        tiled=True,
    )
    own = jnp.sum(parts.astype(f32), axis=0).astype(bf16)
    spread = jnp.broadcast_to(own[None], parts.shape)
    full = lax.all_to_all(spread, "band", split_axis=0, concat_axis=0, tiled=True)
    return full.reshape(rows, width).astype(f32)


def body(
    scaled_atmosphere_field,
    perturbation,
    target,
    weight_map,
    enc_send,
    enc_recv,
    dec_send,
    dec_recv,
    lattice_lift_matrix,
    mixing_rescale_factor,
    expand_matrix,
    contract_matrix,
    readout_matrix,
):
    band_count = lax.axis_size("band")
    channels, grid_rows = scaled_atmosphere_field.shape
    node_rows = MESH_DEV
    cell_ids = jnp.arange(grid_rows, dtype=jnp.int32)
    node_ids = jnp.arange(node_rows, dtype=jnp.int32)
    inputs_b = (scaled_atmosphere_field + perturbation[0].astype(f32)).astype(bf16)
    picker = (enc_send[0].reshape(-1)[:, None] == cell_ids[None, :]).astype(bf16)
    outgoing = mm(picker, inputs_b, 1, 1).astype(bf16)
    arrived = exchange(outgoing, band_count)
    slot_rows = jax.nn.silu(mm(arrived, lattice_lift_matrix, 1, 0)).astype(bf16)
    landing = (node_ids[:, None] == enc_recv[0].reshape(-1)[None, :]).astype(bf16)
    edge_count = jnp.sum(landing.astype(f32), axis=1, keepdims=True)
    mesh_state = mm(landing, slot_rows, 1, 0) / jnp.maximum(edge_count, 1.0)
    recip = lax.rsqrt(jnp.mean(mesh_state * mesh_state, axis=1, keepdims=True) + norm_eps)
    normed_b = (mesh_state * recip * mixing_rescale_factor).astype(bf16)
    hidden_pre = mm(normed_b, expand_matrix, 1, 0)
    hidden_b = jax.nn.silu(hidden_pre).astype(bf16)
    next_b = (mesh_state + mm(hidden_b, contract_matrix, 1, 0)).astype(bf16)
    mesh_picker = (dec_send[0].reshape(-1)[:, None] == node_ids[None, :]).astype(bf16)
    fill_map = (cell_ids[:, None] == dec_recv[0].reshape(-1)[None, :]).astype(bf16)
    inverse = 1.0 / jnp.maximum(jnp.sum(fill_map.astype(f32), axis=1), 1.0)
    projected = mm(next_b, readout_matrix, 1, 0).astype(bf16)
    chosen = mm(mesh_picker, projected, 1, 0).astype(bf16)
    slot_values = exchange(chosen, band_count)
    grid_sum = mm(slot_values, fill_map, 0, 1)
    student_outputs = scaled_atmosphere_field + grid_sum * inverse[None, :]
    all_pred, all_target = (
        lax.all_gather(student_outputs[None], "member", axis=0, tiled=True),
        lax.all_gather(target, "member", axis=0, tiled=True),
    )
    teacher_terms = jnp.sum(slope(student_outputs[None] - all_target.astype(f32)), axis=0)
    own_terms = jnp.sum(slope(student_outputs[None] - all_pred), axis=0)
    pred_grad = weight_map.astype(f32) * (teacher_terms - own_terms)
    scaled = (pred_grad * inverse[None, :]).astype(bf16)
    slot_grad = mm(fill_map, scaled, 0, 1).astype(bf16)
    returned = exchange(slot_grad, band_count)
    node_grad = mm(mesh_picker, returned, 0, 0)
    next_grad = mm2(node_grad, readout_matrix, 1, 1)
    grad_hi, grad_lo = split3(node_grad)
    states = jnp.concatenate([next_b, hidden_b], axis=1)
    small = mm(states, grad_hi, 0, 0) + mm(states, grad_lo, 0, 0)
    hidden_grad = mm2(next_grad, contract_matrix, 1, 1)
    sigma = jax.nn.sigmoid(hidden_pre)
    pre_grad = hidden_grad * sigma * (1.0 + hidden_pre * (1.0 - sigma))
    pre_hi, pre_lo = split3(pre_grad)
    up_part = mm(normed_b, pre_hi, 0, 0) + mm(normed_b, pre_lo, 0, 0)
    normed_grad = mm(pre_hi, expand_matrix, 1, 1) + mm(pre_lo, expand_matrix, 1, 1)
    gain_part = jnp.sum(normed_grad * mesh_state * recip, axis=0)
    gained = normed_grad * mixing_rescale_factor
    state_grad = (
        next_grad
        + recip * gained
        - mesh_state
        * (recip * recip * recip)
        * jnp.mean(gained * mesh_state, axis=1, keepdims=True)
    )
    width = up_part.shape[0]
    factor = 1.0 / math.sqrt(band_count * node_rows)
    packed = jnp.concatenate(
        [up_part, small[:width], small[width:], gain_part[:, None]], axis=1
    )
    pad = -packed.shape[1] % 16
    packed = jnp.pad(packed, ((0, 0), (0, pad)))
    total = sum_over_bands(packed, band_count) * factor
    hid = up_part.shape[1]
    grad_up = total[:, :hid]
    grad_dec = total[:, hid : hid + channels]
    hid_sum = total[:, hid + channels : hid + 2 * channels]
    grad_gain = total[:, hid + 2 * channels]
    grad_down = mm2(hid_sum, readout_matrix, 1, 1)
    return (
        student_outputs[None],
        state_grad.astype(bf16)[None],
        grad_up[None],
        grad_down[None],
        grad_dec[None],
        grad_gain[None],
    )


def solution(mesh):
    return jax.shard_map(
        body,
        mesh=mesh,
        in_specs=(
            P(None, "band"),
            P("member", None, "band"),
            P("member", None, "band"),
            P(None, "band"),
            P("band", None, None),
            P("band", None, None),
            P("band", None, None),
            P("band", None, None),
            P(),
            P(),
            P(),
            P(),
            P(),
        ),
        out_specs=(
            P("member", None, "band"),
            P("member", "band", None),
            P("member", None, None),
            P("member", None, None),
            P("member", None, None),
            P("member", None),
        ),
        check_vma=False,
    )
```

time: 214 us -> 107 us (0.50)
  waiting for transfers between devices: 106 us -> 29 us
  blocking collectives: 56.9 us -> 38.5 us
  between operations: 14.2 us -> 0.92 us
  other arithmetic: 6.51 us -> 1.7 us
  local copies, waits for them, and re-layouts: 5.08 us -> 9.12 us
  starting transfers between devices: 12.6 us -> 15.8 us
    psum x1 -> x0, waiting for transfers between devices: 86.7 us -> none  [body(): lax.psum((up_part, down_part, dec_part, gain_part), 'band')]
    psum x1 -> x0, blocking collectives: 40 us -> none  [body(): lax.psum((up_part, down_part, dec_part, gain_part), 'band')]
    all_to_all x1 -> x2, blocking collectives: 13 us -> 34.5 us  [the longest x1 23.8 us: sum_over_bands(): lax.all_to_all(x.astype(bf16).reshape(band_count, rows // band_count, wid...]
    all_to_all x2 -> x3, waiting for transfers between devices: 19.7 us -> 29 us  [the longest x1 18.1 us: sum_over_bands(): lax.all_to_all(spread, 'band', split_axis=0, concat_axis=0, tiled=True)]
    broadcast_in_dim x3 -> x1, other arithmetic: 5.56 us -> 0.88 us  [body(): state_grad.astype(bf16)[None]]
    all_to_all x2 -> x3, starting transfers between devices: 12.5 us -> 15.8 us  [the longest x2 12.1 us: exchange(): lax.all_to_all(x.reshape(band_count, rows // band_count, width), 'band',...]
    dot_general x14 -> x20, matrix products: 11.4 us -> 10.9 us  [mm(): lax.dot_general(a, b, (((ca,), (cb,)), ((), ())), preferred_element_type=...]
  transfers between devices with their start and end apart: 3 -> 3, of which waited for: 3 -> 3; matrix products, arithmetic and copies ran while one was open for 1% -> 3% of each run, Pallas kernels for 0% -> 0%
where the time goes in v1:
time: 107 us; the launch traced here: 106 us
  blocking collectives  38.5 us (36%)
  waiting for transfers between devices  29 us (27%)
  starting transfers between devices  15.8 us (15%)
  matrix products  10.9 us (10%)
  local copies, waits for them, and re-layouts  9.12 us (9%)
  other arithmetic  1.7 us (2%)
    all_to_all x1, blocking collectives, sum_over_bands(): lax.all_to_all(x.astype(bf16).reshape(band_count, rows // band_count, wid...  23.8 us
    all_to_all x1, waiting for transfers between devices, sum_over_bands(): lax.all_to_all(spread, 'band', split_axis=0, concat_axis=0, tiled=True)  18.1 us
    all_to_all x2, starting transfers between devices, exchange(): lax.all_to_all(x.reshape(band_count, rows // band_count, width), 'band',...  12.1 us
    all_to_all x2, waiting for transfers between devices, exchange(): lax.all_to_all(x.reshape(band_count, rows // band_count, width), 'band',...  10.9 us
    dot_general x20, matrix products, mm(): lax.dot_general(a, b, (((ca,), (cb,)), ((), ())), preferred_element_type=...  10.9 us
    all_to_all x1, blocking collectives, exchange(): lax.all_to_all(x.reshape(band_count, rows // band_count, width), 'band',...  10.7 us
    all_to_all x1, starting transfers between devices, sum_over_bands(): lax.all_to_all(spread, 'band', split_axis=0, concat_axis=0, tiled=True)  3.61 us
  transfers between devices with their start and end apart: 3, of which 3 were waited for; matrix products, arithmetic and copies ran while one was open for 3% of the time, Pallas kernels for 0%

profile of v1, /device:TPU:0, one launch (start us, length us, event | category | flops | bytes accessed | tf_op | source)
XLA Modules:
  0.0 105.9 jit_solution(4076135577425341925)
XLA Ops:
  0.6 0.8 eq.68
  1.5 1.2 %convolution_convert_fusion.2 = bf16[512,80]{0,1:T(8,128)(2,1)S(1)} fusion(s32[512]{0:T(512)S(1)} %eq.68, f32[80,256]{1,0:T(8,128)} %param.13, bf16[1,80,256]{2,1,0:T(8,128)(2,1)} %param.14), kind=kOutput, calls=%fused_computation.17 | convolution fusion | flops 21204992 | bytes 206848 | tf_op jit(solution)/shard_map/dot_general | solution.py:23
  3.4 8.3 %all-to-all-start = ((bf16[16,32,80]{2,1,0:T(8,128)(2,1)}), bf16[16,32,80]{2,1,0:T(8,128)(2,1)S(1)}, u32[]{:S(2)}, u32[]{:S(2)}) async-start(bf16[16,32,80]{2,1,0:T(8,128)(2,1)} %bitcast.1), calls=%async_computation | async-start | bytes 262144 | tf_op jit(solution)/shard_map/all_to_all | solution.py:38
  11.8 0.8 eq.65
  12.7 0.8 eq.73
  13.5 0.8 eq.60
  14.2 2.1 %all_gather.6 = bf16[2,80,256]{2,1,0:T(8,128)(2,1)S(1)} all-gather(bf16[1,80,256]{2,1,0:T(8,128)(2,1)} %param.15), channel_id=1, replica_groups=mesh['band'=16,'member'=2] {'member'}, dimensions={0}, use_global_device_ids=true | all-gather | bytes 122880 | tf_op jit(solution)/shard_map/all_gather | solution.py:102
  16.4 3.1 %all-to-all-done = bf16[16,32,80]{2,1,0:T(8,128)(2,1)S(1)} async-done(((bf16[16,32,80]{2,1,0:T(8,128)(2,1)}), bf16[16,32,80]{2,1,0:T(8,128)(2,1)S(1)}, u32[]{:S(2)}, u32[]{:S(2)}) %all-to-all-start) | async-done | bytes 81952 | tf_op jit(solution)/shard_map/all_to_all | solution.py:38
  19.6 1.6 %multiply_reduce_fusion.2 = (f32[256]{0:T(256)S(1)}, f32[256,512]{1,0:T(8,128)S(1)}) fusion(f32[256]{0:T(256)S(1)} %broadcast_maximum_fusion, bf16[512,80]{1,0:T(8,128)(2,1)S(1)} %bitcast.54, bf16[80,512]{1,0:T(8,128)(2,1)} %param.21, s32[512]{0:T(512)S(1)} %eq.65), kind=kOutput, calls=%fused_computation.36 | convolution fusion | flops 177995520 | bytes 692224 | tf_op jit(solution)/shard_map/dot_general | solution.py:23
  21.4 1.1 %multiply_convert_fusion.1 = (bf16[256,512]{1,0:T(8,128)(2,1)S(1)}, f32[256,512]{1,0:T(8,128)}) fusion(bf16[256,512]{1,0:T(8,128)(2,1)S(1)} %multiply_convert_fusion.2, bf16[512,512]{1,0:T(8,128)(2,1)S(1)} %copy-done), kind=kOutput, calls=%fused_computation.33 | convolution fusion | flops 134873088 | bytes 1572864 | tf_op jit(solution)/shard_map/dot_general | solution.py:23
  24.0 3.8 %all-to-all-start.1 = ((bf16[16,32,80]{2,1,0:T(8,128)(2,1)}), bf16[16,32,80]{2,1,0:T(8,128)(2,1)S(1)}, u32[]{:S(2)}, u32[]{:S(2)}) async-start(bf16[16,32,80]{2,1,0:T(8,128)(2,1)} %bitcast.3), calls=%async_computation.1 | async-start | bytes 262144 | tf_op jit(solution)/shard_map/all_to_all | solution.py:38
  27.9 7.8 %all-to-all-done.1 = bf16[16,32,80]{2,1,0:T(8,128)(2,1)S(1)} async-done(((bf16[16,32,80]{2,1,0:T(8,128)(2,1)}), bf16[16,32,80]{2,1,0:T(8,128)(2,1)S(1)}, u32[]{:S(2)}, u32[]{:S(2)}) %all-to-all-start.1) | async-done | bytes 81952 | tf_op jit(solution)/shard_map/all_to_all | solution.py:38
  35.9 1.9 %all-gather = f32[160,256]{1,0:T(8,128)S(1)} all-gather(f32[80,256]{1,0:T(8,128)S(1)} %fusion.6), channel_id=2, replica_groups=mesh['band'=16,'member'=2] {'member'}, dimensions={0}, use_global_device_ids=true | all-gather | bytes 245760 | tf_op jit(solution)/shard_map/all_gather | solution.py:101
  38.3 10.7 %all_to_all.25 = bf16[16,32,80]{2,1,0:T(8,128)(2,1)S(1)} all-to-all(bf16[16,32,80]{2,1,0:T(8,128)(2,1)S(1)} %bitcast.52), channel_id=1, replica_groups=mesh['band'=16,'member'=2] {'band'}, dimensions={0} | all-to-all | bytes 163840 | tf_op jit(solution)/shard_map/all_to_all | solution.py:38
  51.9 1.2 %multiply_reduce_fusion = (bf16[512]{0:T(512)(128)(2,1)S(1)}, f32[256]{0:T(256)S(1)}, f32[256,512]{1,0:T(8,128)}) fusion(f32[256,512]{1,0:T(8,128)S(1)} %get-tuple-element.39, f32[256]{0:T(256)S(1)} %get-tuple-element.37, f32[512]{0:T(512)S(1)} %copy-done.6, f32[256,512]{1,0:T(8,128)S(1)} %fusion.31, bf16[512,512]{1,0:T(8,128)(2,1)S(1)} %copy-done, ...), kind=kOutput, calls=%fused_computation.25 | convolution fusion | flops 135658752 | bytes 2626560 | tf_op jit(solution)/shard_map/dot_general | solution.py:23
  53.8 23.8 %all_to_all.26 = bf16[16,32,688]{2,1,0:T(8,128)(2,1)S(1)} all-to-all(bf16[16,32,688]{2,1,0:T(8,128)(2,1)S(1)} %bitcast.50), channel_id=1, replica_groups=mesh['band'=16,'member'=2] {'band'}, dimensions={0} | all-to-all | bytes 1409024 | tf_op jit(solution)/shard_map/all_to_all | solution.py:46
  77.8 1.0 broadcast_in_dim.18
  78.7 3.6 %all-to-all-start.4 = ((bf16[16,32,688]{2,1,0:T(8,128)(2,1)}), bf16[16,32,688]{2,1,0:T(8,128)(2,1)S(1)}, u32[]{:S(2)}, u32[]{:S(2)}) async-start(bf16[16,32,688]{2,1,0:T(8,128)(2,1)} %broadcast_in_dim.18), calls=%async_computation.4 | async-start | bytes 1572864 | tf_op jit(solution)/shard_map/all_to_all | solution.py:55
  82.4 0.9 fusion.12
  83.2 18.1 %all-to-all-done.4 = bf16[16,32,688]{2,1,0:T(8,128)(2,1)S(1)} async-done(((bf16[16,32,688]{2,1,0:T(8,128)(2,1)}), bf16[16,32,688]{2,1,0:T(8,128)(2,1)S(1)}, u32[]{:S(2)}, u32[]{:S(2)}) %all-to-all-start.4) | async-done | bytes 704544 | tf_op jit(solution)/shard_map/all_to_all | solution.py:55
  101.5 0.8 slice_reduce_fusion
  102.7 1.1 %slice_bitcast_fusion = f32[1,512,512]{2,1,0:T(8,128)} fusion(f32[512,688]{1,0:T(8,128)S(1)} %bitcast.48), kind=kLoop, calls=%fused_computation.21 | loop fusion | bytes 2097152 | tf_op jit(solution)/shard_map/broadcast_in_dim | solution.py:147
  103.8 0.8 copy.38
  104.6 1.3 %fusion = f32[1,512,512]{2,1,0:T(8,128)} fusion(f32[512,512]{1,0:T(8,128)S(1)} %fusion.23, bf16[512,80]{0,1:T(8,128)(2,1)S(1)} %copy-done.3, f32[512,688]{1,0:T(8,128)S(1)} %bitcast.49), kind=kOutput, calls=%fused_computation.2 | convolution fusion | flops 42369024 | bytes 2441216 | tf_op jit(solution)/shard_map/dot_general | solution.py:23
  (52 shorter events, 7.6 us)
Async XLA Ops:
  0.6 20.7 %copy-start = (bf16[512,512]{1,0:T(8,128)(2,1)S(1)}, bf16[512,512]{1,0:T(8,128)(2,1)}, u32[]{:S(2)}) copy-start(bf16[512,512]{1,0:T(8,128)(2,1)} %param.23) | copy-start | bytes 1572868
  3.4 16.1 %all-to-all-start = ((bf16[16,32,80]{2,1,0:T(8,128)(2,1)}), bf16[16,32,80]{2,1,0:T(8,128)(2,1)S(1)}, u32[]{:S(2)}, u32[]{:S(2)}) async-start(bf16[16,32,80]{2,1,0:T(8,128)(2,1)} %bitcast.1), calls=%async_computation | async-start | bytes 262144 | tf_op jit(solution)/shard_map/all_to_all | solution.py:38
  19.6 1.7 %copy-start.6 = (f32[512]{0:T(512)S(1)}, f32[512]{0:T(512)}, u32[]{:S(2)}) copy-start(f32[512]{0:T(512)} %param.22) | copy-start | bytes 6148
  21.4 1.1 %copy-start.1 = (bf16[512,512]{1,0:T(8,128)(2,1)S(1)}, bf16[512,512]{1,0:T(8,128)(2,1)}, u32[]{:S(2)}) copy-start(bf16[512,512]{1,0:T(8,128)(2,1)} %param.24) | copy-start | bytes 1572868
  21.4 1.4 %copy-start.3 = (bf16[512,80]{0,1:T(8,128)(2,1)S(1)}, bf16[512,80]{0,1:T(8,128)(2,1)}, u32[]{:S(2)}) copy-start(bf16[512,80]{0,1:T(8,128)(2,1)} %param.25) | copy-start | bytes 245764
  22.5 13.2 %copy-start.7 = (f32[80,256]{1,0:T(8,128)S(1)}, f32[80,256]{1,0:T(8,128)}, u32[]{:S(2)}) copy-start(f32[80,256]{1,0:T(8,128)} %param.13) | copy-start | bytes 245764
  22.5 15.4 %copy-start.5 = (bf16[80,256]{1,0:T(8,128)(2,1)S(1)}, bf16[80,256]{1,0:T(8,128)(2,1)}, u32[]{:S(2)}) copy-start(bf16[80,256]{1,0:T(8,128)(2,1)} %param.16) | copy-start | bytes 122884
  24.0 11.6 %all-to-all-start.1 = ((bf16[16,32,80]{2,1,0:T(8,128)(2,1)}), bf16[16,32,80]{2,1,0:T(8,128)(2,1)S(1)}, u32[]{:S(2)}, u32[]{:S(2)}) async-start(bf16[16,32,80]{2,1,0:T(8,128)(2,1)} %bitcast.3), calls=%async_computation.1 | async-start | bytes 262144 | tf_op jit(solution)/shard_map/all_to_all | solution.py:38
  35.9 2.0 %copy-start.4 = (f32[80,256]{1,0:T(8,128)}, f32[80,256]{1,0:T(8,128)S(1)}, u32[]{:S(2)}) copy-start(f32[80,256]{1,0:T(8,128)S(1)} %fusion.6) | copy-start | bytes 245764
  49.5 1.0 copy-start.8
  77.6 4.7 %copy-start.2 = (f32[256,512]{1,0:T(8,128)S(1)}, f32[256,512]{1,0:T(8,128)}, u32[]{:S(2)}) copy-start(f32[256,512]{1,0:T(8,128)} %get-tuple-element.42) | copy-start | bytes 1572868
  78.7 22.6 %all-to-all-start.4 = ((bf16[16,32,688]{2,1,0:T(8,128)(2,1)}), bf16[16,32,688]{2,1,0:T(8,128)(2,1)S(1)}, u32[]{:S(2)}, u32[]{:S(2)}) async-start(bf16[16,32,688]{2,1,0:T(8,128)(2,1)} %broadcast_in_dim.18), calls=%async_computation.4 | async-start | bytes 1572864 | tf_op jit(solution)/shard_map/all_to_all | solution.py:55

commit v2 on v1

--- a/solution.py
+++ b/solution.py
@@ -1,8 +1,11 @@
+import functools
 import math
 
 import jax
 import jax.numpy as jnp
 from jax import lax
+from jax.experimental import pallas as pl
+from jax.experimental.pallas import tpu as pltpu
 from jax.sharding import PartitionSpec as P
 
 MESH_DEV = 256
@@ -56,7 +59,331 @@
     return full.reshape(rows, width).astype(f32)
 
 
-def body(
+TABLE_ROWS = 16
+LANES = 128
+
+
+def one_hot(a, b):
+    return jnp.where(a == b, 1.0, 0.0).astype(bf16)
+
+
+def sigmoid(v):
+    return 0.5 + 0.5 * jnp.tanh(0.5 * v)
+
+
+def table_rows(all_ref, bands, group, xy, s, table_at):
+    mate = s * (bands // group) + xy
+    return all_ref[mate, table_at : table_at + TABLE_ROWS, :].astype(f32)
+
+
+def forward_kernel(
+    group,
+    channels,
+    me_ref,
+    all_ref,
+    lift_ref,
+    scale_ref,
+    expand_ref,
+    contract_ref,
+    readout_ref,
+    normed_ref,
+    slope_ref,
+    state_ref,
+    own_ref,
+    own_pre_ref,
+    chosen_ref,
+    slot_ref,
+):
+    bands = all_ref.shape[0]
+    node_rows, width = normed_ref.shape[1], normed_ref.shape[2]
+    slots = slot_ref.shape[1]
+    cap = slots // bands
+    z, xy = me_ref[0], me_ref[1]
+    subs = lax.broadcasted_iota(jnp.int32, (node_rows, LANES), 0).astype(f32)
+
+    def embed(b, carry):
+        latent = mm(all_ref[b, 0:channels, :], lift_ref[...], 0, 0)
+        latent = (latent * sigmoid(latent)).astype(bf16)
+        slot_ref[:, pl.ds(pl.multiple_of(b * cap, cap), cap), :] = latent.reshape(group, cap, width)
+        return carry
+
+    lax.fori_loop(0, bands, embed, 0)
+
+    def nodes(s, carry):
+        table = table_rows(all_ref, bands, group, xy, s, channels)
+        parts = slots // LANES
+        hot = [jnp.where(subs == table[j : j + 1, :], 1.0, 0.0) for j in range(parts)]
+        count = sum(jnp.sum(h, axis=1, keepdims=True) for h in hot)
+        landing = jnp.concatenate(hot, axis=1).astype(bf16)
+        state = mm(landing, slot_ref[s], 1, 0) / jnp.maximum(count, 1.0)
+        recip = lax.rsqrt(jnp.mean(state * state, axis=1, keepdims=True) + norm_eps)
+        normed = (state * recip * scale_ref[...]).astype(bf16)
+        normed_ref[s] = normed
+        pre = mm(normed, expand_ref[...], 1, 0)
+        gate = sigmoid(pre)
+        hidden = pre * gate
+        slope_ref[s] = (gate + hidden * (1.0 - gate)).astype(bf16)
+        hidden = hidden.astype(bf16)
+        following = (state + mm(hidden, contract_ref[...], 1, 0)).astype(bf16)
+        state_ref[s, :, 0:width] = following
+        state_ref[s, :, width:] = hidden
+
+        @pl.when(s == z)
+        def _():
+            own_ref[...] = state
+            own_pre_ref[...] = pre
+            projected = mm(following, readout_ref[...], 1, 0).astype(bf16)
+            for j in range(parts):
+                pick = one_hot(subs, table[parts + j : parts + j + 1, :])
+                chosen_ref[j * LANES : (j + 1) * LANES, :] = mm(pick, projected, 0, 0).astype(bf16)
+
+        return carry
+
+    lax.fori_loop(0, group, nodes, 0)
+
+
+def backward_kernel(
+    group,
+    channels,
+    me_ref,
+    grad_ref,
+    all_ref,
+    chain_ref,
+    normed_ref,
+    slope_ref,
+    state_ref,
+    own_ref,
+    *rest,
+):
+    piece_refs, (value_ref, up_ref, small_ref) = rest[:-3], rest[-3:]
+    bands = grad_ref.shape[0]
+    slots = value_ref.shape[1]
+    node_rows, width = normed_ref.shape[1], normed_ref.shape[2]
+    cap = slots // bands
+    z, xy = me_ref[0], me_ref[1]
+    subs = lax.broadcasted_iota(jnp.int32, (node_rows, LANES), 0).astype(f32)
+
+    def turn(b, carry):
+        values = grad_ref[b].astype(f32).T.astype(bf16)
+        value_ref[:, pl.ds(pl.multiple_of(b * cap, cap), cap), :] = values.reshape(group, cap, channels)
+        return carry
+
+    lax.fori_loop(0, bands, turn, 0)
+    up_ref[...] = jnp.zeros_like(up_ref)
+    small_ref[...] = jnp.zeros_like(small_ref)
+
+    def nodes(s, carry):
+        table = table_rows(all_ref, bands, group, xy, s, channels)
+        parts = slots // LANES
+        pick = jnp.concatenate(
+            [one_hot(subs, table[parts + j : parts + j + 1, :]) for j in range(parts)], axis=1
+        )
+        node_grad = mm(pick, value_ref[s], 1, 0)
+
+        @pl.when(s == z)
+        def _():
+            own_ref[...] = node_grad
+
+        node_b = node_grad.astype(bf16)
+        pre = (mm(node_b, chain_ref[...], 1, 1) * slope_ref[s].astype(f32)).astype(bf16)
+        up_ref[...] += mm(normed_ref[s], pre, 0, 0)
+        small_ref[...] += mm(node_b, state_ref[s], 0, 0)
+        return carry
+
+    lax.fori_loop(0, group, nodes, 0)
+    count = len(piece_refs)
+    rows = up_ref.shape[0] // count
+    half = up_ref.shape[1] // 2
+    lanes = small_ref.shape[1] // count
+    for p, piece_ref in enumerate(piece_refs):
+        to = xy ^ p
+        at = pl.ds(pl.multiple_of(to * rows, rows), rows)
+        piece_ref[0:rows, :] = up_ref[at, 0:half].astype(bf16)
+        piece_ref[rows : 2 * rows, :] = up_ref[at, half:].astype(bf16)
+        piece_ref[2 * rows :, :] = small_ref[:, pl.ds(pl.multiple_of(to * lanes, lanes), lanes)].astype(bf16)
+
+
+def finish_kernel(factor, channels, me_ref, scale_ref, expand_ref, readout_ref, *rest):
+    count = len(rest) - 5
+    piece_refs, (up_ref, down_ref, dec_ref, gain_ref, small_ref) = rest[:count], rest[count:]
+    rows = up_ref.shape[0] // count
+    half = up_ref.shape[1] // 2
+    lanes = small_ref.shape[1] // count
+    for p, piece_ref in enumerate(piece_refs):
+        to = me_ref[1] ^ p
+        at = pl.ds(pl.multiple_of(to * rows, rows), rows)
+        left = piece_ref[0:rows, :].astype(f32) * factor
+        right = piece_ref[rows : 2 * rows, :].astype(f32) * factor
+        up_ref[at, 0:half] = left
+        up_ref[at, half:] = right
+        small_ref[:, pl.ds(pl.multiple_of(to * lanes, lanes), lanes)] = piece_ref[2 * rows :, :].astype(f32) * factor
+        gain = jnp.sum(left * expand_ref[at, 0:half].astype(f32), axis=1, keepdims=True)
+        gain = gain + jnp.sum(right * expand_ref[at, half:].astype(f32), axis=1, keepdims=True)
+        gain_ref[at, :] = gain / scale_ref[at, :]
+    width = up_ref.shape[0]
+    dec_ref[...] = small_ref[:, 0:width].T
+    hidden = small_ref[:, width:]
+    high = hidden.astype(bf16)
+    low = (hidden - high.astype(f32)).astype(bf16)
+    down_ref[...] = mm(high, readout_ref[...], 0, 1) + mm(low, readout_ref[...], 0, 1)
+
+
+def vmem_call(kernel, outs, name, scratch=(), budget=16):
+    vmem = pl.BlockSpec(memory_space=pltpu.VMEM)
+    smem = pl.BlockSpec(memory_space=pltpu.SMEM)
+
+    def call(scalars, *operands):
+        return pl.pallas_call(
+            kernel,
+            out_shape=[jax.ShapeDtypeStruct(s, d) for s, d in outs],
+            in_specs=[smem] + [vmem] * len(operands),
+            out_specs=[vmem] * len(outs),
+            scratch_shapes=[pltpu.VMEM(s, d) for s, d in scratch],
+            compiler_params=pltpu.CompilerParams(vmem_limit_bytes=budget * 2**20),
+            name=name,
+        )(scalars, *operands)
+
+    return call
+
+
+def to_column(x, bands, group):
+    channels = x.shape[0]
+    blocks = x.reshape(channels, bands // group, -1).transpose(1, 0, 2)
+    return jnp.broadcast_to(blocks[None], (group,) + blocks.shape).reshape(bands, channels, -1)
+
+
+def by_column(table, group):
+    bands, cap = table.shape
+    return table.reshape(group, bands // group, cap).transpose(1, 0, 2).reshape(-1)
+
+
+def all_to_all(x):
+    return lax.all_to_all(x, "band", split_axis=0, concat_axis=0, tiled=True)
+
+
+def member_terms(student_outputs, target, weight_map):
+    all_pred, all_target = (
+        lax.all_gather(student_outputs[None], "member", axis=0, tiled=True),
+        lax.all_gather(target, "member", axis=0, tiled=True),
+    )
+    teacher_terms = jnp.sum(slope(student_outputs[None] - all_target.astype(f32)), axis=0)
+    own_terms = jnp.sum(slope(student_outputs[None] - all_pred), axis=0)
+    return weight_map.astype(f32) * (teacher_terms - own_terms)
+
+
+def state_gradient(node_grad, mesh_state, hidden_pre, scale, expand, contract, readout):
+    recip = lax.rsqrt(jnp.mean(mesh_state * mesh_state, axis=1, keepdims=True) + norm_eps)
+    next_grad = mm2(node_grad, readout, 1, 1)
+    hidden_grad = mm2(next_grad, contract, 1, 1)
+    sigma = jax.nn.sigmoid(hidden_pre)
+    pre_grad = hidden_grad * sigma * (1.0 + hidden_pre * (1.0 - sigma))
+    normed_grad = mm2(pre_grad, expand, 1, 1)
+    gained = normed_grad * scale
+    return (
+        next_grad
+        + recip * gained
+        - mesh_state * (recip * recip * recip) * jnp.mean(gained * mesh_state, axis=1, keepdims=True)
+    ).astype(bf16)
+
+
+def column_body(
+    group,
+    scaled_atmosphere_field,
+    perturbation,
+    target,
+    weight_map,
+    enc_send,
+    enc_recv,
+    dec_send,
+    dec_recv,
+    lattice_lift_matrix,
+    mixing_rescale_factor,
+    expand_matrix,
+    contract_matrix,
+    readout_matrix,
+):
+    bands = lax.axis_size("band")
+    channels, grid_rows = scaled_atmosphere_field.shape
+    node_rows = MESH_DEV
+    width, hid = expand_matrix.shape
+    slots = bands * enc_send.shape[2]
+    crew = bands // group
+    band = lax.axis_index("band").astype(jnp.int32)
+    me = jnp.stack([band // crew, band % crew])
+    cell_ids = jnp.arange(grid_rows, dtype=jnp.int32)
+    inputs_b = (scaled_atmosphere_field + perturbation[0].astype(f32)).astype(bf16)
+    picker = (cell_ids[:, None] == by_column(enc_send[0], group)[None, :]).astype(bf16)
+    outgoing = to_column(mm(inputs_b, picker, 1, 0).astype(bf16), bands, group)
+    tables = jnp.concatenate([enc_recv[0].reshape(-1, LANES), dec_send[0].reshape(-1, LANES)]).astype(bf16)
+    tables = jnp.pad(tables, ((0, TABLE_ROWS - tables.shape[0]), (0, 0)))
+    tables = jnp.broadcast_to(tables[None], (bands,) + tables.shape)
+    arrived = all_to_all(jnp.concatenate([outgoing, tables], axis=1))
+    normed, slopes, states, mesh_state, hidden_pre, chosen = vmem_call(
+        functools.partial(forward_kernel, group, channels),
+        [
+            ((group, node_rows, width), bf16),
+            ((group, node_rows, hid), bf16),
+            ((group, node_rows, width + hid), bf16),
+            ((node_rows, width), f32),
+            ((node_rows, hid), f32),
+            ((slots, channels), bf16),
+        ],
+        "forward",
+        scratch=[((group, slots, width), bf16)],
+    )(
+        me,
+        arrived,
+        lattice_lift_matrix,
+        mixing_rescale_factor[None, :],
+        expand_matrix,
+        contract_matrix,
+        readout_matrix,
+    )
+    chain = mm(contract_matrix, readout_matrix, 1, 0).astype(bf16)
+    slot_values = exchange(chosen, bands)
+    fill_map = (cell_ids[:, None] == dec_recv[0].reshape(-1)[None, :]).astype(bf16)
+    inverse = 1.0 / jnp.maximum(jnp.sum(fill_map.astype(f32), axis=1), 1.0)
+    student_outputs = scaled_atmosphere_field + mm(slot_values, fill_map, 0, 1) * inverse[None, :]
+    pred_grad = member_terms(student_outputs, target, weight_map)
+    scaled = (pred_grad * inverse[None, :]).astype(bf16)
+    spread_map = (cell_ids[:, None] == by_column(dec_recv[0], group)[None, :]).astype(bf16)
+    returned = all_to_all(to_column(mm(scaled, spread_map, 1, 0).astype(bf16), bands, group))
+    piece_rows = 2 * (width // crew) + channels
+    node_grad, *pieces = vmem_call(
+        functools.partial(backward_kernel, group, channels),
+        [((node_rows, channels), f32)] + [((piece_rows, hid // 2), bf16)] * crew,
+        "backward",
+        scratch=[
+            ((group, slots, channels), bf16),
+            ((width, hid), f32),
+            ((channels, width + hid), f32),
+        ],
+    )(me, returned, arrived, chain, normed, slopes, states)
+    swaps = [[(i, i ^ p) for i in range(bands)] for p in range(1, crew)]
+    others = [lax.ppermute(piece, "band", swap) for piece, swap in zip(pieces[1:], swaps)]
+    total = sum(x.astype(f32) for x in [pieces[0]] + others).astype(bf16)
+    totals = [total] + [lax.ppermute(total, "band", swap) for swap in swaps]
+    state_grad = state_gradient(
+        node_grad, mesh_state, hidden_pre, mixing_rescale_factor, expand_matrix, contract_matrix, readout_matrix
+    )
+    factor = 1.0 / math.sqrt(bands * node_rows)
+    grad_up, grad_down, grad_dec, grad_gain = vmem_call(
+        functools.partial(finish_kernel, factor, channels),
+        [((width, hid), f32), ((hid, width), f32), ((width, channels), f32), ((width, 1), f32)],
+        "finish",
+        scratch=[((channels, width + hid), f32)],
+    )(me, mixing_rescale_factor[:, None], expand_matrix, readout_matrix, *totals)
+    return (
+        student_outputs[None],
+        state_grad[None],
+        grad_up[None],
+        grad_down[None],
+        grad_dec[None],
+        grad_gain[:, 0][None],
+    )
+
+
+def band_body(
     scaled_atmosphere_field,
     perturbation,
     target,
@@ -97,58 +424,56 @@
     slot_values = exchange(chosen, band_count)
     grid_sum = mm(slot_values, fill_map, 0, 1)
     student_outputs = scaled_atmosphere_field + grid_sum * inverse[None, :]
-    all_pred, all_target = (
-        lax.all_gather(student_outputs[None], "member", axis=0, tiled=True),
-        lax.all_gather(target, "member", axis=0, tiled=True),
-    )
-    teacher_terms = jnp.sum(slope(student_outputs[None] - all_target.astype(f32)), axis=0)
-    own_terms = jnp.sum(slope(student_outputs[None] - all_pred), axis=0)
-    pred_grad = weight_map.astype(f32) * (teacher_terms - own_terms)
+    pred_grad = member_terms(student_outputs, target, weight_map)
     scaled = (pred_grad * inverse[None, :]).astype(bf16)
     slot_grad = mm(fill_map, scaled, 0, 1).astype(bf16)
     returned = exchange(slot_grad, band_count)
     node_grad = mm(mesh_picker, returned, 0, 0)
-    next_grad = mm2(node_grad, readout_matrix, 1, 1)
     grad_hi, grad_lo = split3(node_grad)
     states = jnp.concatenate([next_b, hidden_b], axis=1)
     small = mm(states, grad_hi, 0, 0) + mm(states, grad_lo, 0, 0)
-    hidden_grad = mm2(next_grad, contract_matrix, 1, 1)
+    hidden_grad = mm2(mm2(node_grad, readout_matrix, 1, 1), contract_matrix, 1, 1)
     sigma = jax.nn.sigmoid(hidden_pre)
-    pre_grad = hidden_grad * sigma * (1.0 + hidden_pre * (1.0 - sigma))
-    pre_hi, pre_lo = split3(pre_grad)
+    pre_hi, pre_lo = split3(hidden_grad * sigma * (1.0 + hidden_pre * (1.0 - sigma)))
     up_part = mm(normed_b, pre_hi, 0, 0) + mm(normed_b, pre_lo, 0, 0)
-    normed_grad = mm(pre_hi, expand_matrix, 1, 1) + mm(pre_lo, expand_matrix, 1, 1)
-    gain_part = jnp.sum(normed_grad * mesh_state * recip, axis=0)
-    gained = normed_grad * mixing_rescale_factor
-    state_grad = (
-        next_grad
-        + recip * gained
-        - mesh_state
-        * (recip * recip * recip)
-        * jnp.mean(gained * mesh_state, axis=1, keepdims=True)
-    )
-    width = up_part.shape[0]
+    state_grad = state_gradient(
+        node_grad, mesh_state, hidden_pre, mixing_rescale_factor, expand_matrix, contract_matrix, readout_matrix
+    )
+    width, hid = up_part.shape
     factor = 1.0 / math.sqrt(band_count * node_rows)
-    packed = jnp.concatenate(
-        [up_part, small[:width], small[width:], gain_part[:, None]], axis=1
-    )
-    pad = -packed.shape[1] % 16
-    packed = jnp.pad(packed, ((0, 0), (0, pad)))
+    packed = jnp.concatenate([up_part, small[:width], small[width:]], axis=1)
+    packed = jnp.pad(packed, ((0, 0), (0, -packed.shape[1] % 16)))
     total = sum_over_bands(packed, band_count) * factor
-    hid = up_part.shape[1]
     grad_up = total[:, :hid]
     grad_dec = total[:, hid : hid + channels]
-    hid_sum = total[:, hid + channels : hid + 2 * channels]
-    grad_gain = total[:, hid + 2 * channels]
-    grad_down = mm2(hid_sum, readout_matrix, 1, 1)
+    grad_down = mm2(total[:, hid + channels : hid + 2 * channels], readout_matrix, 1, 1)
+    grad_gain = jnp.sum(grad_up * expand_matrix.astype(f32), axis=1) / mixing_rescale_factor
     return (
         student_outputs[None],
-        state_grad.astype(bf16)[None],
+        state_grad[None],
         grad_up[None],
         grad_down[None],
         grad_dec[None],
         grad_gain[None],
     )
+
+
+def body(*args):
+    field, enc_send, dec_send, expand = args[0], args[4], args[6], args[10]
+    bands, cap = enc_send.shape[1:]
+    channels, grid_rows = field.shape
+    group = LANES // cap
+    column = (
+        dec_send.shape[2] == cap
+        and LANES % cap == 0
+        and cap % 16 == 0
+        and group * group == bands
+        and channels % 16 == 0
+        and max(grid_rows, MESH_DEV) <= 256
+        and bands * cap * 2 <= TABLE_ROWS * LANES
+        and expand.shape[0] == expand.shape[1]
+    )
+    return column_body(group, *args) if column else band_body(*args)
 
 
 def solution(mesh):

time: 107 us -> 101 us (0.944)
  blocking collectives: 38.5 us -> 3.78 us
  Pallas kernels: 0 us -> 17 us
  waiting for transfers between devices: 29 us -> 36.9 us
  matrix products: 10.9 us -> 3.8 us
  starting transfers between devices: 15.8 us -> 22.7 us
  other arithmetic: 1.7 us -> 4.2 us
  local copies, waits for them, and re-layouts: 9.12 us -> 10.6 us
    all_to_all x2 -> x0, blocking collectives: 34.5 us -> none  [the longest x1 23.8 us: sum_over_bands(): lax.all_to_all(x.astype(bf16).reshape(band_count, rows // band_count, wid...]
    pallas_call x0 -> x3, Pallas kernels: none -> 17 us  [call(): pl.pallas_call(kernel, out_shape=[jax.ShapeDtypeStruct(s, d) for s, d in...]
    all_to_all x2 -> x1, starting transfers between devices: 12.1 us -> 3.59 us  [exchange(): lax.all_to_all(x.reshape(band_count, rows // band_count, width), 'band',...]
    all_to_all x1 -> x2, starting transfers between devices: 3.61 us -> 12 us  [all_to_all(): return lax.all_to_all(x, 'band', split_axis=0, concat_axis=0, tiled=True)]
    ppermute x0 -> x6, waiting for transfers between devices: none -> 7.64 us  [the longest x3 4.06 us: column_body(): totals = [total] + [lax.ppermute(total, 'band', swap) for swap in swaps]]
    ppermute x0 -> x6, starting transfers between devices: none -> 7.11 us  [the longest x3 3.55 us: column_body(): lax.ppermute(piece, 'band', swap)]
    dot_general x20 -> x10, matrix products: 10.9 us -> 3.8 us  [mm(): lax.dot_general(a, b, (((ca,), (cb,)), ((), ())), preferred_element_type=...]
    unnamed x20 -> x34, local copies, waits for them, and re-layouts: 1.29 us -> 8.26 us
  transfers between devices with their start and end apart: 3 -> 9, of which waited for: 3 -> 8; matrix products, arithmetic and copies ran while one was open for 3% -> 4% of each run, Pallas kernels for 0% -> 0%
where the time goes in v2:
time: 101 us; the launch traced here: 100 us
  waiting for transfers between devices  36.9 us (37%)
  starting transfers between devices  22.7 us (22%)
  Pallas kernels  17 us (17%)
  local copies, waits for them, and re-layouts  10.6 us (10%)
  other arithmetic  4.2 us (4%)
  matrix products  3.8 us (4%)
  blocking collectives  3.78 us (4%)
    all_to_all x2, waiting for transfers between devices, all_to_all(): return lax.all_to_all(x, 'band', split_axis=0, concat_axis=0, tiled=True)  21.5 us
    pallas_call x3, Pallas kernels, call(): pl.pallas_call(kernel, out_shape=[jax.ShapeDtypeStruct(s, d) for s, d in...  17 us
    all_to_all x2, starting transfers between devices, all_to_all(): return lax.all_to_all(x, 'band', split_axis=0, concat_axis=0, tiled=True)  12 us
    unnamed x34, local copies, waits for them, and re-layouts  8.26 us
    all_to_all x1, waiting for transfers between devices, exchange(): lax.all_to_all(x.reshape(band_count, rows // band_count, width), 'band',...  7.78 us
    ppermute x3, waiting for transfers between devices, column_body(): totals = [total] + [lax.ppermute(total, 'band', swap) for swap in swaps]  4.06 us
    dot_general x10, matrix products, mm(): lax.dot_general(a, b, (((ca,), (cb,)), ((), ())), preferred_element_type=...  3.8 us
    all_to_all x1, starting transfers between devices, exchange(): lax.all_to_all(x.reshape(band_count, rows // band_count, width), 'band',...  3.59 us
  transfers between devices with their start and end apart: 9, of which 8 were waited for; matrix products, arithmetic and copies ran while one was open for 4% of the time, Pallas kernels for 0%

profile of v2, /device:TPU:0, one launch (start us, length us, event | category | flops | bytes accessed | tf_op | source)
XLA Modules:
  0.0 100.0 jit_solution(8683280388514313297)
XLA Ops:
  1.6 1.1 %convolution_convert_fusion.2 = bf16[80,512]{1,0:T(8,128)(2,1)S(1)} fusion(s32[512]{0:T(512)S(1)} %eq.48, f32[80,256]{1,0:T(8,128)} %param.13, bf16[1,80,256]{2,1,0:T(8,128)(2,1)} %param.14), kind=kOutput, calls=%fused_computation.8 | convolution fusion | flops 21204992 | bytes 206848 | tf_op jit(solution)/shard_map/dot_general | solution.py:26
  5.2 8.5 %all-to-all-start = ((bf16[16,96,128]{2,1,0:T(8,128)(2,1)}), bf16[16,96,128]{2,1,0:T(8,128)(2,1)S(1)}, u32[]{:S(2)}, u32[]{:S(2)}) async-start(bf16[16,96,128]{2,1,0:T(8,128)(2,1)} %pad_maximum_fusion), calls=%async_computation | async-start | bytes 786432 | tf_op jit(solution)/shard_map/all_to_all | solution.py:261
  14.0 1.9 %all_gather.6 = bf16[2,80,256]{2,1,0:T(8,128)(2,1)S(1)} all-gather(bf16[1,80,256]{2,1,0:T(8,128)(2,1)S(1)} %copy-done.13), channel_id=1, replica_groups=mesh['band'=16,'member'=2] {'member'}, dimensions={0}, use_global_device_ids=true | all-gather | bytes 122880 | tf_op jit(solution)/shard_map/all_gather | solution.py:267
  16.1 10.2 %all-to-all-done.all_ref = bf16[16,96,128]{2,1,0:T(8,128)(2,1)S(1)} async-done(((bf16[16,96,128]{2,1,0:T(8,128)(2,1)}), bf16[16,96,128]{2,1,0:T(8,128)(2,1)S(1)}, u32[]{:S(2)}, u32[]{:S(2)}) %all-to-all-start) | async-done | bytes 393248 | tf_op jit(solution)/shard_map/all_to_all | solution.py:261
  26.3 9.4 %forward.1 = (bf16[4,256,512]{2,1,0:T(8,128)(2,1)S(1)}, bf16[4,256,512]{2,1,0:T(8,128)(2,1)S(1)}, bf16[4,256,1024]{2,1,0:T(8,128)(2,1)S(1)}, f32[256,512]{1,0:T(...) custom-call(s32[2]{0:T(128)S(1)} %pad_add_fusion.me_ref, bf16[16,96,128]{2,1,0:T(8,128)(2,1)S(1)} %all-to-all-done.all_ref, ...), custom_call_target="tpu_custom_call" | custom-call | tf_op jit(solution)/shard_map/forward/pallas_call | solution.py:236
  35.7 1.3 %copy-done.2 = bf16[4,256,1024]{2,1,0:T(8,128)(2,1)} copy-done((bf16[4,256,1024]{2,1,0:T(8,128)(2,1)}, bf16[4,256,1024]{2,1,0:T(8,128)(2,1)S(1)}, u32[]{:S(2)}) %copy-start.2) | copy-done | bytes 2097176
  39.0 3.6 %all-to-all-start.1 = ((bf16[16,32,80]{2,1,0:T(8,128)(2,1)}), bf16[16,32,80]{2,1,0:T(8,128)(2,1)S(1)}, u32[]{:S(2)}, u32[]{:S(2)}) async-start(bf16[16,32,80]{2,1,0:T(8,128)(2,1)} %bitcast.8), calls=%async_computation.1 | async-start | bytes 262144 | tf_op jit(solution)/shard_map/all_to_all | solution.py:41
  42.6 7.8 %all-to-all-done.1 = bf16[16,32,80]{2,1,0:T(8,128)(2,1)S(1)} async-done(((bf16[16,32,80]{2,1,0:T(8,128)(2,1)}), bf16[16,32,80]{2,1,0:T(8,128)(2,1)S(1)}, u32[]{:S(2)}, u32[]{:S(2)}) %all-to-all-start.1) | async-done | bytes 81952 | tf_op jit(solution)/shard_map/all_to_all | solution.py:41
  50.6 1.9 %all-gather = f32[160,256]{1,0:T(8,128)S(1)} all-gather(f32[80,256]{1,0:T(8,128)S(1)} %fusion.3), channel_id=2, replica_groups=mesh['band'=16,'member'=2] {'member'}, dimensions={0}, use_global_device_ids=true | all-gather | bytes 245760 | tf_op jit(solution)/shard_map/all_gather | solution.py:266
  53.7 3.5 %all-to-all-start.2 = ((bf16[16,80,128]{2,1,0:T(8,128)(2,1)}), bf16[16,80,128]{2,1,0:T(8,128)(2,1)S(1)}, u32[]{:S(2)}, u32[]{:S(2)}) async-start(bf16[16,80,128]{2,1,0:T(8,128)(2,1)} %bitcast.15), calls=%async_computation.2 | async-start | bytes 655360 | tf_op jit(solution)/shard_map/all_to_all | solution.py:261
  57.8 11.3 %all-to-all-done.2.grad_ref = bf16[16,80,128]{2,1,0:T(8,128)(2,1)S(1)} async-done(((bf16[16,80,128]{2,1,0:T(8,128)(2,1)}), bf16[16,80,128]{2,1,0:T(8,128)(2,1)S(1)}, u32[]{:S(2)}, u32[]{:S(2)}) %all-to-all-start.2) | async-done | bytes 327712 | tf_op jit(solution)/shard_map/all_to_all | solution.py:261
  69.1 1.6 %copy-done.3 = bf16[4,256,1024]{2,1,0:T(8,128)(2,1)S(1)} copy-done((bf16[4,256,1024]{2,1,0:T(8,128)(2,1)S(1)}, bf16[4,256,1024]{2,1,0:T(8,128)(2,1)}, u32[]{:S(2)}) %copy-start.3) | copy-done | bytes 2097176
  70.7 1.2 %copy-done.5 = bf16[4,256,512]{2,1,0:T(8,128)(2,1)S(1)} copy-done((bf16[4,256,512]{2,1,0:T(8,128)(2,1)S(1)}, bf16[4,256,512]{2,1,0:T(8,128)(2,1)}, u32[]{:S(2)}) %copy-start.5) | copy-done | bytes 1048600
  71.9 1.2 %copy-done.7 = bf16[4,256,512]{2,1,0:T(8,128)(2,1)S(1)} copy-done((bf16[4,256,512]{2,1,0:T(8,128)(2,1)S(1)}, bf16[4,256,512]{2,1,0:T(8,128)(2,1)}, u32[]{:S(2)}) %copy-start.7) | copy-done | bytes 1048600
  73.1 5.5 %backward.1 = (f32[256,80]{1,0:T(8,128)S(1)}, bf16[336,256]{1,0:T(8,128)(2,1)S(1)}, bf16[336,256]{1,0:T(8,128)(2,1)S(1)}, bf16[336,256]{1,0:T(8,128)(2,1)S(1)}, bf16[336,256]{1,0:T(8,128)(2,1)S(1)}) custom-call(s32[2]{0:T(128)S(1)} %pad_add_fusion.me_ref, bf16[16,80,128]{2,1,0:T(8,128)(2,1)S(1)} %all-to-all-done.2.grad_ref, ...), custom_call_target="tpu_custom_call" | custom-call | tf_op jit(solution)/shard_map/backward/pallas_call | solution.py:236
  80.0 2.1 %collective-permute-start.2 = (bf16[336,256]{1,0:T(8,128)(2,1)S(1)}, bf16[336,256]{1,0:T(8,128)(2,1)S(1)}, u32[]{:S(2)}, u32[]{:S(2)}) collective-permute-start(bf16[336,256]{1,0:T(8,128)(2,1)S(1)} %get-tuple-element.31), channel_id=1, source_target_pairs={{0,6},{2,4},{4,2},{6,0},{8,14},{10,12},{12,10},{14,8},{16,22},{18,... | collective-permute-start | bytes 516104 | tf_op jit(solution)/shard_map/ppermute | solution.py:363
  84.2 1.1 %collective-permute-done = bf16[336,256]{1,0:T(8,128)(2,1)S(1)} collective-permute-done((bf16[336,256]{1,0:T(8,128)(2,1)S(1)}, bf16[336,256]{1,0:T(8,128)(2,1)S(1)}, u32[]{:S(2)}, u32[]{:S(2)}) %collective-permute-start) | collective-permute-done | bytes 172064 | tf_op jit(solution)/shard_map/ppermute | solution.py:363
  85.2 2.5 %collective-permute-done.1 = bf16[336,256]{1,0:T(8,128)(2,1)S(1)} collective-permute-done((bf16[336,256]{1,0:T(8,128)(2,1)S(1)}, bf16[336,256]{1,0:T(8,128)(2,1)S(1)}, u32[]{:S(2)}, u32[]{:S(2)}) %collective-permute-start.1) | collective-permute-done | bytes 172064 | tf_op jit(solution)/shard_map/ppermute | solution.py:363
  88.7 1.4 %collective-permute-start.4 = (bf16[336,256]{1,0:T(8,128)(2,1)S(1)}, bf16[336,256]{1,0:T(8,128)(2,1)S(1)}, u32[]{:S(2)}, u32[]{:S(2)}) collective-permute-start(bf16[336,256]{1,0:T(8,128)(2,1)S(1)} %add_convert_fusion.rest_0_), channel_id=1, source_target_pairs={{0,4},{2,6},{4,0},{6,2},{8,12},{10,14},{12,8},{14,10},{16,20},{18,... | collective-permute-start | bytes 516104 | tf_op jit(solution)/shard_map/ppermute | solution.py:365
  90.1 1.4 %collective-permute-start.5 = (bf16[336,256]{1,0:T(8,128)(2,1)S(1)}, bf16[336,256]{1,0:T(8,128)(2,1)S(1)}, u32[]{:S(2)}, u32[]{:S(2)}) collective-permute-start(bf16[336,256]{1,0:T(8,128)(2,1)S(1)} %add_convert_fusion.rest_0_), channel_id=1, source_target_pairs={{0,6},{2,4},{4,2},{6,0},{8,14},{10,12},{12,10},{14,8},{16,22},{18,... | collective-permute-start | bytes 516104 | tf_op jit(solution)/shard_map/ppermute | solution.py:365
  92.3 1.0 %collective-permute-done.3.rest_1_ = bf16[336,256]{1,0:T(8,128)(2,1)S(1)} collective-permute-done((bf16[336,256]{1,0:T(8,128)(2,1)S(1)}, bf16[336,256]{1,0:T(8,128)(2,1)S(1)}, u32[]{:S(2)}, u32[]{:S(2)}) %collective-permute-start.3) | collective-permute-done | bytes 172064 | tf_op jit(solution)/shard_map/ppermute | solution.py:365
  93.3 1.5 %collective-permute-done.4.rest_2_ = bf16[336,256]{1,0:T(8,128)(2,1)S(1)} collective-permute-done((bf16[336,256]{1,0:T(8,128)(2,1)S(1)}, bf16[336,256]{1,0:T(8,128)(2,1)S(1)}, u32[]{:S(2)}, u32[]{:S(2)}) %collective-permute-start.4) | collective-permute-done | bytes 172064 | tf_op jit(solution)/shard_map/ppermute | solution.py:365
  94.9 1.5 %collective-permute-done.5.rest_3_ = bf16[336,256]{1,0:T(8,128)(2,1)S(1)} collective-permute-done((bf16[336,256]{1,0:T(8,128)(2,1)S(1)}, bf16[336,256]{1,0:T(8,128)(2,1)S(1)}, u32[]{:S(2)}, u32[]{:S(2)}) %collective-permute-start.5) | collective-permute-done | bytes 172064 | tf_op jit(solution)/shard_map/ppermute | solution.py:365
  96.4 2.2 %finish.1 = (f32[512,512]{1,0:T(8,128)}, f32[512,512]{1,0:T(8,128)}, f32[512,80]{1,0:T(8,128)S(1)}, f32[512,1]{1,0:T(8,128)S(1)}) custom-call(s32[2]{0:T(128)S(1)} %pad_add_fusion.me_ref, f32[512,1]{1,0:T(8,128)S(1)} %copy.58.scale_ref, bf16[512,512]{1,0:T(8,128)(2,1)S(1)} %copy-done, bf16[512,80]{1,0:T(8,128)(2,1)S(1)} %copy.54.readout_ref, ...), custom_call_target="tpu_custom_call" | custom-call | tf_op jit(solution)/shard_map/finish/pallas_call | solution.py:236
  (72 shorter events, 14.4 us)
Async XLA Ops:
  0.6 13.1 %copy-start.10 = (bf16[512,80]{0,1:T(8,128)(2,1)S(1)}, bf16[512,80]{0,1:T(8,128)(2,1)}, u32[]{:S(2)}) copy-start(bf16[512,80]{0,1:T(8,128)(2,1)} %param.25) | copy-start | bytes 245764
  0.6 13.2 %copy-start.14 = (s32[1,16,32]{2,1,0:T(8,128)S(1)}, s32[1,16,32]{2,1,0:T(8,128)}, u32[]{:S(2)}) copy-start(s32[1,16,32]{2,1,0:T(8,128)} %param.20) | copy-start | bytes 6148
  0.7 13.4 %copy-start.13 = (bf16[1,80,256]{2,1,0:T(8,128)(2,1)S(1)}, bf16[1,80,256]{2,1,0:T(8,128)(2,1)}, u32[]{:S(2)}) copy-start(bf16[1,80,256]{2,1,0:T(8,128)(2,1)} %param.15) | copy-start | bytes 122884
  0.7 25.6 %copy-start.9 = (f32[512]{0:T(512)S(1)}, f32[512]{0:T(512)}, u32[]{:S(2)}) copy-start(f32[512]{0:T(512)} %param.22) | copy-start | bytes 6148
  0.7 25.6 %copy-start.8 = (bf16[80,512]{1,0:T(8,128)(2,1)S(1)}, bf16[80,512]{1,0:T(8,128)(2,1)}, u32[]{:S(2)}) copy-start(bf16[80,512]{1,0:T(8,128)(2,1)} %lift_ref.1) | copy-start | bytes 245764
  0.7 25.6 %copy-start = (bf16[512,512]{1,0:T(8,128)(2,1)S(1)}, bf16[512,512]{1,0:T(8,128)(2,1)}, u32[]{:S(2)}) copy-start(bf16[512,512]{1,0:T(8,128)(2,1)} %expand_ref.3) | copy-start | bytes 1572868
  0.7 25.6 %copy-start.1 = (bf16[512,512]{1,0:T(8,128)(2,1)S(1)}, bf16[512,512]{1,0:T(8,128)(2,1)}, u32[]{:S(2)}) copy-start(bf16[512,512]{1,0:T(8,128)(2,1)} %contract_ref.1) | copy-start | bytes 1572868
  4.4 46.0 %copy-start.15 = (f32[80,256]{1,0:T(8,128)S(1)}, f32[80,256]{1,0:T(8,128)}, u32[]{:S(2)}) copy-start(f32[80,256]{1,0:T(8,128)} %param.13) | copy-start | bytes 245764
  5.2 47.4 %copy-start.12 = (bf16[80,256]{1,0:T(8,128)(2,1)S(1)}, bf16[80,256]{1,0:T(8,128)(2,1)}, u32[]{:S(2)}) copy-start(bf16[80,256]{1,0:T(8,128)(2,1)} %param.16) | copy-start | bytes 122884
  5.2 21.1 %all-to-all-start = ((bf16[16,96,128]{2,1,0:T(8,128)(2,1)}), bf16[16,96,128]{2,1,0:T(8,128)(2,1)S(1)}, u32[]{:S(2)}, u32[]{:S(2)}) async-start(bf16[16,96,128]{2,1,0:T(8,128)(2,1)} %pad_maximum_fusion), calls=%async_computation | async-start | bytes 786432 | tf_op jit(solution)/shard_map/all_to_all | solution.py:261
  35.7 1.3 %copy-start.2 = (bf16[4,256,1024]{2,1,0:T(8,128)(2,1)}, bf16[4,256,1024]{2,1,0:T(8,128)(2,1)S(1)}, u32[]{:S(2)}) copy-start(bf16[4,256,1024]{2,1,0:T(8,128)(2,1)S(1)} %get-tuple-element.24.state_ref) | copy-start | bytes 6291460
  37.0 1.0 copy-start.4
  39.0 11.4 %all-to-all-start.1 = ((bf16[16,32,80]{2,1,0:T(8,128)(2,1)}), bf16[16,32,80]{2,1,0:T(8,128)(2,1)S(1)}, u32[]{:S(2)}, u32[]{:S(2)}) async-start(bf16[16,32,80]{2,1,0:T(8,128)(2,1)} %bitcast.8), calls=%async_computation.1 | async-start | bytes 262144 | tf_op jit(solution)/shard_map/all_to_all | solution.py:41
  50.6 28.0 %copy-start.11 = (f32[80,256]{1,0:T(8,128)}, f32[80,256]{1,0:T(8,128)S(1)}, u32[]{:S(2)}) copy-start(f32[80,256]{1,0:T(8,128)S(1)} %fusion.3) | copy-start | bytes 245764
  53.7 15.4 %all-to-all-start.2 = ((bf16[16,80,128]{2,1,0:T(8,128)(2,1)}), bf16[16,80,128]{2,1,0:T(8,128)(2,1)S(1)}, u32[]{:S(2)}, u32[]{:S(2)}) async-start(bf16[16,80,128]{2,1,0:T(8,128)(2,1)} %bitcast.15), calls=%async_computation.2 | async-start | bytes 655360 | tf_op jit(solution)/shard_map/all_to_all | solution.py:261
  69.1 1.6 %copy-start.3 = (bf16[4,256,1024]{2,1,0:T(8,128)(2,1)S(1)}, bf16[4,256,1024]{2,1,0:T(8,128)(2,1)}, u32[]{:S(2)}) copy-start(bf16[4,256,1024]{2,1,0:T(8,128)(2,1)} %copy-done.2) | copy-start | bytes 6291460
  70.7 1.2 %copy-start.5 = (bf16[4,256,512]{2,1,0:T(8,128)(2,1)S(1)}, bf16[4,256,512]{2,1,0:T(8,128)(2,1)}, u32[]{:S(2)}) copy-start(bf16[4,256,512]{2,1,0:T(8,128)(2,1)} %copy-done.4) | copy-start | bytes 3145732
  71.9 1.2 %copy-start.7 = (bf16[4,256,512]{2,1,0:T(8,128)(2,1)S(1)}, bf16[4,256,512]{2,1,0:T(8,128)(2,1)}, u32[]{:S(2)}) copy-start(bf16[4,256,512]{2,1,0:T(8,128)(2,1)} %copy-done.6) | copy-start | bytes 3145732
  78.6 6.6 %collective-permute-start = (bf16[336,256]{1,0:T(8,128)(2,1)S(1)}, bf16[336,256]{1,0:T(8,128)(2,1)S(1)}, u32[]{:S(2)}, u32[]{:S(2)}) collective-permute-start(bf16[336,256]{1,0:T(8,128)(2,1)S(1)} %get-tuple-element.29), channel_id=1, source_target_pairs={{0,2},{2,0},{4,6},{6,4},{8,10},{10,8},{12,14},{14,12},{16,18},{18,... | collective-permute-start | bytes 516104 | tf_op jit(solution)/shard_map/ppermute | solution.py:363
  79.2 8.5 %collective-permute-start.1 = (bf16[336,256]{1,0:T(8,128)(2,1)S(1)}, bf16[336,256]{1,0:T(8,128)(2,1)S(1)}, u32[]{:S(2)}, u32[]{:S(2)}) collective-permute-start(bf16[336,256]{1,0:T(8,128)(2,1)S(1)} %get-tuple-element.30), channel_id=1, source_target_pairs={{0,4},{2,6},{4,0},{6,2},{8,12},{10,14},{12,8},{14,10},{16,20},{18,... | collective-permute-start | bytes 516104 | tf_op jit(solution)/shard_map/ppermute | solution.py:363
  80.0 7.7 %collective-permute-start.2 = (bf16[336,256]{1,0:T(8,128)(2,1)S(1)}, bf16[336,256]{1,0:T(8,128)(2,1)S(1)}, u32[]{:S(2)}, u32[]{:S(2)}) collective-permute-start(bf16[336,256]{1,0:T(8,128)(2,1)S(1)} %get-tuple-element.31), channel_id=1, source_target_pairs={{0,6},{2,4},{4,2},{6,0},{8,14},{10,12},{12,10},{14,8},{16,22},{18,... | collective-permute-start | bytes 516104 | tf_op jit(solution)/shard_map/ppermute | solution.py:363
  87.9 5.5 %collective-permute-start.3 = (bf16[336,256]{1,0:T(8,128)(2,1)S(1)}, bf16[336,256]{1,0:T(8,128)(2,1)S(1)}, u32[]{:S(2)}, u32[]{:S(2)}) collective-permute-start(bf16[336,256]{1,0:T(8,128)(2,1)S(1)} %add_convert_fusion.rest_0_), channel_id=1, source_target_pairs={{0,2},{2,0},{4,6},{6,4},{8,10},{10,8},{12,14},{14,12},{16,18},{18,... | collective-permute-start | bytes 516104 | tf_op jit(solution)/shard_map/ppermute | solution.py:365
  88.7 6.2 %collective-permute-start.4 = (bf16[336,256]{1,0:T(8,128)(2,1)S(1)}, bf16[336,256]{1,0:T(8,128)(2,1)S(1)}, u32[]{:S(2)}, u32[]{:S(2)}) collective-permute-start(bf16[336,256]{1,0:T(8,128)(2,1)S(1)} %add_convert_fusion.rest_0_), channel_id=1, source_target_pairs={{0,4},{2,6},{4,0},{6,2},{8,12},{10,14},{12,8},{14,10},{16,20},{18,... | collective-permute-start | bytes 516104 | tf_op jit(solution)/shard_map/ppermute | solution.py:365
  90.1 6.3 %collective-permute-start.5 = (bf16[336,256]{1,0:T(8,128)(2,1)S(1)}, bf16[336,256]{1,0:T(8,128)(2,1)S(1)}, u32[]{:S(2)}, u32[]{:S(2)}) collective-permute-start(bf16[336,256]{1,0:T(8,128)(2,1)S(1)} %add_convert_fusion.rest_0_), channel_id=1, source_target_pairs={{0,6},{2,4},{4,2},{6,0},{8,14},{10,12},{12,10},{14,8},{16,22},{18,... | collective-permute-start | bytes 516104 | tf_op jit(solution)/shard_map/ppermute | solution.py:365
  (1 other events, 1.0 us)

commit v3 on v2

--- a/solution.py
+++ b/solution.py
@@ -76,9 +76,83 @@
     return all_ref[mate, table_at : table_at + TABLE_ROWS, :].astype(f32)
 
 
+def lane_blocks(table, group, rows, row_of):
+    bands, cap = table.shape
+    r = lax.broadcasted_iota(jnp.int32, (rows, bands), 0)
+    b = lax.broadcasted_iota(jnp.int32, (rows, bands), 1)
+    slot = lax.broadcasted_iota(jnp.int32, (cap, LANES), 0)
+    lane = lax.broadcasted_iota(jnp.int32, (cap, LANES), 1)
+    out = jnp.zeros((rows, LANES), f32)
+    for j in range(group):
+        rows_j = mm(jnp.where(row_of(r, j) == b, 1.0, 0.0).astype(bf16), table, 1, 0).astype(bf16)
+        out = out + mm(rows_j, one_hot(lane, slot + j * cap), 1, 0)
+    return out
+
+
+def column_order(table_ref, group):
+    table = table_ref[0].astype(f32).astype(bf16)
+    crew = table.shape[0] // group
+    return lane_blocks(table, group, 8, lambda r, j: jnp.where(r < crew, j * crew + r, -1)), crew
+
+
+def send_copies(group, crew, block_ref, out_ref, sems):
+    return [
+        pltpu.make_async_copy(block_ref, out_ref.at[j * crew : (j + 1) * crew], sems.at[j]) for j in range(group)
+    ]
+
+
+def encode_kernel(group, ready, field_ref, noise_ref, send_ref, recv_ref, mesh_ref, out_ref, block_ref, sems):
+    channels, grid_rows = field_ref.shape
+    ready(0, 1, 2, 3, 4)
+    inputs = (field_ref[...] + noise_ref[0].astype(f32)).astype(bf16) * 0.5
+    order, crew = column_order(send_ref, group)
+    subs = lax.broadcasted_iota(jnp.int32, (grid_rows, LANES), 0).astype(f32)
+    bands = recv_ref.shape[1]
+    rows = bands // group
+    recv = recv_ref[0].astype(f32).astype(bf16)
+    mesh = mesh_ref[0].astype(f32).astype(bf16)
+    table = lane_blocks(recv, group, TABLE_ROWS, lambda r, j: jnp.where(r < rows, r * group + j, -1))
+    table = table + lane_blocks(
+        mesh,
+        group,
+        TABLE_ROWS,
+        lambda r, j: jnp.where((r >= rows) & (r < 2 * rows), (r - rows) * group + j, -1),
+    )
+    for c in range(crew):
+        pick = one_hot(subs, order[c : c + 1, :])
+        block_ref[c, 0:channels, :] = mm(inputs, pick, 1, 0).astype(bf16)
+        block_ref[c, channels:, :] = table.astype(bf16)
+    copies = send_copies(group, crew, block_ref, out_ref, sems)
+    for copy in copies:
+        copy.start()
+    for copy in copies:
+        copy.wait()
+
+
+def loss_kernel(
+    group, student_ref, pred_ref, target_ref, weight_ref, inverse_ref, recv_ref, out_ref, block_ref, sems
+):
+    grid_rows = student_ref.shape[1]
+    student = student_ref[...]
+    terms = jnp.zeros_like(student)
+    for j in range(pred_ref.shape[0]):
+        terms = terms + slope(student - target_ref[j].astype(f32)) - slope(student - pred_ref[j])
+    scaled = (weight_ref[...].astype(f32) * terms * inverse_ref[...]).astype(bf16)
+    order, crew = column_order(recv_ref, group)
+    subs = lax.broadcasted_iota(jnp.int32, (grid_rows, LANES), 0).astype(f32)
+    for c in range(crew):
+        block_ref[c] = mm(scaled, one_hot(subs, order[c : c + 1, :]), 1, 0).astype(bf16)
+    copies = send_copies(group, crew, block_ref, out_ref, sems)
+    for copy in copies:
+        copy.start()
+    for copy in copies:
+        copy.wait()
+
+
 def forward_kernel(
     group,
     channels,
+    ready,
     me_ref,
     all_ref,
     lift_ref,
@@ -92,7 +166,15 @@
     own_ref,
     own_pre_ref,
     chosen_ref,
+    table_ref,
     slot_ref,
+    normed_buf,
+    slope_buf,
+    state_buf,
+    own_buf,
+    own_pre_buf,
+    sems,
+    own_sems,
 ):
     bands = all_ref.shape[0]
     node_rows, width = normed_ref.shape[1], normed_ref.shape[2]
@@ -103,36 +185,50 @@
 
     def embed(b, carry):
         latent = mm(all_ref[b, 0:channels, :], lift_ref[...], 0, 0)
-        latent = (latent * sigmoid(latent)).astype(bf16)
+        latent = (latent + latent * jnp.tanh(latent)).astype(bf16)
         slot_ref[:, pl.ds(pl.multiple_of(b * cap, cap), cap), :] = latent.reshape(group, cap, width)
         return carry
 
-    lax.fori_loop(0, bands, embed, 0)
-
-    def nodes(s, carry):
+    lax.fori_loop(0, bands, embed, 0, unroll=4)
+    ready(2, 3, 4, 5)
+    kept = [(normed_buf, normed_ref), (slope_buf, slope_ref), (state_buf, state_ref)]
+    own_copies = [
+        pltpu.make_async_copy(own_buf, own_ref, own_sems.at[0]),
+        pltpu.make_async_copy(own_pre_buf, own_pre_ref, own_sems.at[1]),
+    ]
+
+    def copies(s):
+        return [pltpu.make_async_copy(a.at[s], b.at[s], sems.at[i, s]) for i, (a, b) in enumerate(kept)]
+
+    def nodes(i, carry):
+        s = lax.rem(z + i, group)
         table = table_rows(all_ref, bands, group, xy, s, channels)
+        table_ref[s] = table
         parts = slots // LANES
-        hot = [jnp.where(subs == table[j : j + 1, :], 1.0, 0.0) for j in range(parts)]
-        count = sum(jnp.sum(h, axis=1, keepdims=True) for h in hot)
-        landing = jnp.concatenate(hot, axis=1).astype(bf16)
-        state = mm(landing, slot_ref[s], 1, 0) / jnp.maximum(count, 1.0)
+        landing = jnp.concatenate([one_hot(subs, table[j : j + 1, :]) for j in range(parts)], axis=1)
+        count = mm(landing, jnp.ones((slots, LANES), bf16), 1, 0)[:, 0:1]
+        state = mm(landing, slot_ref[s], 1, 0) * (1.0 / jnp.maximum(count, 1.0))
         recip = lax.rsqrt(jnp.mean(state * state, axis=1, keepdims=True) + norm_eps)
         normed = (state * recip * scale_ref[...]).astype(bf16)
-        normed_ref[s] = normed
+        normed_buf[s] = normed
         pre = mm(normed, expand_ref[...], 1, 0)
-        gate = sigmoid(pre)
-        hidden = pre * gate
-        slope_ref[s] = (gate + hidden * (1.0 - gate)).astype(bf16)
-        hidden = hidden.astype(bf16)
+        bent = jnp.tanh(pre)
+        above = 1.0 + bent
+        slope_buf[s] = (above * (1.0 + pre * (1.0 - bent))).astype(bf16)
+        hidden = (pre * above).astype(bf16)
         following = (state + mm(hidden, contract_ref[...], 1, 0)).astype(bf16)
-        state_ref[s, :, 0:width] = following
-        state_ref[s, :, width:] = hidden
-
-        @pl.when(s == z)
+        state_buf[s, :, 0:width] = following
+        state_buf[s, :, width:] = hidden
+        for copy in copies(s):
+            copy.start()
+
+        @pl.when(i == 0)
         def _():
-            own_ref[...] = state
-            own_pre_ref[...] = pre
-            projected = mm(following, readout_ref[...], 1, 0).astype(bf16)
+            own_buf[...] = state
+            own_pre_buf[...] = pre
+            for copy in own_copies:
+                copy.start()
+            projected = mm(following, readout_ref[...], 1, 1).astype(bf16)
             for j in range(parts):
                 pick = one_hot(subs, table[parts + j : parts + j + 1, :])
                 chosen_ref[j * LANES : (j + 1) * LANES, :] = mm(pick, projected, 0, 0).astype(bf16)
@@ -140,6 +236,11 @@
         return carry
 
     lax.fori_loop(0, group, nodes, 0)
+    for copy in own_copies:
+        copy.wait()
+    for s in range(group):
+        for copy in copies(s):
+            copy.wait()
 
 
 def backward_kernel(
@@ -147,7 +248,7 @@
     channels,
     me_ref,
     grad_ref,
-    all_ref,
+    table_ref,
     chain_ref,
     normed_ref,
     slope_ref,
@@ -155,25 +256,31 @@
     own_ref,
     *rest,
 ):
-    piece_refs, (value_ref, up_ref, small_ref) = rest[:-3], rest[-3:]
+    piece_refs, (value_ref, node_ref, up_ref, small_ref, normed_buf, slope_buf, state_buf, sems) = rest[:-8], rest[-8:]
     bands = grad_ref.shape[0]
     slots = value_ref.shape[1]
     node_rows, width = normed_ref.shape[1], normed_ref.shape[2]
     cap = slots // bands
     z, xy = me_ref[0], me_ref[1]
     subs = lax.broadcasted_iota(jnp.int32, (node_rows, LANES), 0).astype(f32)
+    kept = [(slope_ref, slope_buf), (normed_ref, normed_buf), (state_ref, state_buf)]
+
+    def copies(s):
+        return [pltpu.make_async_copy(a.at[s], b.at[s], sems.at[i, s]) for i, (a, b) in enumerate(kept)]
+
+    for s in range(group):
+        for copy in copies(s):
+            copy.start()
 
     def turn(b, carry):
         values = grad_ref[b].astype(f32).T.astype(bf16)
         value_ref[:, pl.ds(pl.multiple_of(b * cap, cap), cap), :] = values.reshape(group, cap, channels)
         return carry
 
-    lax.fori_loop(0, bands, turn, 0)
-    up_ref[...] = jnp.zeros_like(up_ref)
-    small_ref[...] = jnp.zeros_like(small_ref)
+    lax.fori_loop(0, bands, turn, 0, unroll=4)
 
     def nodes(s, carry):
-        table = table_rows(all_ref, bands, group, xy, s, channels)
+        table = table_ref[s]
         parts = slots // LANES
         pick = jnp.concatenate(
             [one_hot(subs, table[parts + j : parts + j + 1, :]) for j in range(parts)], axis=1
@@ -185,12 +292,20 @@
             own_ref[...] = node_grad
 
         node_b = node_grad.astype(bf16)
-        pre = (mm(node_b, chain_ref[...], 1, 1) * slope_ref[s].astype(f32)).astype(bf16)
-        up_ref[...] += mm(normed_ref[s], pre, 0, 0)
-        small_ref[...] += mm(node_b, state_ref[s], 0, 0)
+        at = pl.ds(pl.multiple_of(s * node_rows, node_rows), node_rows)
+        node_ref[at, :] = node_b
+        copies(s)[0].wait()
+        pre = mm(node_b, chain_ref[...], 1, 0)
+        slope_buf[s] = (pre * slope_buf[s].astype(f32)).astype(bf16)
         return carry
 
     lax.fori_loop(0, group, nodes, 0)
+    for s in range(group):
+        for copy in copies(s)[1:]:
+            copy.wait()
+    everything = (group * node_rows, -1)
+    up_ref[...] = 2.0 * mm(normed_buf[...].reshape(everything), slope_buf[...].reshape(everything), 0, 0)
+    small_ref[...] = mm(node_ref[...], state_buf[...].reshape(everything), 0, 0)
     count = len(piece_refs)
     rows = up_ref.shape[0] // count
     half = up_ref.shape[1] // 2
@@ -204,57 +319,88 @@
 
 
 def finish_kernel(factor, channels, me_ref, scale_ref, expand_ref, readout_ref, *rest):
-    count = len(rest) - 5
-    piece_refs, (up_ref, down_ref, dec_ref, gain_ref, small_ref) = rest[:count], rest[count:]
+    count = len(rest) - 8
+    piece_refs = rest[:count]
+    up_out, down_out, dec_ref, gain_ref, small_ref, up_ref, down_ref, sems = rest[count:]
     rows = up_ref.shape[0] // count
     half = up_ref.shape[1] // 2
     lanes = small_ref.shape[1] // count
+    width = up_ref.shape[0]
+    places = [pl.ds(pl.multiple_of((me_ref[1] ^ p) * rows, rows), rows) for p in range(count)]
+    up_copies = [pltpu.make_async_copy(up_ref.at[at], up_out.at[at], sems.at[0, p]) for p, at in enumerate(places)]
+    down_copies = [
+        pltpu.make_async_copy(down_ref.at[at], down_out.at[at], sems.at[1, p])
+        for p, at in enumerate(pl.ds(p * rows, rows) for p in range(count))
+    ]
     for p, piece_ref in enumerate(piece_refs):
-        to = me_ref[1] ^ p
-        at = pl.ds(pl.multiple_of(to * rows, rows), rows)
-        left = piece_ref[0:rows, :].astype(f32) * factor
-        right = piece_ref[rows : 2 * rows, :].astype(f32) * factor
-        up_ref[at, 0:half] = left
-        up_ref[at, half:] = right
-        small_ref[:, pl.ds(pl.multiple_of(to * lanes, lanes), lanes)] = piece_ref[2 * rows :, :].astype(f32) * factor
-        gain = jnp.sum(left * expand_ref[at, 0:half].astype(f32), axis=1, keepdims=True)
-        gain = gain + jnp.sum(right * expand_ref[at, half:].astype(f32), axis=1, keepdims=True)
-        gain_ref[at, :] = gain / scale_ref[at, :]
-    width = up_ref.shape[0]
-    dec_ref[...] = small_ref[:, 0:width].T
-    hidden = small_ref[:, width:]
-    high = hidden.astype(bf16)
-    low = (hidden - high.astype(f32)).astype(bf16)
-    down_ref[...] = mm(high, readout_ref[...], 0, 1) + mm(low, readout_ref[...], 0, 1)
-
-
-def vmem_call(kernel, outs, name, scratch=(), budget=16):
+        up_ref[places[p], 0:half] = piece_ref[0:rows, :].astype(f32) * factor
+        up_ref[places[p], half:] = piece_ref[rows : 2 * rows, :].astype(f32) * factor
+        up_copies[p].start()
+        at = pl.ds(pl.multiple_of((me_ref[1] ^ p) * lanes, lanes), lanes)
+        small_ref[:, at] = piece_ref[2 * rows :, :].astype(f32) * factor
+    high = small_ref[:, width:].astype(bf16)
+    low = (small_ref[:, width:] - high.astype(f32)).astype(bf16)
+    for p in range(count):
+        at = slice(p * rows, (p + 1) * rows)
+        down_ref[at, :] = mm(high[:, at], readout_ref[...], 0, 0) + mm(low[:, at], readout_ref[...], 0, 0)
+        down_copies[p].start()
+    dec_ref[...] = small_ref[:, 0:width]
+    for at in places:
+        gain = up_ref[at, :] * expand_ref[at, :].astype(f32)
+        gain = sum(gain[:, j : j + LANES] for j in range(0, 2 * half, LANES))
+        gain_ref[:, at] = jnp.sum(gain.T, axis=0, keepdims=True) / scale_ref[:, at]
+    for copy in up_copies + down_copies:
+        copy.wait()
+
+
+def vmem_call(kernel, outs, name, scratch=(), sems=(), budget=24, left_in=(), left_out=(), fetched=()):
     vmem = pl.BlockSpec(memory_space=pltpu.VMEM)
     smem = pl.BlockSpec(memory_space=pltpu.SMEM)
+    left = pl.BlockSpec(memory_space=pltpu.HBM)
+    fetched = list(fetched)
 
     def call(scalars, *operands):
+        first = 0 if scalars is None else 1
+        outside = set(left_in) | set(fetched)
+
+        def run(*refs):
+            refs = list(refs)
+            if fetched:
+                bufs, sem = refs[-1 - len(fetched) : -1], refs[-1]
+                refs = refs[: -1 - len(fetched)]
+                copies = {
+                    at: pltpu.make_async_copy(refs[first + at], buf, sem.at[i])
+                    for i, (at, buf) in enumerate(zip(fetched, bufs))
+                }
+                for at, buf in zip(fetched, bufs):
+                    copies[at].start()
+                    refs[first + at] = buf
+
+                def ready(*which):
+                    for at in which:
+                        copies[at].wait()
+
+                kernel(ready, *refs)
+            else:
+                kernel(*refs)
+
         return pl.pallas_call(
-            kernel,
-            out_shape=[jax.ShapeDtypeStruct(s, d) for s, d in outs],
-            in_specs=[smem] + [vmem] * len(operands),
-            out_specs=[vmem] * len(outs),
-            scratch_shapes=[pltpu.VMEM(s, d) for s, d in scratch],
+            run,
+            out_shape=[(pltpu.HBM if i in left_out else jax.ShapeDtypeStruct)(s, d) for i, (s, d) in enumerate(outs)],
+            in_specs=[smem] * first + [left if i in outside else vmem for i in range(len(operands))],
+            out_specs=[left if i in left_out else vmem for i in range(len(outs))],
+            scratch_shapes=[pltpu.VMEM(s, d) for s, d in scratch]
+            + [pltpu.SemaphoreType.DMA(s) for s in sems]
+            + [pltpu.VMEM(operands[i].shape, operands[i].dtype) for i in fetched]
+            + ([pltpu.SemaphoreType.DMA((len(fetched),))] if fetched else []),
             compiler_params=pltpu.CompilerParams(vmem_limit_bytes=budget * 2**20),
             name=name,
-        )(scalars, *operands)
+        )(
+            *([] if scalars is None else [scalars]),
+            *[pltpu.with_memory_space_constraint(x, pltpu.HBM) if i in outside else x for i, x in enumerate(operands)],
+        )
 
     return call
-
-
-def to_column(x, bands, group):
-    channels = x.shape[0]
-    blocks = x.reshape(channels, bands // group, -1).transpose(1, 0, 2)
-    return jnp.broadcast_to(blocks[None], (group,) + blocks.shape).reshape(bands, channels, -1)
-
-
-def by_column(table, group):
-    bands, cap = table.shape
-    return table.reshape(group, bands // group, cap).transpose(1, 0, 2).reshape(-1)
 
 
 def all_to_all(x):
@@ -311,43 +457,56 @@
     band = lax.axis_index("band").astype(jnp.int32)
     me = jnp.stack([band // crew, band % crew])
     cell_ids = jnp.arange(grid_rows, dtype=jnp.int32)
-    inputs_b = (scaled_atmosphere_field + perturbation[0].astype(f32)).astype(bf16)
-    picker = (cell_ids[:, None] == by_column(enc_send[0], group)[None, :]).astype(bf16)
-    outgoing = to_column(mm(inputs_b, picker, 1, 0).astype(bf16), bands, group)
-    tables = jnp.concatenate([enc_recv[0].reshape(-1, LANES), dec_send[0].reshape(-1, LANES)]).astype(bf16)
-    tables = jnp.pad(tables, ((0, TABLE_ROWS - tables.shape[0]), (0, 0)))
-    tables = jnp.broadcast_to(tables[None], (bands,) + tables.shape)
-    arrived = all_to_all(jnp.concatenate([outgoing, tables], axis=1))
-    normed, slopes, states, mesh_state, hidden_pre, chosen = vmem_call(
+    block = (crew, channels + TABLE_ROWS, LANES)
+    outgoing = vmem_call(
+        functools.partial(encode_kernel, group),
+        [((bands, channels + TABLE_ROWS, LANES), bf16)],
+        "encode",
+        scratch=[(block, bf16)],
+        sems=[(group,)],
+        left_out=(0,),
+        fetched=range(5),
+    )(None, scaled_atmosphere_field, perturbation, enc_send, enc_recv, dec_send)[0]
+    arrived = all_to_all(outgoing)
+    kept = [
+        ((group, node_rows, width), bf16),
+        ((group, node_rows, hid), bf16),
+        ((group, node_rows, width + hid), bf16),
+    ]
+    own = [((node_rows, width), f32), ((node_rows, hid), f32)]
+    normed, slopes, states, mesh_state, half_pre, chosen, column_tables = vmem_call(
         functools.partial(forward_kernel, group, channels),
-        [
-            ((group, node_rows, width), bf16),
-            ((group, node_rows, hid), bf16),
-            ((group, node_rows, width + hid), bf16),
-            ((node_rows, width), f32),
-            ((node_rows, hid), f32),
-            ((slots, channels), bf16),
-        ],
+        kept + own + [((slots, channels), bf16), ((group, TABLE_ROWS, LANES), f32)],
         "forward",
-        scratch=[((group, slots, width), bf16)],
+        scratch=[((group, slots, width), bf16)] + kept + own,
+        sems=[(3, group), (2,)],
+        left_out=range(5),
+        fetched=(2, 3, 4, 5),
     )(
         me,
         arrived,
         lattice_lift_matrix,
-        mixing_rescale_factor[None, :],
+        0.5 * mixing_rescale_factor[None, :],
         expand_matrix,
         contract_matrix,
-        readout_matrix,
-    )
-    chain = mm(contract_matrix, readout_matrix, 1, 0).astype(bf16)
+        readout_matrix.T,
+    )
+    chain = (0.5 * mm(readout_matrix, contract_matrix, 0, 1)).astype(bf16)
     slot_values = exchange(chosen, bands)
     fill_map = (cell_ids[:, None] == dec_recv[0].reshape(-1)[None, :]).astype(bf16)
     inverse = 1.0 / jnp.maximum(jnp.sum(fill_map.astype(f32), axis=1), 1.0)
     student_outputs = scaled_atmosphere_field + mm(slot_values, fill_map, 0, 1) * inverse[None, :]
-    pred_grad = member_terms(student_outputs, target, weight_map)
-    scaled = (pred_grad * inverse[None, :]).astype(bf16)
-    spread_map = (cell_ids[:, None] == by_column(dec_recv[0], group)[None, :]).astype(bf16)
-    returned = all_to_all(to_column(mm(scaled, spread_map, 1, 0).astype(bf16), bands, group))
+    all_pred = lax.all_gather(student_outputs, "member", axis=0)
+    all_target = lax.all_gather(target[0], "member", axis=0)
+    outgoing = vmem_call(
+        functools.partial(loss_kernel, group),
+        [((bands, channels, LANES), bf16)],
+        "loss",
+        scratch=[((crew, channels, LANES), bf16)],
+        sems=[(group,)],
+        left_out=(0,),
+    )(None, student_outputs, all_pred, all_target, weight_map, inverse[None, :], dec_recv)[0]
+    returned = all_to_all(outgoing)
     piece_rows = 2 * (width // crew) + channels
     node_grad, *pieces = vmem_call(
         functools.partial(backward_kernel, group, channels),
@@ -355,31 +514,45 @@
         "backward",
         scratch=[
             ((group, slots, channels), bf16),
+            ((group * node_rows, channels), bf16),
             ((width, hid), f32),
             ((channels, width + hid), f32),
+            kept[0],
+            kept[1],
+            kept[2],
         ],
-    )(me, returned, arrived, chain, normed, slopes, states)
+        sems=[(3, group)],
+        left_in=(3, 4, 5),
+    )(me, returned, column_tables, chain, normed, slopes, states)
     swaps = [[(i, i ^ p) for i in range(bands)] for p in range(1, crew)]
     others = [lax.ppermute(piece, "band", swap) for piece, swap in zip(pieces[1:], swaps)]
     total = sum(x.astype(f32) for x in [pieces[0]] + others).astype(bf16)
     totals = [total] + [lax.ppermute(total, "band", swap) for swap in swaps]
     state_grad = state_gradient(
-        node_grad, mesh_state, hidden_pre, mixing_rescale_factor, expand_matrix, contract_matrix, readout_matrix
+        node_grad,
+        mesh_state,
+        2.0 * half_pre,
+        mixing_rescale_factor,
+        expand_matrix,
+        contract_matrix,
+        readout_matrix,
     )
     factor = 1.0 / math.sqrt(bands * node_rows)
     grad_up, grad_down, grad_dec, grad_gain = vmem_call(
         functools.partial(finish_kernel, factor, channels),
-        [((width, hid), f32), ((hid, width), f32), ((width, channels), f32), ((width, 1), f32)],
+        [((width, hid), f32), ((hid, width), f32), ((channels, width), f32), ((1, width), f32)],
         "finish",
-        scratch=[((channels, width + hid), f32)],
-    )(me, mixing_rescale_factor[:, None], expand_matrix, readout_matrix, *totals)
+        scratch=[((channels, width + hid), f32), ((width, hid), f32), ((hid, width), f32)],
+        sems=[(2, crew)],
+        left_out=(0, 1),
+    )(me, mixing_rescale_factor[None, :], expand_matrix, readout_matrix.T, *totals)
     return (
         student_outputs[None],
         state_grad[None],
         grad_up[None],
         grad_down[None],
-        grad_dec[None],
-        grad_gain[:, 0][None],
+        grad_dec.T[None],
+        grad_gain,
     )
 
 

time: 101 us -> 88.7 us (0.88)
  local copies, waits for them, and re-layouts: 10.6 us -> 2.31 us
  waiting for transfers between devices: 36.9 us -> 34.3 us
  Pallas kernels: 17 us -> 18.9 us
  other arithmetic: 4.2 us -> 2.48 us
  matrix products: 3.8 us -> 2.44 us
    unnamed x34 -> x22, local copies, waits for them, and re-layouts: 8.26 us -> 1.5 us
    pallas_call x3 -> x5, Pallas kernels: 17 us -> 18.9 us  [call(): pl.pallas_call(run, out_shape=[(pltpu.HBM if i in left_out else jax.Shape...]
    all_to_all x2, waiting for transfers between devices: 21.5 us -> 19.8 us  [all_to_all(): return lax.all_to_all(x, 'band', split_axis=0, concat_axis=0, tiled=True)]
    another operation x2 -> x0, other arithmetic: 1.4 us -> none
    dot_general x10 -> x8, matrix products: 3.8 us -> 2.44 us  [mm(): lax.dot_general(a, b, (((ca,), (cb,)), ((), ())), preferred_element_type=...]
    mul x0 -> x1, other arithmetic: none -> 1.26 us  [column_body(): 0.5 * mixing_rescale_factor[None, :]]
  transfers between devices with their start and end apart: 9 -> 9, of which waited for: 8 -> 7; matrix products, arithmetic and copies ran while one was open for 4% -> 6% of each run, Pallas kernels for 0% -> 0%
where the time goes in v3:
time: 88.7 us; the launch traced here: 88.1 us
  waiting for transfers between devices  34.3 us (39%)
  starting transfers between devices  22.7 us (26%)
  Pallas kernels  18.9 us (21%)
  blocking collectives  3.99 us (4%)
  other arithmetic  2.48 us (3%)
  matrix products  2.44 us (3%)
  local copies, waits for them, and re-layouts  2.31 us (3%)
  between operations  0.91 us (1%)
    all_to_all x2, waiting for transfers between devices, all_to_all(): return lax.all_to_all(x, 'band', split_axis=0, concat_axis=0, tiled=True)  19.8 us
    pallas_call x5, Pallas kernels, call(): pl.pallas_call(run, out_shape=[(pltpu.HBM if i in left_out else jax.Shape...  18.9 us
    all_to_all x2, starting transfers between devices, all_to_all(): return lax.all_to_all(x, 'band', split_axis=0, concat_axis=0, tiled=True)  12 us
    all_to_all x1, waiting for transfers between devices, exchange(): lax.all_to_all(x.reshape(band_count, rows // band_count, width), 'band',...  7.78 us
    ppermute x3, waiting for transfers between devices, column_body(): totals = [total] + [lax.ppermute(total, 'band', swap) for swap in swaps]  3.77 us
    all_to_all x1, starting transfers between devices, exchange(): lax.all_to_all(x.reshape(band_count, rows // band_count, width), 'band',...  3.6 us
    ppermute x3, starting transfers between devices, column_body(): totals = [total] + [lax.ppermute(total, 'band', swap) for swap in swaps]  3.55 us
    ppermute x3, starting transfers between devices, column_body(): lax.ppermute(piece, 'band', swap)  3.55 us
  transfers between devices with their start and end apart: 9, of which 7 were waited for; matrix products, arithmetic and copies ran while one was open for 6% of the time, Pallas kernels for 0%

profile of v3, /device:TPU:0, one launch (start us, length us, event | category | flops | bytes accessed | tf_op | source)
XLA Modules:
  0.0 88.1 jit_solution(11940728041468940488)
XLA Ops:
  0.7 2.3 %encode.1 = bf16[16,96,128]{2,1,0:T(8,128)(2,1)} custom-call(f32[80,256]{1,0:T(8,128)} %refs_0_.1, bf16[1,80,256]{2,1,0:T(8,128)(2,1)} %refs_1_.1, s32[1,16,32]{2,1,0:T(8,128)} %refs_2_.3, s32[1,16,32]{2,1,0:T(8,128)} %refs_3_.2, s32[1,16,32]{2,1,0:T(8,128)} %refs_4_.2), custom_call_target="tpu_custom_call" | custom-call | tf_op jit(solution)/shard_map/encode/pallas_call | solution.py:387
  3.0 8.5 %all-to-all-start = ((bf16[16,96,128]{2,1,0:T(8,128)(2,1)}), bf16[16,96,128]{2,1,0:T(8,128)(2,1)S(1)}, u32[]{:S(2)}, u32[]{:S(2)}) async-start(bf16[16,96,128]{2,1,0:T(8,128)(2,1)} %encode.1), calls=%async_computation | async-start | bytes 786432 | tf_op jit(solution)/shard_map/all_to_all | solution.py:407
  11.5 0.8 eq.18
  12.3 2.1 %all_gather.8.refs_2_ = bf16[2,80,256]{2,1,0:T(8,128)(2,1)S(1)} all-gather(bf16[1,80,256]{2,1,0:T(8,128)(2,1)} %param.15), channel_id=1, replica_groups=mesh['band'=16,'member'=2] {'member'}, dimensions={0}, use_global_device_ids=true | all-gather | bytes 122880 | tf_op jit(solution)/shard_map/all_gather | solution.py:500
  14.6 1.3 %broadcast_multiply_fusion = f32[512]{0:T(512)} fusion(f32[512]{0:T(512)} %param.22), kind=kLoop, calls=%fused_computation.34 | loop fusion | flops 512 | bytes 4096 | tf_op jit(solution)/shard_map/mul | solution.py:489
  15.9 8.2 %all-to-all-done.refs_1_ = bf16[16,96,128]{2,1,0:T(8,128)(2,1)S(1)} async-done(((bf16[16,96,128]{2,1,0:T(8,128)(2,1)}), bf16[16,96,128]{2,1,0:T(8,128)(2,1)S(1)}, u32[]{:S(2)}, u32[]{:S(2)}) %all-to-all-start) | async-done | bytes 393248 | tf_op jit(solution)/shard_map/all_to_all | solution.py:407
  24.1 0.9 %copy-done.3 = bf16[80,512]{1,0:T(8,128)(2,1)S(1)} copy-done((bf16[80,512]{1,0:T(8,128)(2,1)S(1)}, bf16[80,512]{1,0:T(8,128)(2,1)}, u32[]{:S(2)}) %copy-start.3) | copy-done | bytes 81944
  25.0 8.1 %forward.1 = (bf16[4,256,512]{2,1,0:T(8,128)(2,1)}, bf16[4,256,512]{2,1,0:T(8,128)(2,1)}, bf16[4,256,1024]{2,1,0:T(8,128)(2,1)}, f32[256,512]{1,0:T(8,128)}, f32...) custom-call(s32[2]{0:T(128)S(1)} %pad_add_fusion.refs_0_, ...), custom_call_target="tpu_custom_call" | custom-call | tf_op jit(solution)/shard_map/forward/pallas_call | solution.py:387
  33.1 3.6 %all-to-all-start.1 = ((bf16[16,32,80]{2,1,0:T(8,128)(2,1)}), bf16[16,32,80]{2,1,0:T(8,128)(2,1)S(1)}, u32[]{:S(2)}, u32[]{:S(2)}) async-start(bf16[16,32,80]{2,1,0:T(8,128)(2,1)} %bitcast.4), calls=%async_computation.1 | async-start | bytes 262144 | tf_op jit(solution)/shard_map/all_to_all | solution.py:41
  36.8 7.8 %all-to-all-done.1 = bf16[16,32,80]{2,1,0:T(8,128)(2,1)S(1)} async-done(((bf16[16,32,80]{2,1,0:T(8,128)(2,1)}), bf16[16,32,80]{2,1,0:T(8,128)(2,1)S(1)}, u32[]{:S(2)}, u32[]{:S(2)}) %all-to-all-start.1) | async-done | bytes 81952 | tf_op jit(solution)/shard_map/all_to_all | solution.py:41
  44.8 1.9 %all-gather = f32[160,256]{1,0:T(8,128)S(1)} all-gather(f32[80,256]{1,0:T(8,128)S(1)} %fusion.4.refs_0_), channel_id=2, replica_groups=mesh['band'=16,'member'=2] {'member'}, dimensions={0}, use_global_device_ids=true | all-gather | bytes 245760 | tf_op jit(solution)/shard_map/all_gather | solution.py:499
  46.7 1.3 %loss.1 = bf16[16,80,128]{2,1,0:T(8,128)(2,1)} custom-call(f32[80,256]{1,0:T(8,128)S(1)} %fusion.4.refs_0_, f32[2,80,256]{2,1,0:T(8,128)S(1)} %bitcast.28, bf16[2,80,256]{2,1,0:T(8,128)(2,1)S(1)} %all_gather.8.refs_2_, bf16[80,256]{1,0:T(8,128)(2,1)S(1)} %copy-done.4, f32[1,256]{1,0:T(1,128)S(1)} %bitcast.31, s32[1,16,32]{2,1,0:T(8,128)S(1)} %copy-done.5), custom_call_target="tpu_custom_call" | custom-call | tf_op jit(solution)/shard_map/loss/pallas_call | solution.py:387
  48.1 3.6 %all-to-all-start.2 = ((bf16[16,80,128]{2,1,0:T(8,128)(2,1)}), bf16[16,80,128]{2,1,0:T(8,128)(2,1)S(1)}, u32[]{:S(2)}, u32[]{:S(2)}) async-start(bf16[16,80,128]{2,1,0:T(8,128)(2,1)} %loss.1), calls=%async_computation.2 | async-start | bytes 655360 | tf_op jit(solution)/shard_map/all_to_all | solution.py:407
  51.9 11.5 %all-to-all-done.2.refs_1_ = bf16[16,80,128]{2,1,0:T(8,128)(2,1)S(1)} async-done(((bf16[16,80,128]{2,1,0:T(8,128)(2,1)}), bf16[16,80,128]{2,1,0:T(8,128)(2,1)S(1)}, u32[]{:S(2)}, u32[]{:S(2)}) %all-to-all-start.2) | async-done | bytes 327712 | tf_op jit(solution)/shard_map/all_to_all | solution.py:407
  63.5 4.3 %backward.1 = (f32[256,80]{1,0:T(8,128)S(1)}, bf16[336,256]{1,0:T(8,128)(2,1)S(1)}, bf16[336,256]{1,0:T(8,128)(2,1)S(1)}, bf16[336,256]{1,0:T(8,128)(2,1)S(1)}, bf16[336,256]{1,0:T(8,128)(2,1)S(1)}) custom-call(s32[2]{0:T(128)S(1)} %pad_add_fusion.refs_0_, bf16[16,80,128]{2,1,0:T(8,128)(2,1)S(1)} %all-to-all-done.2.refs_1_, ...), custom_call_target="tpu_custom_call" | custom-call | tf_op jit(solution)/shard_map/backward/pallas_call | solution.py:387
  68.4 0.8 collective-permute-start.1
  69.2 2.1 %collective-permute-start.2 = (bf16[336,256]{1,0:T(8,128)(2,1)S(1)}, bf16[336,256]{1,0:T(8,128)(2,1)S(1)}, u32[]{:S(2)}, u32[]{:S(2)}) collective-permute-start(bf16[336,256]{1,0:T(8,128)(2,1)S(1)} %get-tuple-element.33), channel_id=1, source_target_pairs={{0,6},{2,4},{4,2},{6,0},{8,14},{10,12},{12,10},{14,8},{16,22},{18,... | collective-permute-start | bytes 516104 | tf_op jit(solution)/shard_map/ppermute | solution.py:528
  74.4 2.5 %collective-permute-done.1 = bf16[336,256]{1,0:T(8,128)(2,1)S(1)} collective-permute-done((bf16[336,256]{1,0:T(8,128)(2,1)S(1)}, bf16[336,256]{1,0:T(8,128)(2,1)S(1)}, u32[]{:S(2)}, u32[]{:S(2)}) %collective-permute-start.1) | collective-permute-done | bytes 172064 | tf_op jit(solution)/shard_map/ppermute | solution.py:528
  77.0 1.6 %collective-permute-start.5 = (bf16[336,256]{1,0:T(8,128)(2,1)S(1)}, bf16[336,256]{1,0:T(8,128)(2,1)S(1)}, u32[]{:S(2)}, u32[]{:S(2)}) collective-permute-start(bf16[336,256]{1,0:T(8,128)(2,1)S(1)} %add_convert_fusion.refs_4_), channel_id=1, source_target_pairs={{0,6},{2,4},{4,2},{6,0},{8,14},{10,12},{12,10},{14,8},{16,22},{18,... | collective-permute-start | bytes 516104 | tf_op jit(solution)/shard_map/ppermute | solution.py:530
  79.3 1.3 %collective-permute-start.3 = (bf16[336,256]{1,0:T(8,128)(2,1)S(1)}, bf16[336,256]{1,0:T(8,128)(2,1)S(1)}, u32[]{:S(2)}, u32[]{:S(2)}) collective-permute-start(bf16[336,256]{1,0:T(8,128)(2,1)S(1)} %add_convert_fusion.refs_4_), channel_id=1, source_target_pairs={{0,2},{2,0},{4,6},{6,4},{8,10},{10,8},{12,14},{14,12},{16,18},{18,... | collective-permute-start | bytes 516104 | tf_op jit(solution)/shard_map/ppermute | solution.py:530
  80.6 0.9 %fusion.6 = bf16[1,256,512]{2,1,0:T(8,128)(2,1)} fusion(f32[256,512]{1,0:T(8,128)S(1)} %copy-done.8, f32[256,512]{1,0:T(8,128)S(1)} %convolution_add_fusion, f32[256,512]{1,0:T(8,128)S(1)} %get-tuple-element.42, f32[256]{0:T(256)S(1)} %broadcast_multiply_fusion.1, f32[256]{0:T(256)S(1)} %get-tuple-element.41, f32[256]{0:T(256)S(1)} %get-tuple-element.40), kind=kLoop, calls=%fused_computation.19 | loop fusion | flops 786432 | bytes 1838080 | tf_op jit(solution)/shard_map/broadcast_in_dim | solution.py:551
  81.5 2.0 %collective-permute-done.5.refs_7_ = bf16[336,256]{1,0:T(8,128)(2,1)S(1)} collective-permute-done((bf16[336,256]{1,0:T(8,128)(2,1)S(1)}, bf16[336,256]{1,0:T(8,128)(2,1)S(1)}, u32[]{:S(2)}, u32[]{:S(2)}) %collective-permute-start.5) | collective-permute-done | bytes 172064 | tf_op jit(solution)/shard_map/ppermute | solution.py:530
  83.5 1.7 %collective-permute-done.4.refs_6_ = bf16[336,256]{1,0:T(8,128)(2,1)S(1)} collective-permute-done((bf16[336,256]{1,0:T(8,128)(2,1)S(1)}, bf16[336,256]{1,0:T(8,128)(2,1)S(1)}, u32[]{:S(2)}, u32[]{:S(2)}) %collective-permute-start.4) | collective-permute-done | bytes 172064 | tf_op jit(solution)/shard_map/ppermute | solution.py:530
  85.2 2.8 %finish.1 = (f32[512,512]{1,0:T(8,128)}, f32[512,512]{1,0:T(8,128)}, f32[80,512]{1,0:T(8,128)}, f32[1,512]{1,0:T(1,128)}) custom-call(s32[2]{0:T(128)S(1)} %pad_add_fusion.refs_0_, f32[1,512]{1,0:T(1,128)S(1)} %bitcast.30, bf16[512,512]{1,0:T(8,128)(2,1)S(1)} %copy-done, bf16[80,512]{1,0:T(8,128)(2,1)S(1)} %bitcast.27, ...), custom_call_target="tpu_custom_call" | custom-call | tf_op jit(solution)/shard_map/finish/pallas_call | solution.py:387
  (40 shorter events, 5.1 us)
Async XLA Ops:
  0.6 43.9 %copy-start.9 = (f32[80,256]{1,0:T(8,128)S(1)}, f32[80,256]{1,0:T(8,128)}, u32[]{:S(2)}) copy-start(f32[80,256]{1,0:T(8,128)} %refs_0_.1) | copy-start | bytes 245764
  0.6 46.1 %copy-start.5 = (s32[1,16,32]{2,1,0:T(8,128)S(1)}, s32[1,16,32]{2,1,0:T(8,128)}, u32[]{:S(2)}) copy-start(s32[1,16,32]{2,1,0:T(8,128)} %refs_5_.3) | copy-start | bytes 6148
  0.7 46.1 %copy-start.4 = (bf16[80,256]{1,0:T(8,128)(2,1)S(1)}, bf16[80,256]{1,0:T(8,128)(2,1)}, u32[]{:S(2)}) copy-start(bf16[80,256]{1,0:T(8,128)(2,1)} %refs_3_.3) | copy-start | bytes 122884
  3.0 48.7 %copy-start.7 = (bf16[512,512]{1,0:T(8,128)(2,1)S(1)}, bf16[512,512]{1,0:T(8,128)(2,1)}, u32[]{:S(2)}) copy-start(bf16[512,512]{1,0:T(8,128)(2,1)} %refs_5_.2) | copy-start | bytes 1572868
  3.0 21.1 %all-to-all-start = ((bf16[16,96,128]{2,1,0:T(8,128)(2,1)}), bf16[16,96,128]{2,1,0:T(8,128)(2,1)S(1)}, u32[]{:S(2)}, u32[]{:S(2)}) async-start(bf16[16,96,128]{2,1,0:T(8,128)(2,1)} %encode.1), calls=%async_computation | async-start | bytes 786432 | tf_op jit(solution)/shard_map/all_to_all | solution.py:407
  11.5 40.2 %copy-start.1 = (bf16[512,80]{0,1:T(8,128)(2,1)S(1)}, bf16[512,80]{0,1:T(8,128)(2,1)}, u32[]{:S(2)}) copy-start(bf16[512,80]{0,1:T(8,128)(2,1)} %param.25) | copy-start | bytes 245764
  24.1 0.9 %copy-start.3 = (bf16[80,512]{1,0:T(8,128)(2,1)S(1)}, bf16[80,512]{1,0:T(8,128)(2,1)}, u32[]{:S(2)}) copy-start(bf16[80,512]{1,0:T(8,128)(2,1)} %refs_2_.4) | copy-start | bytes 245764
  33.1 11.4 %all-to-all-start.1 = ((bf16[16,32,80]{2,1,0:T(8,128)(2,1)}), bf16[16,32,80]{2,1,0:T(8,128)(2,1)S(1)}, u32[]{:S(2)}, u32[]{:S(2)}) async-start(bf16[16,32,80]{2,1,0:T(8,128)(2,1)} %bitcast.4), calls=%async_computation.1 | async-start | bytes 262144 | tf_op jit(solution)/shard_map/all_to_all | solution.py:41
  44.8 23.0 %copy-start.2 = (f32[80,256]{1,0:T(8,128)}, f32[80,256]{1,0:T(8,128)S(1)}, u32[]{:S(2)}) copy-start(f32[80,256]{1,0:T(8,128)S(1)} %fusion.4.refs_0_) | copy-start | bytes 245764
  48.1 15.4 %all-to-all-start.2 = ((bf16[16,80,128]{2,1,0:T(8,128)(2,1)}), bf16[16,80,128]{2,1,0:T(8,128)(2,1)S(1)}, u32[]{:S(2)}, u32[]{:S(2)}) async-start(bf16[16,80,128]{2,1,0:T(8,128)(2,1)} %loss.1), calls=%async_computation.2 | async-start | bytes 655360 | tf_op jit(solution)/shard_map/all_to_all | solution.py:407
  67.8 4.3 %copy-start.10 = (f32[256,512]{1,0:T(8,128)S(1)}, f32[256,512]{1,0:T(8,128)}, u32[]{:S(2)}) copy-start(f32[256,512]{1,0:T(8,128)} %get-tuple-element.29) | copy-start | bytes 1572868
  67.8 6.6 %collective-permute-start = (bf16[336,256]{1,0:T(8,128)(2,1)S(1)}, bf16[336,256]{1,0:T(8,128)(2,1)S(1)}, u32[]{:S(2)}, u32[]{:S(2)}) collective-permute-start(bf16[336,256]{1,0:T(8,128)(2,1)S(1)} %get-tuple-element.31), channel_id=1, source_target_pairs={{0,2},{2,0},{4,6},{6,4},{8,10},{10,8},{12,14},{14,12},{16,18},{18,... | collective-permute-start | bytes 516104 | tf_op jit(solution)/shard_map/ppermute | solution.py:528
  68.4 8.5 %collective-permute-start.1 = (bf16[336,256]{1,0:T(8,128)(2,1)S(1)}, bf16[336,256]{1,0:T(8,128)(2,1)S(1)}, u32[]{:S(2)}, u32[]{:S(2)}) collective-permute-start(bf16[336,256]{1,0:T(8,128)(2,1)S(1)} %get-tuple-element.32), channel_id=1, source_target_pairs={{0,4},{2,6},{4,0},{6,2},{8,12},{10,14},{12,8},{14,10},{16,20},{18,... | collective-permute-start | bytes 516104 | tf_op jit(solution)/shard_map/ppermute | solution.py:528
  69.2 7.7 %collective-permute-start.2 = (bf16[336,256]{1,0:T(8,128)(2,1)S(1)}, bf16[336,256]{1,0:T(8,128)(2,1)S(1)}, u32[]{:S(2)}, u32[]{:S(2)}) collective-permute-start(bf16[336,256]{1,0:T(8,128)(2,1)S(1)} %get-tuple-element.33), channel_id=1, source_target_pairs={{0,6},{2,4},{4,2},{6,0},{8,14},{10,12},{12,10},{14,8},{16,22},{18,... | collective-permute-start | bytes 516104 | tf_op jit(solution)/shard_map/ppermute | solution.py:528
  72.1 1.0 %copy-start = (bf16[512,512]{1,0:T(8,128)(2,1)S(1)}, bf16[512,512]{1,0:T(8,128)(2,1)}, u32[]{:S(2)}) copy-start(bf16[512,512]{1,0:T(8,128)(2,1)} %refs_2_.5) | copy-start | bytes 1572868
  72.1 1.4 %copy-start.6 = (f32[512]{0:T(512)S(1)}, f32[512]{0:T(512)}, u32[]{:S(2)}) copy-start(f32[512]{0:T(512)} %param.22) | copy-start | bytes 6148
  72.1 1.4 %copy-start.8 = (f32[256,512]{1,0:T(8,128)S(1)}, f32[256,512]{1,0:T(8,128)}, u32[]{:S(2)}) copy-start(f32[256,512]{1,0:T(8,128)} %get-tuple-element.28) | copy-start | bytes 1572868
  77.0 6.5 %collective-permute-start.5 = (bf16[336,256]{1,0:T(8,128)(2,1)S(1)}, bf16[336,256]{1,0:T(8,128)(2,1)S(1)}, u32[]{:S(2)}, u32[]{:S(2)}) collective-permute-start(bf16[336,256]{1,0:T(8,128)(2,1)S(1)} %add_convert_fusion.refs_4_), channel_id=1, source_target_pairs={{0,6},{2,4},{4,2},{6,0},{8,14},{10,12},{12,10},{14,8},{16,22},{18,... | collective-permute-start | bytes 516104 | tf_op jit(solution)/shard_map/ppermute | solution.py:530
  78.7 6.6 %collective-permute-start.4 = (bf16[336,256]{1,0:T(8,128)(2,1)S(1)}, bf16[336,256]{1,0:T(8,128)(2,1)S(1)}, u32[]{:S(2)}, u32[]{:S(2)}) collective-permute-start(bf16[336,256]{1,0:T(8,128)(2,1)S(1)} %add_convert_fusion.refs_4_), channel_id=1, source_target_pairs={{0,4},{2,6},{4,0},{6,2},{8,12},{10,14},{12,8},{14,10},{16,20},{18,... | collective-permute-start | bytes 516104 | tf_op jit(solution)/shard_map/ppermute | solution.py:530
  79.3 5.9 %collective-permute-start.3 = (bf16[336,256]{1,0:T(8,128)(2,1)S(1)}, bf16[336,256]{1,0:T(8,128)(2,1)S(1)}, u32[]{:S(2)}, u32[]{:S(2)}) collective-permute-start(bf16[336,256]{1,0:T(8,128)(2,1)S(1)} %add_convert_fusion.refs_4_), channel_id=1, source_target_pairs={{0,2},{2,0},{4,6},{6,4},{8,10},{10,8},{12,14},{14,12},{16,18},{18,... | collective-permute-start | bytes 516104 | tf_op jit(solution)/shard_map/ppermute | solution.py:530

commit v4 on v3

--- a/solution.py
+++ b/solution.py
@@ -7,6 +7,7 @@
 from jax.experimental import pallas as pl
 from jax.experimental.pallas import tpu as pltpu
 from jax.sharding import PartitionSpec as P
+
 
 MESH_DEV = 256
 
@@ -65,15 +66,6 @@
 
 def one_hot(a, b):
     return jnp.where(a == b, 1.0, 0.0).astype(bf16)
-
-
-def sigmoid(v):
-    return 0.5 + 0.5 * jnp.tanh(0.5 * v)
-
-
-def table_rows(all_ref, bands, group, xy, s, table_at):
-    mate = s * (bands // group) + xy
-    return all_ref[mate, table_at : table_at + TABLE_ROWS, :].astype(f32)
 
 
 def lane_blocks(table, group, rows, row_of):
@@ -101,32 +93,32 @@
     ]
 
 
-def encode_kernel(group, ready, field_ref, noise_ref, send_ref, recv_ref, mesh_ref, out_ref, block_ref, sems):
-    channels, grid_rows = field_ref.shape
+def encode_kernel(
+    group, ready, field_ref, noise_ref, send_ref, recv_ref, mesh_ref, out_ref, table_ref, block_ref, sems
+):
+    grid_rows = field_ref.shape[1]
+    bands, _ = send_ref.shape[1:]
+    rows = bands // group
     ready(0, 1, 2, 3, 4)
     inputs = (field_ref[...] + noise_ref[0].astype(f32)).astype(bf16) * 0.5
-    order, crew = column_order(send_ref, group)
+
+    def in_rows(ref, first):
+        table = ref[0].astype(f32).astype(bf16)
+        return lane_blocks(
+            table,
+            group,
+            TABLE_ROWS,
+            lambda r, j: jnp.where((r >= first) & (r < first + rows), (r - first) * group + j, -1),
+        )
+
+    order = in_rows(send_ref, 0)
+    table_ref[...] = in_rows(recv_ref, 0) + in_rows(mesh_ref, rows)
     subs = lax.broadcasted_iota(jnp.int32, (grid_rows, LANES), 0).astype(f32)
-    bands = recv_ref.shape[1]
-    rows = bands // group
-    recv = recv_ref[0].astype(f32).astype(bf16)
-    mesh = mesh_ref[0].astype(f32).astype(bf16)
-    table = lane_blocks(recv, group, TABLE_ROWS, lambda r, j: jnp.where(r < rows, r * group + j, -1))
-    table = table + lane_blocks(
-        mesh,
-        group,
-        TABLE_ROWS,
-        lambda r, j: jnp.where((r >= rows) & (r < 2 * rows), (r - rows) * group + j, -1),
-    )
-    for c in range(crew):
-        pick = one_hot(subs, order[c : c + 1, :])
-        block_ref[c, 0:channels, :] = mm(inputs, pick, 1, 0).astype(bf16)
-        block_ref[c, channels:, :] = table.astype(bf16)
-    copies = send_copies(group, crew, block_ref, out_ref, sems)
-    for copy in copies:
-        copy.start()
-    for copy in copies:
-        copy.wait()
+    pick = jnp.concatenate([one_hot(subs, order[r : r + 1, :]) for r in range(rows)], axis=1)
+    block_ref[...] = mm(inputs, pick, 1, 0).T.astype(bf16).reshape(block_ref.shape)
+    copy = pltpu.make_async_copy(block_ref, out_ref, sems.at[0])
+    copy.start()
+    copy.wait()
 
 
 def loss_kernel(
@@ -149,97 +141,97 @@
         copy.wait()
 
 
-def forward_kernel(
-    group,
+def node_forward(cells, channel_dim, table, scale_ref, expand_ref, contract_ref, lift_ref, ready):
+    node_rows = MESH_DEV
+    slots = cells.shape[1 - channel_dim]
+    subs = lax.broadcasted_iota(jnp.int32, (node_rows, LANES), 0).astype(f32)
+    latent = mm(cells, lift_ref[...], channel_dim, 0)
+    latent = (latent + latent * jnp.tanh(latent)).astype(bf16)
+    parts = slots // LANES
+    landing = jnp.concatenate([one_hot(subs, table[j : j + 1, :]) for j in range(parts)], axis=1)
+    count = mm(landing, jnp.ones((slots, LANES), bf16), 1, 0)[:, 0:1]
+    state = mm(landing, latent, 1, 0) * (1.0 / jnp.maximum(count, 1.0))
+    recip = lax.rsqrt(jnp.mean(state * state, axis=1, keepdims=True) + norm_eps)
+    ready()
+    normed = (state * recip * scale_ref[...]).astype(bf16)
+    pre = mm(normed, expand_ref[...], 1, 0)
+    bent = jnp.tanh(pre)
+    above = 1.0 + bent
+    bend = (above * (1.0 + pre * (1.0 - bent))).astype(bf16)
+    hidden = (pre * above).astype(bf16)
+    following = (state + mm(hidden, contract_ref[...], 1, 0)).astype(bf16)
+    return state, pre, normed, bend, following, hidden
+
+
+def own_kernel(
     channels,
     ready,
-    me_ref,
-    all_ref,
+    cells_ref,
+    table_ref,
     lift_ref,
     scale_ref,
     expand_ref,
     contract_ref,
     readout_ref,
-    normed_ref,
-    slope_ref,
-    state_ref,
-    own_ref,
-    own_pre_ref,
     chosen_ref,
-    table_ref,
-    slot_ref,
-    normed_buf,
-    slope_buf,
-    state_buf,
-    own_buf,
-    own_pre_buf,
-    sems,
-    own_sems,
+    *rest,
 ):
-    bands = all_ref.shape[0]
-    node_rows, width = normed_ref.shape[1], normed_ref.shape[2]
-    slots = slot_ref.shape[1]
-    cap = slots // bands
-    z, xy = me_ref[0], me_ref[1]
-    subs = lax.broadcasted_iota(jnp.int32, (node_rows, LANES), 0).astype(f32)
-
-    def embed(b, carry):
-        latent = mm(all_ref[b, 0:channels, :], lift_ref[...], 0, 0)
-        latent = (latent + latent * jnp.tanh(latent)).astype(bf16)
-        slot_ref[:, pl.ds(pl.multiple_of(b * cap, cap), cap), :] = latent.reshape(group, cap, width)
-        return carry
-
-    lax.fori_loop(0, bands, embed, 0, unroll=4)
-    ready(2, 3, 4, 5)
-    kept = [(normed_buf, normed_ref), (slope_buf, slope_ref), (state_buf, state_ref)]
-    own_copies = [
-        pltpu.make_async_copy(own_buf, own_ref, own_sems.at[0]),
-        pltpu.make_async_copy(own_pre_buf, own_pre_ref, own_sems.at[1]),
+    count = (len(rest) - 1) // 2
+    out_refs, bufs, sems = rest[:count], rest[count:-1], rest[-1]
+    copies = [pltpu.make_async_copy(a, b, sems.at[i]) for i, (a, b) in enumerate(zip(bufs, out_refs))]
+    parcel_buf, state_buf, pre_buf, normed_buf, bend_buf, both_buf = bufs
+    slots = cells_ref.shape[0]
+    width = both_buf.shape[1] // 2
+    parts = slots // LANES
+    table = table_ref[...]
+    parcel_buf[0:channels, :] = cells_ref[...].astype(f32).T.astype(bf16)
+    parcel_buf[channels:, :] = jnp.concatenate([table] * parts, axis=1).astype(bf16)
+    copies[0].start()
+    state, pre, normed, bend, following, hidden = node_forward(
+        cells_ref[...], 1, table, scale_ref, expand_ref, contract_ref, lift_ref, lambda: ready(3, 4, 5, 6)
+    )
+    both_buf[:, 0:width] = following
+    projected = mm(following, readout_ref[...], 1, 1).astype(bf16)
+    subs = lax.broadcasted_iota(jnp.int32, (state.shape[0], LANES), 0).astype(f32)
+    for j in range(parts):
+        pick = one_hot(subs, table[parts + j : parts + j + 1, :])
+        chosen_ref[j * LANES : (j + 1) * LANES, :] = mm(pick, projected, 0, 0).astype(bf16)
+    state_buf[...] = state
+    pre_buf[...] = pre
+    normed_buf[...] = normed
+    bend_buf[...] = bend
+    both_buf[:, width:] = hidden
+    for copy in copies[1:]:
+        copy.start()
+    for copy in copies:
+        copy.wait()
+
+
+def mates_kernel(channels, ready, lift_ref, scale_ref, expand_ref, contract_ref, *rest):
+    mates = len(rest) - 8
+    parcel_refs = rest[:mates]
+    normed_out, bend_out, both_out, table_ref, normed_buf, bend_buf, both_buf, sems = rest[mates:]
+    width = both_buf.shape[2] // 2
+    ready(*range(4 + mates))
+    pairs = [(normed_buf, normed_out), (bend_buf, bend_out), (both_buf, both_out)]
+    copies = [
+        [pltpu.make_async_copy(a.at[m], b.at[m], sems.at[i, m]) for i, (a, b) in enumerate(pairs)]
+        for m in range(mates)
     ]
-
-    def copies(s):
-        return [pltpu.make_async_copy(a.at[s], b.at[s], sems.at[i, s]) for i, (a, b) in enumerate(kept)]
-
-    def nodes(i, carry):
-        s = lax.rem(z + i, group)
-        table = table_rows(all_ref, bands, group, xy, s, channels)
-        table_ref[s] = table
-        parts = slots // LANES
-        landing = jnp.concatenate([one_hot(subs, table[j : j + 1, :]) for j in range(parts)], axis=1)
-        count = mm(landing, jnp.ones((slots, LANES), bf16), 1, 0)[:, 0:1]
-        state = mm(landing, slot_ref[s], 1, 0) * (1.0 / jnp.maximum(count, 1.0))
-        recip = lax.rsqrt(jnp.mean(state * state, axis=1, keepdims=True) + norm_eps)
-        normed = (state * recip * scale_ref[...]).astype(bf16)
-        normed_buf[s] = normed
-        pre = mm(normed, expand_ref[...], 1, 0)
-        bent = jnp.tanh(pre)
-        above = 1.0 + bent
-        slope_buf[s] = (above * (1.0 + pre * (1.0 - bent))).astype(bf16)
-        hidden = (pre * above).astype(bf16)
-        following = (state + mm(hidden, contract_ref[...], 1, 0)).astype(bf16)
-        state_buf[s, :, 0:width] = following
-        state_buf[s, :, width:] = hidden
-        for copy in copies(s):
+    for m, parcel_ref in enumerate(parcel_refs):
+        table = parcel_ref[channels:, 0:LANES].astype(f32)
+        table_ref[m] = table
+        _, _, normed, bend, following, hidden = node_forward(
+            parcel_ref[0:channels, :], 0, table, scale_ref, expand_ref, contract_ref, lift_ref, lambda: None
+        )
+        normed_buf[m] = normed
+        bend_buf[m] = bend
+        both_buf[m, :, 0:width] = following
+        both_buf[m, :, width:] = hidden
+        for copy in copies[m]:
             copy.start()
-
-        @pl.when(i == 0)
-        def _():
-            own_buf[...] = state
-            own_pre_buf[...] = pre
-            for copy in own_copies:
-                copy.start()
-            projected = mm(following, readout_ref[...], 1, 1).astype(bf16)
-            for j in range(parts):
-                pick = one_hot(subs, table[parts + j : parts + j + 1, :])
-                chosen_ref[j * LANES : (j + 1) * LANES, :] = mm(pick, projected, 0, 0).astype(bf16)
-
-        return carry
-
-    lax.fori_loop(0, group, nodes, 0)
-    for copy in own_copies:
-        copy.wait()
-    for s in range(group):
-        for copy in copies(s):
+    for line in copies:
+        for copy in line:
             copy.wait()
 
 
@@ -249,27 +241,38 @@
     me_ref,
     grad_ref,
     table_ref,
+    mate_table_ref,
     chain_ref,
     normed_ref,
-    slope_ref,
-    state_ref,
+    bend_ref,
+    both_ref,
+    mate_normed_ref,
+    mate_bend_ref,
+    mate_both_ref,
     own_ref,
     *rest,
 ):
-    piece_refs, (value_ref, node_ref, up_ref, small_ref, normed_buf, slope_buf, state_buf, sems) = rest[:-8], rest[-8:]
+    piece_refs, (value_ref, node_ref, up_ref, small_ref, normed_buf, bend_buf, both_buf, sems) = rest[:-8], rest[-8:]
     bands = grad_ref.shape[0]
     slots = value_ref.shape[1]
-    node_rows, width = normed_ref.shape[1], normed_ref.shape[2]
+    node_rows = normed_ref.shape[0]
     cap = slots // bands
     z, xy = me_ref[0], me_ref[1]
     subs = lax.broadcasted_iota(jnp.int32, (node_rows, LANES), 0).astype(f32)
-    kept = [(slope_ref, slope_buf), (normed_ref, normed_buf), (state_ref, state_buf)]
-
-    def copies(s):
-        return [pltpu.make_async_copy(a.at[s], b.at[s], sems.at[i, s]) for i, (a, b) in enumerate(kept)]
-
-    for s in range(group):
-        for copy in copies(s):
+    kept = [
+        (bend_ref, mate_bend_ref, bend_buf),
+        (normed_ref, mate_normed_ref, normed_buf),
+        (both_ref, mate_both_ref, both_buf),
+    ]
+    copies = [
+        [
+            pltpu.make_async_copy(mate.at[s - 1] if s else own, buf.at[s], sems.at[i, s])
+            for i, (own, mate, buf) in enumerate(kept)
+        ]
+        for s in range(group)
+    ]
+    for line in copies:
+        for copy in line:
             copy.start()
 
     def turn(b, carry):
@@ -278,34 +281,26 @@
         return carry
 
     lax.fori_loop(0, bands, turn, 0, unroll=4)
-
-    def nodes(s, carry):
-        table = table_ref[s]
-        parts = slots // LANES
+    parts = slots // LANES
+    for s in range(group):
+        table = mate_table_ref[s - 1] if s else table_ref[...]
         pick = jnp.concatenate(
             [one_hot(subs, table[parts + j : parts + j + 1, :]) for j in range(parts)], axis=1
         )
-        node_grad = mm(pick, value_ref[s], 1, 0)
-
-        @pl.when(s == z)
-        def _():
+        node_grad = mm(pick, value_ref[z ^ s], 1, 0)
+        if s == 0:
             own_ref[...] = node_grad
-
         node_b = node_grad.astype(bf16)
-        at = pl.ds(pl.multiple_of(s * node_rows, node_rows), node_rows)
-        node_ref[at, :] = node_b
-        copies(s)[0].wait()
+        node_ref[s * node_rows : (s + 1) * node_rows, :] = node_b
+        copies[s][0].wait()
         pre = mm(node_b, chain_ref[...], 1, 0)
-        slope_buf[s] = (pre * slope_buf[s].astype(f32)).astype(bf16)
-        return carry
-
-    lax.fori_loop(0, group, nodes, 0)
-    for s in range(group):
-        for copy in copies(s)[1:]:
+        bend_buf[s] = (pre * bend_buf[s].astype(f32)).astype(bf16)
+    for line in copies:
+        for copy in line[1:]:
             copy.wait()
     everything = (group * node_rows, -1)
-    up_ref[...] = 2.0 * mm(normed_buf[...].reshape(everything), slope_buf[...].reshape(everything), 0, 0)
-    small_ref[...] = mm(node_ref[...], state_buf[...].reshape(everything), 0, 0)
+    up_ref[...] = 2.0 * mm(normed_buf[...].reshape(everything), bend_buf[...].reshape(everything), 0, 0)
+    small_ref[...] = mm(node_ref[...], both_buf[...].reshape(everything), 0, 0)
     count = len(piece_refs)
     rows = up_ref.shape[0] // count
     half = up_ref.shape[1] // 2
@@ -318,7 +313,7 @@
         piece_ref[2 * rows :, :] = small_ref[:, pl.ds(pl.multiple_of(to * lanes, lanes), lanes)].astype(bf16)
 
 
-def finish_kernel(factor, channels, me_ref, scale_ref, expand_ref, readout_ref, *rest):
+def finish_kernel(factor, me_ref, scale_ref, expand_ref, readout_ref, *rest):
     count = len(rest) - 8
     piece_refs = rest[:count]
     up_out, down_out, dec_ref, gain_ref, small_ref, up_ref, down_ref, sems = rest[count:]
@@ -353,7 +348,7 @@
         copy.wait()
 
 
-def vmem_call(kernel, outs, name, scratch=(), sems=(), budget=24, left_in=(), left_out=(), fetched=()):
+def vmem_call(kernel, outs, scratch=(), sems=(), budget=24, left_in=(), left_out=(), fetched=()):
     vmem = pl.BlockSpec(memory_space=pltpu.VMEM)
     smem = pl.BlockSpec(memory_space=pltpu.SMEM)
     left = pl.BlockSpec(memory_space=pltpu.HBM)
@@ -394,7 +389,6 @@
             + [pltpu.VMEM(operands[i].shape, operands[i].dtype) for i in fetched]
             + ([pltpu.SemaphoreType.DMA((len(fetched),))] if fetched else []),
             compiler_params=pltpu.CompilerParams(vmem_limit_bytes=budget * 2**20),
-            name=name,
         )(
             *([] if scalars is None else [scalars]),
             *[pltpu.with_memory_space_constraint(x, pltpu.HBM) if i in outside else x for i, x in enumerate(operands)],
@@ -457,40 +451,49 @@
     band = lax.axis_index("band").astype(jnp.int32)
     me = jnp.stack([band // crew, band % crew])
     cell_ids = jnp.arange(grid_rows, dtype=jnp.int32)
-    block = (crew, channels + TABLE_ROWS, LANES)
-    outgoing = vmem_call(
+    cap = enc_send.shape[2]
+    block = ((bands, cap, channels), bf16)
+    outgoing, table = vmem_call(
         functools.partial(encode_kernel, group),
-        [((bands, channels + TABLE_ROWS, LANES), bf16)],
-        "encode",
-        scratch=[(block, bf16)],
-        sems=[(group,)],
+        [block, ((TABLE_ROWS, LANES), f32)],
+        scratch=[block],
+        sems=[(1,)],
         left_out=(0,),
         fetched=range(5),
-    )(None, scaled_atmosphere_field, perturbation, enc_send, enc_recv, dec_send)[0]
-    arrived = all_to_all(outgoing)
-    kept = [
-        ((group, node_rows, width), bf16),
-        ((group, node_rows, hid), bf16),
-        ((group, node_rows, width + hid), bf16),
-    ]
-    own = [((node_rows, width), f32), ((node_rows, hid), f32)]
-    normed, slopes, states, mesh_state, half_pre, chosen, column_tables = vmem_call(
-        functools.partial(forward_kernel, group, channels),
-        kept + own + [((slots, channels), bf16), ((group, TABLE_ROWS, LANES), f32)],
-        "forward",
-        scratch=[((group, slots, width), bf16)] + kept + own,
-        sems=[(3, group), (2,)],
-        left_out=range(5),
-        fetched=(2, 3, 4, 5),
+    )(None, scaled_atmosphere_field, perturbation, enc_send, enc_recv, dec_send)
+    arrived = all_to_all(outgoing).reshape(slots, channels)
+    half_scale = 0.5 * mixing_rescale_factor[None, :]
+    kept = [((node_rows, width), bf16), ((node_rows, hid), bf16), ((node_rows, width + hid), bf16)]
+    sent = [((channels + TABLE_ROWS, slots), bf16), ((node_rows, width), f32), ((node_rows, hid), f32)] + kept
+    chosen, parcel, mesh_state, half_pre, normed, bend, both = vmem_call(
+        functools.partial(own_kernel, channels),
+        [((slots, channels), bf16)] + sent,
+        scratch=sent,
+        sems=[(len(sent),)],
+        left_out=range(1, 1 + len(sent)),
+        fetched=(3, 4, 5, 6),
     )(
-        me,
+        None,
         arrived,
+        table,
         lattice_lift_matrix,
-        0.5 * mixing_rescale_factor[None, :],
+        half_scale,
         expand_matrix,
         contract_matrix,
         readout_matrix.T,
     )
+    parcels = [
+        lax.ppermute(parcel, "band", [(i, i ^ (m * crew)) for i in range(bands)]) for m in range(1, group)
+    ]
+    mate_kept = [((group - 1,) + shape, dtype) for shape, dtype in kept]
+    mate_normed, mate_bend, mate_both, mate_table = vmem_call(
+        functools.partial(mates_kernel, channels),
+        mate_kept + [((group - 1, TABLE_ROWS, LANES), f32)],
+        scratch=mate_kept,
+        sems=[(3, group - 1)],
+        left_out=(0, 1, 2),
+        fetched=range(4 + len(parcels)),
+    )(None, lattice_lift_matrix, half_scale, expand_matrix, contract_matrix, *parcels)
     chain = (0.5 * mm(readout_matrix, contract_matrix, 0, 1)).astype(bf16)
     slot_values = exchange(chosen, bands)
     fill_map = (cell_ids[:, None] == dec_recv[0].reshape(-1)[None, :]).astype(bf16)
@@ -501,7 +504,6 @@
     outgoing = vmem_call(
         functools.partial(loss_kernel, group),
         [((bands, channels, LANES), bf16)],
-        "loss",
         scratch=[((crew, channels, LANES), bf16)],
         sems=[(group,)],
         left_out=(0,),
@@ -511,19 +513,16 @@
     node_grad, *pieces = vmem_call(
         functools.partial(backward_kernel, group, channels),
         [((node_rows, channels), f32)] + [((piece_rows, hid // 2), bf16)] * crew,
-        "backward",
         scratch=[
             ((group, slots, channels), bf16),
             ((group * node_rows, channels), bf16),
             ((width, hid), f32),
             ((channels, width + hid), f32),
-            kept[0],
-            kept[1],
-            kept[2],
-        ],
+        ]
+        + [((group,) + shape, dtype) for shape, dtype in kept],
         sems=[(3, group)],
-        left_in=(3, 4, 5),
-    )(me, returned, column_tables, chain, normed, slopes, states)
+        left_in=range(4, 10),
+    )(me, returned, table, mate_table, chain, normed, bend, both, mate_normed, mate_bend, mate_both)
     swaps = [[(i, i ^ p) for i in range(bands)] for p in range(1, crew)]
     others = [lax.ppermute(piece, "band", swap) for piece, swap in zip(pieces[1:], swaps)]
     total = sum(x.astype(f32) for x in [pieces[0]] + others).astype(bf16)
@@ -539,9 +538,8 @@
     )
     factor = 1.0 / math.sqrt(bands * node_rows)
     grad_up, grad_down, grad_dec, grad_gain = vmem_call(
-        functools.partial(finish_kernel, factor, channels),
+        functools.partial(finish_kernel, factor),
         [((width, hid), f32), ((hid, width), f32), ((channels, width), f32), ((1, width), f32)],
-        "finish",
         scratch=[((channels, width + hid), f32), ((width, hid), f32), ((hid, width), f32)],
         sems=[(2, crew)],
         left_out=(0, 1),

time: 88.7 us -> 95.5 us (1.077)
  starting transfers between devices: 22.7 us -> 27.1 us
  local copies, waits for them, and re-layouts: 2.31 us -> 4.79 us
    all_to_all x2, waiting for transfers between devices: 19.8 us -> 3.56 us  [all_to_all(): return lax.all_to_all(x, 'band', split_axis=0, concat_axis=0, tiled=True)]
    ppermute x0 -> x3, waiting for transfers between devices: none -> 14.3 us  [column_body(): lax.ppermute(parcel, 'band', [(i, i ^ m * crew) for i in range(bands)])]
    ppermute x0 -> x3, starting transfers between devices: none -> 4.45 us  [column_body(): lax.ppermute(parcel, 'band', [(i, i ^ m * crew) for i in range(bands)])]
    unnamed x22 -> x32, local copies, waits for them, and re-layouts: 1.5 us -> 4.01 us
    ppermute x3, waiting for transfers between devices: 3.77 us -> 4.81 us  [column_body(): totals = [total] + [lax.ppermute(total, 'band', swap) for swap in swaps]]
    pallas_call x5 -> x6, Pallas kernels: 18.9 us -> 19.4 us  [call(): pl.pallas_call(run, out_shape=[(pltpu.HBM if i in left_out else jax.Shape...]
  transfers between devices with their start and end apart: 9 -> 12, of which waited for: 7 -> 7; matrix products, arithmetic and copies ran while one was open for 6% -> 6% of each run, Pallas kernels for 0% -> 6%
where the time goes in v4:
time: 95.5 us; the launch traced here: 94.8 us
  waiting for transfers between devices  33.6 us (35%)
  starting transfers between devices  27.1 us (28%)
  Pallas kernels  19.4 us (20%)
  local copies, waits for them, and re-layouts  4.79 us (5%)
  blocking collectives  3.99 us (4%)
  other arithmetic  2.48 us (3%)
  matrix products  2.45 us (3%)
    pallas_call x6, Pallas kernels, call(): pl.pallas_call(run, out_shape=[(pltpu.HBM if i in left_out else jax.Shape...  19.4 us
    ppermute x3, waiting for transfers between devices, column_body(): lax.ppermute(parcel, 'band', [(i, i ^ m * crew) for i in range(bands)])  14.3 us
    all_to_all x2, starting transfers between devices, all_to_all(): return lax.all_to_all(x, 'band', split_axis=0, concat_axis=0, tiled=True)  11.9 us
    all_to_all x1, waiting for transfers between devices, exchange(): lax.all_to_all(x.reshape(band_count, rows // band_count, width), 'band',...  7.75 us
    ppermute x3, waiting for transfers between devices, column_body(): totals = [total] + [lax.ppermute(total, 'band', swap) for swap in swaps]  4.81 us
    ppermute x3, starting transfers between devices, column_body(): lax.ppermute(parcel, 'band', [(i, i ^ m * crew) for i in range(bands)])  4.45 us
    unnamed x32, local copies, waits for them, and re-layouts  4.01 us
    all_to_all x1, starting transfers between devices, exchange(): lax.all_to_all(x.reshape(band_count, rows // band_count, width), 'band',...  3.66 us
  transfers between devices with their start and end apart: 12, of which 7 were waited for; matrix products, arithmetic and copies ran while one was open for 6% of the time, Pallas kernels for 6%

profile of v4, /device:TPU:0, one launch (start us, length us, event | category | flops | bytes accessed | tf_op | source)
XLA Modules:
  0.0 94.8 jit_solution(13766258649585037628)
XLA Ops:
  0.7 2.3 %shard_map.172 = (bf16[16,32,80]{2,1,0:T(8,128)(2,1)}, f32[16,128]{1,0:T(8,128)S(1)}) custom-call(f32[80,256]{1,0:T(8,128)} %refs_0_.2, bf16[1,80,256]{2,1,0:T(8,128)(2,1)} %refs_1_.1, s32[1,16,32]{2,1,0:T(8,128)} %refs_2_.4, s32[1,16,32]{2,1,0:T(8,128)} %refs_3_.3, s32[1,16,32]{2,1,0:T(8,128)} %refs_4_.2), custom_call_target="tpu_custom_call" | custom-call | tf_op jit(solution)/shard_map/pallas_call | solution.py:382
  2.9 8.4 %all-to-all-start = ((bf16[16,32,80]{2,1,0:T(8,128)(2,1)}), bf16[16,32,80]{2,1,0:T(8,128)(2,1)S(1)}, u32[]{:S(2)}, u32[]{:S(2)}) async-start(bf16[16,32,80]{2,1,0:T(8,128)(2,1)} %get-tuple-element.28), calls=%async_computation | async-start | bytes 262144 | tf_op jit(solution)/shard_map/all_to_all | solution.py:401
  11.3 1.3 %broadcast_multiply_fusion = f32[512]{0:T(512)} fusion(f32[512]{0:T(512)} %param.22), kind=kLoop, calls=%fused_computation.34 | loop fusion | flops 512 | bytes 4096 | tf_op jit(solution)/shard_map/mul | solution.py:465
  13.3 2.1 %all_gather.8.refs_2_ = bf16[2,80,256]{2,1,0:T(8,128)(2,1)S(1)} all-gather(bf16[1,80,256]{2,1,0:T(8,128)(2,1)} %param.15), channel_id=1, replica_groups=mesh['band'=16,'member'=2] {'member'}, dimensions={0}, use_global_device_ids=true | all-gather | bytes 122880 | tf_op jit(solution)/shard_map/all_gather | solution.py:503
  15.5 3.6 %all-to-all-done = bf16[16,32,80]{2,1,0:T(8,128)(2,1)S(1)} async-done(((bf16[16,32,80]{2,1,0:T(8,128)(2,1)}), bf16[16,32,80]{2,1,0:T(8,128)(2,1)S(1)}, u32[]{:S(2)}, u32[]{:S(2)}) %all-to-all-start) | async-done | bytes 81952 | tf_op jit(solution)/shard_map/all_to_all | solution.py:401
  20.0 3.5 %shard_map.173 = (bf16[512,80]{1,0:T(8,128)(2,1)}, bf16[96,512]{1,0:T(8,128)(2,1)}, f32[256,512]{1,0:T(8,128)}, f32[256,512]{1,0:T(8,128)}, bf16[256,512]{1,0:T(...) custom-call(bf16[512,80]{1,0:T(8,128)(2,1)S(1)} %bitcast.30, ...), custom_call_target="tpu_custom_call" | custom-call | tf_op jit(solution)/shard_map/pallas_call | solution.py:382
  23.6 3.7 %all-to-all-start.1 = ((bf16[16,32,80]{2,1,0:T(8,128)(2,1)}), bf16[16,32,80]{2,1,0:T(8,128)(2,1)S(1)}, u32[]{:S(2)}, u32[]{:S(2)}) async-start(bf16[16,32,80]{2,1,0:T(8,128)(2,1)} %bitcast.3), calls=%async_computation.1 | async-start | bytes 262144 | tf_op jit(solution)/shard_map/all_to_all | solution.py:42
  27.2 7.8 %all-to-all-done.1 = bf16[16,32,80]{2,1,0:T(8,128)(2,1)S(1)} async-done(((bf16[16,32,80]{2,1,0:T(8,128)(2,1)}), bf16[16,32,80]{2,1,0:T(8,128)(2,1)S(1)}, u32[]{:S(2)}, u32[]{:S(2)}) %all-to-all-start.1) | async-done | bytes 81952 | tf_op jit(solution)/shard_map/all_to_all | solution.py:42
  35.2 1.9 %all-gather = f32[160,256]{1,0:T(8,128)S(1)} all-gather(f32[80,256]{1,0:T(8,128)S(1)} %fusion.4.refs_0_), channel_id=2, replica_groups=mesh['band'=16,'member'=2] {'member'}, dimensions={0}, use_global_device_ids=true | all-gather | bytes 245760 | tf_op jit(solution)/shard_map/all_gather | solution.py:502
  37.2 1.3 %shard_map.174 = bf16[16,80,128]{2,1,0:T(8,128)(2,1)} custom-call(f32[80,256]{1,0:T(8,128)S(1)} %fusion.4.refs_0_, f32[2,80,256]{2,1,0:T(8,128)S(1)} %bitcast.29, bf16[2,80,256]{2,1,0:T(8,128)(2,1)S(1)} %all_gather.8.refs_2_, bf16[80,256]{1,0:T(8,128)(2,1)S(1)} %copy-done.4, f32[1,256]{1,0:T(1,128)S(1)} %bitcast.33, s32[1,16,32]{2,1,0:T(8,128)S(1)} %copy-done.5), custom_call_target="tpu_custom_call" | custom-call | tf_op jit(solution)/shard_map/pallas_call | solution.py:382
  38.5 3.6 %all-to-all-start.2 = ((bf16[16,80,128]{2,1,0:T(8,128)(2,1)}), bf16[16,80,128]{2,1,0:T(8,128)(2,1)S(1)}, u32[]{:S(2)}, u32[]{:S(2)}) async-start(bf16[16,80,128]{2,1,0:T(8,128)(2,1)} %shard_map.174), calls=%async_computation.2 | async-start | bytes 655360 | tf_op jit(solution)/shard_map/all_to_all | solution.py:401
  42.4 3.7 %collective-permute-start.2 = (bf16[96,512]{1,0:T(8,128)(2,1)S(1)}, bf16[96,512]{1,0:T(8,128)(2,1)S(1)}, u32[]{:S(2)}, u32[]{:S(2)}) collective-permute-start(bf16[96,512]{1,0:T(8,128)(2,1)S(1)} %copy-done.15), channel_id=1, source_target_pairs={{0,24},{2,26},{4,28},{6,30},{8,16},{10,18},{12,20},{14,22},{16,8},... | collective-permute-start | bytes 294920 | tf_op jit(solution)/shard_map/ppermute | solution.py:486
  46.9 7.9 %collective-permute-done.2.refs_6_ = bf16[96,512]{1,0:T(8,128)(2,1)S(1)} collective-permute-done((bf16[96,512]{1,0:T(8,128)(2,1)S(1)}, bf16[96,512]{1,0:T(8,128)(2,1)S(1)}, u32[]{:S(2)}, u32[]{:S(2)}) %collective-permute-start.2) | collective-permute-done | bytes 98336 | tf_op jit(solution)/shard_map/ppermute | solution.py:486
  54.9 6.3 %collective-permute-done.1.refs_5_ = bf16[96,512]{1,0:T(8,128)(2,1)S(1)} collective-permute-done((bf16[96,512]{1,0:T(8,128)(2,1)S(1)}, bf16[96,512]{1,0:T(8,128)(2,1)S(1)}, u32[]{:S(2)}, u32[]{:S(2)}) %collective-permute-start.1) | collective-permute-done | bytes 98336 | tf_op jit(solution)/shard_map/ppermute | solution.py:486
  62.5 5.5 %shard_map.175 = (bf16[3,256,512]{2,1,0:T(8,128)(2,1)}, bf16[3,256,512]{2,1,0:T(8,128)(2,1)}, bf16[3,256,1024]{2,1,0:T(8,128)(2,1)}, f32[3,16,128]{2,1,0:T(8,128)S(1)}) custom-call(bf16[80,512]{1,0:T(8,128)(2,1)} %refs_0_.3, f32[1,512]{1,0:T(1,128)} %bitcast.36, bf16[512,512]{1,0:T(8,128)(2,1)} %refs_2_.7, bf16[512,512]{1,0:T(8,128)(2,1)} %refs_3_.5, ...), custom_call_target="tpu_custom_call" | custom-call | tf_op jit(solution)/shard_map/pallas_call | solution.py:382
  68.0 3.9 %shard_map.176 = (f32[256,80]{1,0:T(8,128)S(1)}, bf16[336,256]{1,0:T(8,128)(2,1)S(1)}, bf16[336,256]{1,0:T(8,128)(2,1)S(1)}, bf16[336,256]{1,0:T(8,128)(2,1)S(1)}, bf16[336,256]{1,0:T(8,128)(2,1)S(1)}) custom-call(s32[2]{0:T(128)S(1)} %pad_add_fusion.refs_0_, bf16[16,80,128]{2,1,0:T(8,128)(2,1)S(1)} %all-to-all-done.2.refs_1_, ...), custom_call_target="tpu_custom_call" | custom-call | tf_op jit(solution)/shard_map/pallas_call | solution.py:382
  71.9 1.5 %collective-permute-start.3 = (bf16[336,256]{1,0:T(8,128)(2,1)S(1)}, bf16[336,256]{1,0:T(8,128)(2,1)S(1)}, u32[]{:S(2)}, u32[]{:S(2)}) collective-permute-start(bf16[336,256]{1,0:T(8,128)(2,1)S(1)} %get-tuple-element.43), channel_id=1, source_target_pairs={{0,2},{2,0},{4,6},{6,4},{8,10},{10,8},{12,14},{14,12},{16,18},{18,... | collective-permute-start | bytes 516104 | tf_op jit(solution)/shard_map/ppermute | solution.py:527
  73.5 1.5 %collective-permute-start.4 = (bf16[336,256]{1,0:T(8,128)(2,1)S(1)}, bf16[336,256]{1,0:T(8,128)(2,1)S(1)}, u32[]{:S(2)}, u32[]{:S(2)}) collective-permute-start(bf16[336,256]{1,0:T(8,128)(2,1)S(1)} %get-tuple-element.44), channel_id=1, source_target_pairs={{0,4},{2,6},{4,0},{6,2},{8,12},{10,14},{12,8},{14,10},{16,20},{18,... | collective-permute-start | bytes 516104 | tf_op jit(solution)/shard_map/ppermute | solution.py:527
  79.3 3.2 %collective-permute-done.4 = bf16[336,256]{1,0:T(8,128)(2,1)S(1)} collective-permute-done((bf16[336,256]{1,0:T(8,128)(2,1)S(1)}, bf16[336,256]{1,0:T(8,128)(2,1)S(1)}, u32[]{:S(2)}, u32[]{:S(2)}) %collective-permute-start.4) | collective-permute-done | bytes 172064 | tf_op jit(solution)/shard_map/ppermute | solution.py:527
  82.7 1.4 %collective-permute-start.8 = (bf16[336,256]{1,0:T(8,128)(2,1)S(1)}, bf16[336,256]{1,0:T(8,128)(2,1)S(1)}, u32[]{:S(2)}, u32[]{:S(2)}) collective-permute-start(bf16[336,256]{1,0:T(8,128)(2,1)S(1)} %add_convert_fusion.refs_4_), channel_id=1, source_target_pairs={{0,6},{2,4},{4,2},{6,0},{8,14},{10,12},{12,10},{14,8},{16,22},{18,... | collective-permute-start | bytes 516104 | tf_op jit(solution)/shard_map/ppermute | solution.py:529
  84.1 1.2 %collective-permute-start.7 = (bf16[336,256]{1,0:T(8,128)(2,1)S(1)}, bf16[336,256]{1,0:T(8,128)(2,1)S(1)}, u32[]{:S(2)}, u32[]{:S(2)}) collective-permute-start(bf16[336,256]{1,0:T(8,128)(2,1)S(1)} %add_convert_fusion.refs_4_), channel_id=1, source_target_pairs={{0,4},{2,6},{4,0},{6,2},{8,12},{10,14},{12,8},{14,10},{16,20},{18,... | collective-permute-start | bytes 516104 | tf_op jit(solution)/shard_map/ppermute | solution.py:529
  87.1 3.2 %collective-permute-done.8.refs_7_ = bf16[336,256]{1,0:T(8,128)(2,1)S(1)} collective-permute-done((bf16[336,256]{1,0:T(8,128)(2,1)S(1)}, bf16[336,256]{1,0:T(8,128)(2,1)S(1)}, u32[]{:S(2)}, u32[]{:S(2)}) %collective-permute-start.8) | collective-permute-done | bytes 172064 | tf_op jit(solution)/shard_map/ppermute | solution.py:529
  90.4 1.6 %collective-permute-done.7.refs_6_ = bf16[336,256]{1,0:T(8,128)(2,1)S(1)} collective-permute-done((bf16[336,256]{1,0:T(8,128)(2,1)S(1)}, bf16[336,256]{1,0:T(8,128)(2,1)S(1)}, u32[]{:S(2)}, u32[]{:S(2)}) %collective-permute-start.7) | collective-permute-done | bytes 172064 | tf_op jit(solution)/shard_map/ppermute | solution.py:529
  91.9 2.8 %shard_map.177 = (f32[512,512]{1,0:T(8,128)}, f32[512,512]{1,0:T(8,128)}, f32[80,512]{1,0:T(8,128)}, f32[1,512]{1,0:T(1,128)}) custom-call(s32[2]{0:T(128)S(1)} %pad_add_fusion.refs_0_, f32[1,512]{1,0:T(1,128)S(1)} %bitcast.32, bf16[512,512]{1,0:T(8,128)(2,1)S(1)} %copy-done, bf16[80,512]{1,0:T(8,128)(2,1)S(1)} %bitcast.28, ...), custom_call_target="tpu_custom_call" | custom-call | tf_op jit(solution)/shard_map/pallas_call | solution.py:382
  (57 shorter events, 10.7 us)
Async XLA Ops:
  0.6 34.4 %copy-start.13 = (f32[80,256]{1,0:T(8,128)S(1)}, f32[80,256]{1,0:T(8,128)}, u32[]{:S(2)}) copy-start(f32[80,256]{1,0:T(8,128)} %refs_0_.2) | copy-start | bytes 245764
  0.6 36.5 %copy-start.5 = (s32[1,16,32]{2,1,0:T(8,128)S(1)}, s32[1,16,32]{2,1,0:T(8,128)}, u32[]{:S(2)}) copy-start(s32[1,16,32]{2,1,0:T(8,128)} %refs_5_.3) | copy-start | bytes 6148
  0.7 36.5 %copy-start.4 = (bf16[80,256]{1,0:T(8,128)(2,1)S(1)}, bf16[80,256]{1,0:T(8,128)(2,1)}, u32[]{:S(2)}) copy-start(bf16[80,256]{1,0:T(8,128)(2,1)} %refs_3_.4) | copy-start | bytes 122884
  2.9 16.2 %all-to-all-start = ((bf16[16,32,80]{2,1,0:T(8,128)(2,1)}), bf16[16,32,80]{2,1,0:T(8,128)(2,1)S(1)}, u32[]{:S(2)}, u32[]{:S(2)}) async-start(bf16[16,32,80]{2,1,0:T(8,128)(2,1)} %get-tuple-element.28), calls=%async_computation | async-start | bytes 262144 | tf_op jit(solution)/shard_map/all_to_all | solution.py:401
  20.0 22.1 %copy-start.1 = (bf16[512,80]{0,1:T(8,128)(2,1)S(1)}, bf16[512,80]{0,1:T(8,128)(2,1)}, u32[]{:S(2)}) copy-start(bf16[512,80]{0,1:T(8,128)(2,1)} %param.25) | copy-start | bytes 245764
  20.0 22.1 %copy-start.7 = (bf16[512,512]{1,0:T(8,128)(2,1)S(1)}, bf16[512,512]{1,0:T(8,128)(2,1)}, u32[]{:S(2)}) copy-start(bf16[512,512]{1,0:T(8,128)(2,1)} %refs_3_.5) | copy-start | bytes 1572868
  23.5 18.8 %copy-start.15 = (bf16[96,512]{1,0:T(8,128)(2,1)S(1)}, bf16[96,512]{1,0:T(8,128)(2,1)}, u32[]{:S(2)}) copy-start(bf16[96,512]{1,0:T(8,128)(2,1)} %get-tuple-element.31) | copy-start | bytes 294916
  23.6 11.4 %all-to-all-start.1 = ((bf16[16,32,80]{2,1,0:T(8,128)(2,1)}), bf16[16,32,80]{2,1,0:T(8,128)(2,1)S(1)}, u32[]{:S(2)}, u32[]{:S(2)}) async-start(bf16[16,32,80]{2,1,0:T(8,128)(2,1)} %bitcast.3), calls=%async_computation.1 | async-start | bytes 262144 | tf_op jit(solution)/shard_map/all_to_all | solution.py:42
  35.2 32.7 %copy-start.3 = (f32[80,256]{1,0:T(8,128)}, f32[80,256]{1,0:T(8,128)S(1)}, u32[]{:S(2)}) copy-start(f32[80,256]{1,0:T(8,128)S(1)} %fusion.4.refs_0_) | copy-start | bytes 245764
  38.5 29.5 %all-to-all-start.2 = ((bf16[16,80,128]{2,1,0:T(8,128)(2,1)}), bf16[16,80,128]{2,1,0:T(8,128)(2,1)S(1)}, u32[]{:S(2)}, u32[]{:S(2)}) async-start(bf16[16,80,128]{2,1,0:T(8,128)(2,1)} %shard_map.174), calls=%async_computation.2 | async-start | bytes 655360 | tf_op jit(solution)/shard_map/all_to_all | solution.py:401
  42.4 12.5 %collective-permute-start.2 = (bf16[96,512]{1,0:T(8,128)(2,1)S(1)}, bf16[96,512]{1,0:T(8,128)(2,1)S(1)}, u32[]{:S(2)}, u32[]{:S(2)}) collective-permute-start(bf16[96,512]{1,0:T(8,128)(2,1)S(1)} %copy-done.15), channel_id=1, source_target_pairs={{0,24},{2,26},{4,28},{6,30},{8,16},{10,18},{12,20},{14,22},{16,8},... | collective-permute-start | bytes 294920 | tf_op jit(solution)/shard_map/ppermute | solution.py:486
  46.1 15.1 %collective-permute-start.1 = (bf16[96,512]{1,0:T(8,128)(2,1)S(1)}, bf16[96,512]{1,0:T(8,128)(2,1)S(1)}, u32[]{:S(2)}, u32[]{:S(2)}) collective-permute-start(bf16[96,512]{1,0:T(8,128)(2,1)S(1)} %copy-done.15), channel_id=1, source_target_pairs={{0,16},{2,18},{4,20},{6,22},{8,24},{10,26},{12,28},{14,30},{16,0},... | collective-permute-start | bytes 294920 | tf_op jit(solution)/shard_map/ppermute | solution.py:486
  46.1 15.1 %collective-permute-start = (bf16[96,512]{1,0:T(8,128)(2,1)S(1)}, bf16[96,512]{1,0:T(8,128)(2,1)S(1)}, u32[]{:S(2)}, u32[]{:S(2)}) collective-permute-start(bf16[96,512]{1,0:T(8,128)(2,1)S(1)} %copy-done.15), channel_id=1, source_target_pairs={{0,8},{2,10},{4,12},{6,14},{8,0},{10,2},{12,4},{14,6},{16,24},{18,... | collective-permute-start | bytes 294920 | tf_op jit(solution)/shard_map/ppermute | solution.py:486
  54.9 6.3 %copy-start.10 = (bf16[96,512]{1,0:T(8,128)(2,1)}, bf16[96,512]{1,0:T(8,128)(2,1)S(1)}, u32[]{:S(2)}) copy-start(bf16[96,512]{1,0:T(8,128)(2,1)S(1)} %collective-permute-done.2.refs_6_) | copy-start | bytes 294916
  71.9 4.0 %copy-start.8 = (bf16[512,512]{1,0:T(8,128)(2,1)S(1)}, bf16[512,512]{1,0:T(8,128)(2,1)}, u32[]{:S(2)}) copy-start(bf16[512,512]{1,0:T(8,128)(2,1)} %refs_3_.5) | copy-start | bytes 1572868
  71.9 7.4 %collective-permute-start.3 = (bf16[336,256]{1,0:T(8,128)(2,1)S(1)}, bf16[336,256]{1,0:T(8,128)(2,1)S(1)}, u32[]{:S(2)}, u32[]{:S(2)}) collective-permute-start(bf16[336,256]{1,0:T(8,128)(2,1)S(1)} %get-tuple-element.43), channel_id=1, source_target_pairs={{0,2},{2,0},{4,6},{6,4},{8,10},{10,8},{12,14},{14,12},{16,18},{18,... | collective-permute-start | bytes 516104 | tf_op jit(solution)/shard_map/ppermute | solution.py:527
  73.5 9.1 %collective-permute-start.4 = (bf16[336,256]{1,0:T(8,128)(2,1)S(1)}, bf16[336,256]{1,0:T(8,128)(2,1)S(1)}, u32[]{:S(2)}, u32[]{:S(2)}) collective-permute-start(bf16[336,256]{1,0:T(8,128)(2,1)S(1)} %get-tuple-element.44), channel_id=1, source_target_pairs={{0,4},{2,6},{4,0},{6,2},{8,12},{10,14},{12,8},{14,10},{16,20},{18,... | collective-permute-start | bytes 516104 | tf_op jit(solution)/shard_map/ppermute | solution.py:527
  75.0 7.6 %collective-permute-start.5 = (bf16[336,256]{1,0:T(8,128)(2,1)S(1)}, bf16[336,256]{1,0:T(8,128)(2,1)S(1)}, u32[]{:S(2)}, u32[]{:S(2)}) collective-permute-start(bf16[336,256]{1,0:T(8,128)(2,1)S(1)} %get-tuple-element.45), channel_id=1, source_target_pairs={{0,6},{2,4},{4,2},{6,0},{8,14},{10,12},{12,10},{14,8},{16,22},{18,... | collective-permute-start | bytes 516104 | tf_op jit(solution)/shard_map/ppermute | solution.py:527
  75.7 1.0 %copy-start.14 = (f32[256,512]{1,0:T(8,128)S(1)}, f32[256,512]{1,0:T(8,128)}, u32[]{:S(2)}) copy-start(f32[256,512]{1,0:T(8,128)} %get-tuple-element.41) | copy-start | bytes 1572868
  76.7 1.0 %copy-start = (bf16[512,512]{1,0:T(8,128)(2,1)S(1)}, bf16[512,512]{1,0:T(8,128)(2,1)}, u32[]{:S(2)}) copy-start(bf16[512,512]{1,0:T(8,128)(2,1)} %refs_2_.7) | copy-start | bytes 1572868
  77.8 1.1 %copy-start.9 = (f32[256,512]{1,0:T(8,128)S(1)}, f32[256,512]{1,0:T(8,128)}, u32[]{:S(2)}) copy-start(f32[256,512]{1,0:T(8,128)} %get-tuple-element.40) | copy-start | bytes 1572868
  82.7 7.7 %collective-permute-start.8 = (bf16[336,256]{1,0:T(8,128)(2,1)S(1)}, bf16[336,256]{1,0:T(8,128)(2,1)S(1)}, u32[]{:S(2)}, u32[]{:S(2)}) collective-permute-start(bf16[336,256]{1,0:T(8,128)(2,1)S(1)} %add_convert_fusion.refs_4_), channel_id=1, source_target_pairs={{0,6},{2,4},{4,2},{6,0},{8,14},{10,12},{12,10},{14,8},{16,22},{18,... | collective-permute-start | bytes 516104 | tf_op jit(solution)/shard_map/ppermute | solution.py:529
  84.1 7.8 %collective-permute-start.7 = (bf16[336,256]{1,0:T(8,128)(2,1)S(1)}, bf16[336,256]{1,0:T(8,128)(2,1)S(1)}, u32[]{:S(2)}, u32[]{:S(2)}) collective-permute-start(bf16[336,256]{1,0:T(8,128)(2,1)S(1)} %add_convert_fusion.refs_4_), channel_id=1, source_target_pairs={{0,4},{2,6},{4,0},{6,2},{8,12},{10,14},{12,8},{14,10},{16,20},{18,... | collective-permute-start | bytes 516104 | tf_op jit(solution)/shard_map/ppermute | solution.py:529
  85.3 6.7 %collective-permute-start.6 = (bf16[336,256]{1,0:T(8,128)(2,1)S(1)}, bf16[336,256]{1,0:T(8,128)(2,1)S(1)}, u32[]{:S(2)}, u32[]{:S(2)}) collective-permute-start(bf16[336,256]{1,0:T(8,128)(2,1)S(1)} %add_convert_fusion.refs_4_), channel_id=1, source_target_pairs={{0,2},{2,0},{4,6},{6,4},{8,10},{10,8},{12,14},{14,12},{16,18},{18,... | collective-permute-start | bytes 516104 | tf_op jit(solution)/shard_map/ppermute | solution.py:529
  (4 other events, 2.8 us)

commit v5 on v4

--- a/solution.py
+++ b/solution.py
@@ -60,7 +60,7 @@
     return full.reshape(rows, width).astype(f32)
 
 
-TABLE_ROWS = 16
+TABLE_ROWS = 8
 LANES = 128
 
 
@@ -141,7 +141,7 @@
         copy.wait()
 
 
-def node_forward(cells, channel_dim, table, scale_ref, expand_ref, contract_ref, lift_ref, ready):
+def node_forward(cells, channel_dim, table, scale_ref, expand_ref, contract_ref, lift_ref, ready, keep=None):
     node_rows = MESH_DEV
     slots = cells.shape[1 - channel_dim]
     subs = lax.broadcasted_iota(jnp.int32, (node_rows, LANES), 0).astype(f32)
@@ -152,12 +152,20 @@
     count = mm(landing, jnp.ones((slots, LANES), bf16), 1, 0)[:, 0:1]
     state = mm(landing, latent, 1, 0) * (1.0 / jnp.maximum(count, 1.0))
     recip = lax.rsqrt(jnp.mean(state * state, axis=1, keepdims=True) + norm_eps)
+    if keep:
+        keep(2, state)
     ready()
     normed = (state * recip * scale_ref[...]).astype(bf16)
+    if keep:
+        keep(4, normed)
     pre = mm(normed, expand_ref[...], 1, 0)
+    if keep:
+        keep(3, pre)
     bent = jnp.tanh(pre)
     above = 1.0 + bent
     bend = (above * (1.0 + pre * (1.0 - bent))).astype(bf16)
+    if keep:
+        keep(5, bend)
     hidden = (pre * above).astype(bf16)
     following = (state + mm(hidden, contract_ref[...], 1, 0)).astype(bf16)
     return state, pre, normed, bend, following, hidden
@@ -176,53 +184,77 @@
     chosen_ref,
     *rest,
 ):
-    count = (len(rest) - 1) // 2
-    out_refs, bufs, sems = rest[:count], rest[count:-1], rest[-1]
+    count = len(rest) // 2
+    out_refs, bufs, sems = (chosen_ref,) + rest[: count - 1], rest[count - 1 : -1], rest[-1]
     copies = [pltpu.make_async_copy(a, b, sems.at[i]) for i, (a, b) in enumerate(zip(bufs, out_refs))]
-    parcel_buf, state_buf, pre_buf, normed_buf, bend_buf, both_buf = bufs
+    chosen_buf, parcel_buf, _, _, _, _, both_buf = bufs
     slots = cells_ref.shape[0]
     width = both_buf.shape[1] // 2
     parts = slots // LANES
     table = table_ref[...]
     parcel_buf[0:channels, :] = cells_ref[...].astype(f32).T.astype(bf16)
     parcel_buf[channels:, :] = jnp.concatenate([table] * parts, axis=1).astype(bf16)
-    copies[0].start()
-    state, pre, normed, bend, following, hidden = node_forward(
-        cells_ref[...], 1, table, scale_ref, expand_ref, contract_ref, lift_ref, lambda: ready(3, 4, 5, 6)
+    copies[1].start()
+
+    def keep(at, value):
+        bufs[at][...] = value
+        copies[at].start()
+
+    ready(2)
+    state, _, _, _, following, hidden = node_forward(
+        cells_ref[...],
+        1,
+        table,
+        scale_ref,
+        expand_ref,
+        contract_ref,
+        lift_ref,
+        lambda: ready(3, 4, 5, 6),
+        keep,
     )
     both_buf[:, 0:width] = following
+    both_buf[:, width:] = hidden
+    copies[6].start()
     projected = mm(following, readout_ref[...], 1, 1).astype(bf16)
     subs = lax.broadcasted_iota(jnp.int32, (state.shape[0], LANES), 0).astype(f32)
     for j in range(parts):
         pick = one_hot(subs, table[parts + j : parts + j + 1, :])
-        chosen_ref[j * LANES : (j + 1) * LANES, :] = mm(pick, projected, 0, 0).astype(bf16)
-    state_buf[...] = state
-    pre_buf[...] = pre
-    normed_buf[...] = normed
-    bend_buf[...] = bend
-    both_buf[:, width:] = hidden
-    for copy in copies[1:]:
-        copy.start()
+        chosen_buf[j * LANES : (j + 1) * LANES, :] = mm(pick, projected, 0, 0).astype(bf16)
+    copies[0].start()
     for copy in copies:
         copy.wait()
 
 
-def mates_kernel(channels, ready, lift_ref, scale_ref, expand_ref, contract_ref, *rest):
-    mates = len(rest) - 8
-    parcel_refs = rest[:mates]
-    normed_out, bend_out, both_out, table_ref, normed_buf, bend_buf, both_buf, sems = rest[mates:]
+def mates_kernel(
+    channels,
+    ready,
+    lift_ref,
+    scale_ref,
+    expand_ref,
+    contract_ref,
+    parcel_ref,
+    normed_out,
+    bend_out,
+    both_out,
+    table_ref,
+    normed_buf,
+    bend_buf,
+    both_buf,
+    sems,
+):
+    mates = table_ref.shape[0]
     width = both_buf.shape[2] // 2
-    ready(*range(4 + mates))
+    ready(*range(5))
     pairs = [(normed_buf, normed_out), (bend_buf, bend_out), (both_buf, both_out)]
     copies = [
         [pltpu.make_async_copy(a.at[m], b.at[m], sems.at[i, m]) for i, (a, b) in enumerate(pairs)]
         for m in range(mates)
     ]
-    for m, parcel_ref in enumerate(parcel_refs):
-        table = parcel_ref[channels:, 0:LANES].astype(f32)
+    for m in range(mates):
+        table = parcel_ref[m, channels:, 0:LANES].astype(f32)
         table_ref[m] = table
         _, _, normed, bend, following, hidden = node_forward(
-            parcel_ref[0:channels, :], 0, table, scale_ref, expand_ref, contract_ref, lift_ref, lambda: None
+            parcel_ref[m, 0:channels, :], 0, table, scale_ref, expand_ref, contract_ref, lift_ref, lambda: None
         )
         normed_buf[m] = normed
         bend_buf[m] = bend
@@ -238,36 +270,34 @@
 def backward_kernel(
     group,
     channels,
+    mate_count,
     me_ref,
     grad_ref,
+    chain_ref,
     table_ref,
-    mate_table_ref,
-    chain_ref,
     normed_ref,
     bend_ref,
     both_ref,
-    mate_normed_ref,
-    mate_bend_ref,
-    mate_both_ref,
-    own_ref,
     *rest,
 ):
-    piece_refs, (value_ref, node_ref, up_ref, small_ref, normed_buf, bend_buf, both_buf, sems) = rest[:-8], rest[-8:]
+    mate_refs, own_ref, piece_refs = rest[:mate_count], rest[mate_count], rest[mate_count + 1 : -8]
+    value_ref, node_ref, up_ref, small_ref, normed_buf, bend_buf, both_buf, sems = rest[-8:]
     bands = grad_ref.shape[0]
     slots = value_ref.shape[1]
     node_rows = normed_ref.shape[0]
     cap = slots // bands
     z, xy = me_ref[0], me_ref[1]
     subs = lax.broadcasted_iota(jnp.int32, (node_rows, LANES), 0).astype(f32)
-    kept = [
-        (bend_ref, mate_bend_ref, bend_buf),
-        (normed_ref, mate_normed_ref, normed_buf),
-        (both_ref, mate_both_ref, both_buf),
-    ]
+    held = [(table_ref[...], bend_ref, normed_ref, both_ref)]
+    for at in range(0, mate_count, 4):
+        mate_normed, mate_bend, mate_both, mate_table = mate_refs[at : at + 4]
+        held += [
+            (mate_table[m], mate_bend.at[m], mate_normed.at[m], mate_both.at[m]) for m in range(mate_table.shape[0])
+        ]
     copies = [
         [
-            pltpu.make_async_copy(mate.at[s - 1] if s else own, buf.at[s], sems.at[i, s])
-            for i, (own, mate, buf) in enumerate(kept)
+            pltpu.make_async_copy(ref, buf.at[s], sems.at[i, s])
+            for i, (ref, buf) in enumerate(zip(held[s][1:], (bend_buf, normed_buf, both_buf)))
         ]
         for s in range(group)
     ]
@@ -283,7 +313,7 @@
     lax.fori_loop(0, bands, turn, 0, unroll=4)
     parts = slots // LANES
     for s in range(group):
-        table = mate_table_ref[s - 1] if s else table_ref[...]
+        table = held[s][0]
         pick = jnp.concatenate(
             [one_hot(subs, table[parts + j : parts + j + 1, :]) for j in range(parts)], axis=1
         )
@@ -314,9 +344,9 @@
 
 
 def finish_kernel(factor, me_ref, scale_ref, expand_ref, readout_ref, *rest):
-    count = len(rest) - 8
+    count = len(rest) - 11
     piece_refs = rest[:count]
-    up_out, down_out, dec_ref, gain_ref, small_ref, up_ref, down_ref, sems = rest[count:]
+    up_out, down_out, dec_out, gain_out, small_ref, up_ref, down_ref, dec_ref, gain_ref, sems, last_sems = rest[count:]
     rows = up_ref.shape[0] // count
     half = up_ref.shape[1] // 2
     lanes = small_ref.shape[1] // count
@@ -333,18 +363,24 @@
         up_copies[p].start()
         at = pl.ds(pl.multiple_of((me_ref[1] ^ p) * lanes, lanes), lanes)
         small_ref[:, at] = piece_ref[2 * rows :, :].astype(f32) * factor
+    dec_ref[...] = small_ref[:, 0:width]
+    last_copies = [
+        pltpu.make_async_copy(dec_ref, dec_out, last_sems.at[0]),
+        pltpu.make_async_copy(gain_ref, gain_out, last_sems.at[1]),
+    ]
+    last_copies[0].start()
     high = small_ref[:, width:].astype(bf16)
     low = (small_ref[:, width:] - high.astype(f32)).astype(bf16)
     for p in range(count):
         at = slice(p * rows, (p + 1) * rows)
         down_ref[at, :] = mm(high[:, at], readout_ref[...], 0, 0) + mm(low[:, at], readout_ref[...], 0, 0)
         down_copies[p].start()
-    dec_ref[...] = small_ref[:, 0:width]
     for at in places:
         gain = up_ref[at, :] * expand_ref[at, :].astype(f32)
         gain = sum(gain[:, j : j + LANES] for j in range(0, 2 * half, LANES))
         gain_ref[:, at] = jnp.sum(gain.T, axis=0, keepdims=True) / scale_ref[:, at]
-    for copy in up_copies + down_copies:
+    last_copies[1].start()
+    for copy in up_copies + down_copies + last_copies:
         copy.wait()
 
 
@@ -464,14 +500,14 @@
     arrived = all_to_all(outgoing).reshape(slots, channels)
     half_scale = 0.5 * mixing_rescale_factor[None, :]
     kept = [((node_rows, width), bf16), ((node_rows, hid), bf16), ((node_rows, width + hid), bf16)]
-    sent = [((channels + TABLE_ROWS, slots), bf16), ((node_rows, width), f32), ((node_rows, hid), f32)] + kept
+    sent = [((slots, channels), bf16), ((channels + TABLE_ROWS, slots), bf16), ((node_rows, width), f32), ((node_rows, hid), f32)] + kept
     chosen, parcel, mesh_state, half_pre, normed, bend, both = vmem_call(
         functools.partial(own_kernel, channels),
-        [((slots, channels), bf16)] + sent,
+        sent,
         scratch=sent,
         sems=[(len(sent),)],
-        left_out=range(1, 1 + len(sent)),
-        fetched=(3, 4, 5, 6),
+        left_out=range(len(sent)),
+        fetched=(2, 3, 4, 5, 6),
     )(
         None,
         arrived,
@@ -482,18 +518,20 @@
         contract_matrix,
         readout_matrix.T,
     )
-    parcels = [
-        lax.ppermute(parcel, "band", [(i, i ^ (m * crew)) for i in range(bands)]) for m in range(1, group)
-    ]
-    mate_kept = [((group - 1,) + shape, dtype) for shape, dtype in kept]
-    mate_normed, mate_bend, mate_both, mate_table = vmem_call(
-        functools.partial(mates_kernel, channels),
-        mate_kept + [((group - 1, TABLE_ROWS, LANES), f32)],
-        scratch=mate_kept,
-        sems=[(3, group - 1)],
-        left_out=(0, 1, 2),
-        fetched=range(4 + len(parcels)),
-    )(None, lattice_lift_matrix, half_scale, expand_matrix, contract_matrix, *parcels)
+    parcels, mates = parcel[None], []
+    while parcels.shape[0] < group:
+        held = parcels.shape[0]
+        more = lax.ppermute(parcels, "band", [(i, i ^ (held * crew)) for i in range(bands)])
+        parcels = jnp.concatenate([parcels, more])
+        mate_kept = [((held,) + shape, dtype) for shape, dtype in kept]
+        mates += vmem_call(
+            functools.partial(mates_kernel, channels),
+            mate_kept + [((held, TABLE_ROWS, LANES), f32)],
+            scratch=mate_kept,
+            sems=[(3, held)],
+            left_out=(0, 1, 2),
+            fetched=range(5),
+        )(None, lattice_lift_matrix, half_scale, expand_matrix, contract_matrix, more)
     chain = (0.5 * mm(readout_matrix, contract_matrix, 0, 1)).astype(bf16)
     slot_values = exchange(chosen, bands)
     fill_map = (cell_ids[:, None] == dec_recv[0].reshape(-1)[None, :]).astype(bf16)
@@ -511,7 +549,7 @@
     returned = all_to_all(outgoing)
     piece_rows = 2 * (width // crew) + channels
     node_grad, *pieces = vmem_call(
-        functools.partial(backward_kernel, group, channels),
+        functools.partial(backward_kernel, group, channels, len(mates)),
         [((node_rows, channels), f32)] + [((piece_rows, hid // 2), bf16)] * crew,
         scratch=[
             ((group, slots, channels), bf16),
@@ -521,8 +559,8 @@
         ]
         + [((group,) + shape, dtype) for shape, dtype in kept],
         sems=[(3, group)],
-        left_in=range(4, 10),
-    )(me, returned, table, mate_table, chain, normed, bend, both, mate_normed, mate_bend, mate_both)
+        left_in=[3, 4, 5] + [6 + i for i in range(len(mates)) if i % 4 < 3],
+    )(me, returned, chain, table, normed, bend, both, *mates)
     swaps = [[(i, i ^ p) for i in range(bands)] for p in range(1, crew)]
     others = [lax.ppermute(piece, "band", swap) for piece, swap in zip(pieces[1:], swaps)]
     total = sum(x.astype(f32) for x in [pieces[0]] + others).astype(bf16)
@@ -537,12 +575,13 @@
         readout_matrix,
     )
     factor = 1.0 / math.sqrt(bands * node_rows)
+    whole = [((width, hid), f32), ((hid, width), f32), ((channels, width), f32), ((1, width), f32)]
     grad_up, grad_down, grad_dec, grad_gain = vmem_call(
         functools.partial(finish_kernel, factor),
-        [((width, hid), f32), ((hid, width), f32), ((channels, width), f32), ((1, width), f32)],
-        scratch=[((channels, width + hid), f32), ((width, hid), f32), ((hid, width), f32)],
-        sems=[(2, crew)],
-        left_out=(0, 1),
+        whole,
+        scratch=[((channels, width + hid), f32)] + whole,
+        sems=[(2, crew), (2,)],
+        left_out=range(4),
     )(me, mixing_rescale_factor[None, :], expand_matrix, readout_matrix.T, *totals)
     return (
         student_outputs[None],

time: 95.5 us -> 95.2 us (level)
  Pallas kernels: 19.4 us -> 20.8 us
  waiting for transfers between devices: 33.6 us -> 32.5 us
    ppermute x3 -> x2, waiting for transfers between devices: 14.3 us -> 11.8 us  [column_body(): lax.ppermute(parcels, 'band', [(i, i ^ held * crew) for i in range(bands)])]
    all_to_all x2, waiting for transfers between devices: 3.56 us -> 5.14 us  [all_to_all(): return lax.all_to_all(x, 'band', split_axis=0, concat_axis=0, tiled=True)]
    pallas_call x6 -> x7, Pallas kernels: 19.4 us -> 20.8 us  [call(): pl.pallas_call(run, out_shape=[(pltpu.HBM if i in left_out else jax.Shape...]
    ppermute x3 -> x2, starting transfers between devices: 4.45 us -> 4.73 us  [column_body(): lax.ppermute(parcels, 'band', [(i, i ^ held * crew) for i in range(bands)])]
    unnamed x32 -> x30, local copies, waits for them, and re-layouts: 4.01 us -> 4.2 us
  transfers between devices with their start and end apart: 12 -> 11, of which waited for: 7 -> 7; matrix products, arithmetic and copies ran while one was open for 6% -> 4% of each run, Pallas kernels for 6% -> 8%
where the time goes in v5:
time: 95.2 us; the launch traced here: 94.3 us
  waiting for transfers between devices  32.5 us (34%)
  starting transfers between devices  27.7 us (29%)
  Pallas kernels  20.8 us (22%)
  local copies, waits for them, and re-layouts  4.28 us (4%)
  blocking collectives  3.91 us (4%)
  matrix products  2.43 us (3%)
  other arithmetic  1.81 us (2%)
    pallas_call x7, Pallas kernels, call(): pl.pallas_call(run, out_shape=[(pltpu.HBM if i in left_out else jax.Shape...  20.8 us
    all_to_all x2, starting transfers between devices, all_to_all(): return lax.all_to_all(x, 'band', split_axis=0, concat_axis=0, tiled=True)  12.2 us
    ppermute x2, waiting for transfers between devices, column_body(): lax.ppermute(parcels, 'band', [(i, i ^ held * crew) for i in range(bands)])  11.8 us
    all_to_all x1, waiting for transfers between devices, exchange(): lax.all_to_all(x.reshape(band_count, rows // band_count, width), 'band',...  7.75 us
    ppermute x3, waiting for transfers between devices, column_body(): totals = [total] + [lax.ppermute(total, 'band', swap) for swap in swaps]  5.18 us
    all_to_all x2, waiting for transfers between devices, all_to_all(): return lax.all_to_all(x, 'band', split_axis=0, concat_axis=0, tiled=True)  5.14 us
    ppermute x2, starting transfers between devices, column_body(): lax.ppermute(parcels, 'band', [(i, i ^ held * crew) for i in range(bands)])  4.73 us
    unnamed x30, local copies, waits for them, and re-layouts  4.2 us
  transfers between devices with their start and end apart: 11, of which 7 were waited for; matrix products, arithmetic and copies ran while one was open for 4% of the time, Pallas kernels for 8%

profile of v5, /device:TPU:0, one launch (start us, length us, event | category | flops | bytes accessed | tf_op | source)
XLA Modules:
  0.0 94.3 jit_solution(15006184290423027751)
XLA Ops:
  0.6 2.2 %shard_map.172 = (bf16[16,32,80]{2,1,0:T(8,128)(2,1)}, f32[8,128]{1,0:T(8,128)S(1)}) custom-call(f32[80,256]{1,0:T(8,128)} %refs_0_.3, bf16[1,80,256]{2,1,0:T(8,128)(2,1)} %refs_1_.1, s32[1,16,32]{2,1,0:T(8,128)} %refs_2_.5, s32[1,16,32]{2,1,0:T(8,128)} %refs_3_.4, s32[1,16,32]{2,1,0:T(8,128)} %refs_4_.2), custom_call_target="tpu_custom_call" | custom-call | tf_op jit(solution)/shard_map/pallas_call | solution.py:418
  2.9 8.5 %all-to-all-start = ((bf16[16,32,80]{2,1,0:T(8,128)(2,1)}), bf16[16,32,80]{2,1,0:T(8,128)(2,1)S(1)}, u32[]{:S(2)}, u32[]{:S(2)}) async-start(bf16[16,32,80]{2,1,0:T(8,128)(2,1)} %get-tuple-element.32), calls=%async_computation | async-start | bytes 262144 | tf_op jit(solution)/shard_map/all_to_all | solution.py:437
  12.1 1.9 %all_gather.8.refs_2_ = bf16[2,80,256]{2,1,0:T(8,128)(2,1)S(1)} all-gather(bf16[1,80,256]{2,1,0:T(8,128)(2,1)S(1)} %copy-done.13), channel_id=1, replica_groups=mesh['band'=16,'member'=2] {'member'}, dimensions={0}, use_global_device_ids=true | all-gather | bytes 122880 | tf_op jit(solution)/shard_map/all_gather | solution.py:541
  14.1 5.1 %all-to-all-done = bf16[16,32,80]{2,1,0:T(8,128)(2,1)S(1)} async-done(((bf16[16,32,80]{2,1,0:T(8,128)(2,1)}), bf16[16,32,80]{2,1,0:T(8,128)(2,1)S(1)}, u32[]{:S(2)}, u32[]{:S(2)}) %all-to-all-start) | async-done | bytes 81952 | tf_op jit(solution)/shard_map/all_to_all | solution.py:437
  19.2 3.3 %shard_map.173 = (bf16[512,80]{1,0:T(8,128)(2,1)}, bf16[88,512]{1,0:T(8,128)(2,1)}, f32[256,512]{1,0:T(8,128)}, f32[256,512]{1,0:T(8,128)}, bf16[256,512]{1,0:T(...) custom-call(bf16[512,80]{1,0:T(8,128)(2,1)S(1)} %bitcast.31, ...), custom_call_target="tpu_custom_call" | custom-call | tf_op jit(solution)/shard_map/pallas_call | solution.py:418
  22.5 3.7 %all-to-all-start.1 = ((bf16[16,32,80]{2,1,0:T(8,128)(2,1)}), bf16[16,32,80]{2,1,0:T(8,128)(2,1)S(1)}, u32[]{:S(2)}, u32[]{:S(2)}) async-start(bf16[16,32,80]{2,1,0:T(8,128)(2,1)} %bitcast.35), calls=%async_computation.1 | async-start | bytes 262144 | tf_op jit(solution)/shard_map/all_to_all | solution.py:42
  26.2 7.8 %all-to-all-done.1 = bf16[16,32,80]{2,1,0:T(8,128)(2,1)S(1)} async-done(((bf16[16,32,80]{2,1,0:T(8,128)(2,1)}), bf16[16,32,80]{2,1,0:T(8,128)(2,1)S(1)}, u32[]{:S(2)}, u32[]{:S(2)}) %all-to-all-start.1) | async-done | bytes 81952 | tf_op jit(solution)/shard_map/all_to_all | solution.py:42
  34.2 2.1 %all-gather = f32[160,256]{1,0:T(8,128)S(1)} all-gather(f32[80,256]{1,0:T(8,128)S(1)} %fusion.4.refs_0_), channel_id=2, replica_groups=mesh['band'=16,'member'=2] {'member'}, dimensions={0}, use_global_device_ids=true | all-gather | bytes 245760 | tf_op jit(solution)/shard_map/all_gather | solution.py:540
  36.3 1.4 %shard_map.174 = bf16[16,80,128]{2,1,0:T(8,128)(2,1)} custom-call(f32[80,256]{1,0:T(8,128)S(1)} %fusion.4.refs_0_, f32[2,80,256]{2,1,0:T(8,128)S(1)} %bitcast.30, bf16[2,80,256]{2,1,0:T(8,128)(2,1)S(1)} %all_gather.8.refs_2_, bf16[80,256]{1,0:T(8,128)(2,1)S(1)} %copy-done.3, f32[1,256]{1,0:T(1,128)S(1)} %bitcast.34, s32[1,16,32]{2,1,0:T(8,128)S(1)} %copy-done.4), custom_call_target="tpu_custom_call" | custom-call | tf_op jit(solution)/shard_map/pallas_call | solution.py:418
  37.7 3.7 %all-to-all-start.2 = ((bf16[16,80,128]{2,1,0:T(8,128)(2,1)}), bf16[16,80,128]{2,1,0:T(8,128)(2,1)S(1)}, u32[]{:S(2)}, u32[]{:S(2)}) async-start(bf16[16,80,128]{2,1,0:T(8,128)(2,1)} %shard_map.174), calls=%async_computation.2 | async-start | bytes 655360 | tf_op jit(solution)/shard_map/all_to_all | solution.py:437
  41.4 1.9 %collective-permute-start = (bf16[1,88,512]{2,1,0:T(8,128)(2,1)S(1)}, bf16[1,88,512]{2,1,0:T(8,128)(2,1)S(1)}, u32[]{:S(2)}, u32[]{:S(2)}) collective-permute-start(bf16[1,88,512]{2,1,0:T(8,128)(2,1)S(1)} %bitcast.37), channel_id=1, source_target_pairs={{0,8},{2,10},{4,12},{6,14},{8,0},{10,2},{12,4},{14,6},{16,24},{18,... | collective-permute-start | bytes 270344 | tf_op jit(solution)/shard_map/ppermute | solution.py:524
  43.3 7.5 %collective-permute-done.refs_4_ = bf16[1,88,512]{2,1,0:T(8,128)(2,1)S(1)} collective-permute-done((bf16[1,88,512]{2,1,0:T(8,128)(2,1)S(1)}, bf16[1,88,512]{2,1,0:T(8,128)(2,1)S(1)}, u32[]{:S(2)}, u32[]{:S(2)}) %collective-permute-start) | collective-permute-done | bytes 90144 | tf_op jit(solution)/shard_map/ppermute | solution.py:524
  51.5 2.9 %collective-permute-start.1 = (bf16[2,88,512]{2,1,0:T(8,128)(2,1)S(1)}, bf16[2,88,512]{2,1,0:T(8,128)(2,1)S(1)}, u32[]{:S(2)}, u32[]{:S(2)}) collective-permute-start(bf16[2,88,512]{2,1,0:T(8,128)(2,1)S(1)} %pad_maximum_fusion), channel_id=1, source_target_pairs={{0,16},{2,18},{4,20},{6,22},{8,24},{10,26},{12,28},{14,30},{16,0},... | collective-permute-start | bytes 540680 | tf_op jit(solution)/shard_map/ppermute | solution.py:524
  54.7 3.3 %shard_map.175 = (bf16[1,256,512]{2,1,0:T(8,128)(2,1)}, bf16[1,256,512]{2,1,0:T(8,128)(2,1)}, bf16[1,256,1024]{2,1,0:T(8,128)(2,1)}, f32[1,8,128]{2,1,0:T(8,128)S(1)}) custom-call(bf16[80,512]{1,0:T(8,128)(2,1)} %refs_0_.5, f32[1,512]{1,0:T(1,128)} %bitcast.40, bf16[512,512]{1,0:T(8,128)(2,1)} %refs_2_.9, bf16[512,512]{1,0:T(8,128)(2,1)} %refs_3_.7, ...), custom_call_target="tpu_custom_call" | custom-call | tf_op jit(solution)/shard_map/pallas_call | solution.py:418
  58.0 4.2 %collective-permute-done.1.refs_4_ = bf16[2,88,512]{2,1,0:T(8,128)(2,1)S(1)} collective-permute-done((bf16[2,88,512]{2,1,0:T(8,128)(2,1)S(1)}, bf16[2,88,512]{2,1,0:T(8,128)(2,1)S(1)}, u32[]{:S(2)}, u32[]{:S(2)}) %collective-permute-start.1) | collective-permute-done | bytes 180256 | tf_op jit(solution)/shard_map/ppermute | solution.py:524
  62.9 4.4 %shard_map.176 = (bf16[2,256,512]{2,1,0:T(8,128)(2,1)}, bf16[2,256,512]{2,1,0:T(8,128)(2,1)}, bf16[2,256,1024]{2,1,0:T(8,128)(2,1)}, f32[2,8,128]{2,1,0:T(8,128)S(1)}) custom-call(bf16[80,512]{1,0:T(8,128)(2,1)} %refs_0_.5, f32[1,512]{1,0:T(1,128)} %bitcast.41, bf16[512,512]{1,0:T(8,128)(2,1)} %refs_2_.9, bf16[512,512]{1,0:T(8,128)(2,1)} %refs_3_.7, ...), custom_call_target="tpu_custom_call" | custom-call | tf_op jit(solution)/shard_map/pallas_call | solution.py:418
  67.3 3.9 %shard_map.177 = (f32[256,80]{1,0:T(8,128)S(1)}, bf16[336,256]{1,0:T(8,128)(2,1)S(1)}, bf16[336,256]{1,0:T(8,128)(2,1)S(1)}, bf16[336,256]{1,0:T(8,128)(2,1)S(1)}, bf16[336,256]{1,0:T(8,128)(2,1)S(1)}) custom-call(s32[2]{0:T(128)S(1)} %pad_add_fusion.refs_0_, bf16[16,80,128]{2,1,0:T(8,128)(2,1)S(1)} %all-to-all-done.2.refs_1_, ...), custom_call_target="tpu_custom_call" | custom-call | tf_op jit(solution)/shard_map/pallas_call | solution.py:418
  71.3 1.5 %collective-permute-start.2 = (bf16[336,256]{1,0:T(8,128)(2,1)S(1)}, bf16[336,256]{1,0:T(8,128)(2,1)S(1)}, u32[]{:S(2)}, u32[]{:S(2)}) collective-permute-start(bf16[336,256]{1,0:T(8,128)(2,1)S(1)} %get-tuple-element.51), channel_id=1, source_target_pairs={{0,2},{2,0},{4,6},{6,4},{8,10},{10,8},{12,14},{14,12},{16,18},{18,... | collective-permute-start | bytes 516104 | tf_op jit(solution)/shard_map/ppermute | solution.py:565
  72.8 1.5 %collective-permute-start.3 = (bf16[336,256]{1,0:T(8,128)(2,1)S(1)}, bf16[336,256]{1,0:T(8,128)(2,1)S(1)}, u32[]{:S(2)}, u32[]{:S(2)}) collective-permute-start(bf16[336,256]{1,0:T(8,128)(2,1)S(1)} %get-tuple-element.52), channel_id=1, source_target_pairs={{0,4},{2,6},{4,0},{6,2},{8,12},{10,14},{12,8},{14,10},{16,20},{18,... | collective-permute-start | bytes 516104 | tf_op jit(solution)/shard_map/ppermute | solution.py:565
  79.7 2.6 %collective-permute-done.3 = bf16[336,256]{1,0:T(8,128)(2,1)S(1)} collective-permute-done((bf16[336,256]{1,0:T(8,128)(2,1)S(1)}, bf16[336,256]{1,0:T(8,128)(2,1)S(1)}, u32[]{:S(2)}, u32[]{:S(2)}) %collective-permute-start.3) | collective-permute-done | bytes 172064 | tf_op jit(solution)/shard_map/ppermute | solution.py:565
  82.4 1.5 %collective-permute-start.7 = (bf16[336,256]{1,0:T(8,128)(2,1)S(1)}, bf16[336,256]{1,0:T(8,128)(2,1)S(1)}, u32[]{:S(2)}, u32[]{:S(2)}) collective-permute-start(bf16[336,256]{1,0:T(8,128)(2,1)S(1)} %add_convert_fusion.refs_4_), channel_id=1, source_target_pairs={{0,6},{2,4},{4,2},{6,0},{8,14},{10,12},{12,10},{14,8},{16,22},{18,... | collective-permute-start | bytes 516104 | tf_op jit(solution)/shard_map/ppermute | solution.py:567
  86.9 3.3 %collective-permute-done.7.refs_7_ = bf16[336,256]{1,0:T(8,128)(2,1)S(1)} collective-permute-done((bf16[336,256]{1,0:T(8,128)(2,1)S(1)}, bf16[336,256]{1,0:T(8,128)(2,1)S(1)}, u32[]{:S(2)}, u32[]{:S(2)}) %collective-permute-start.7) | collective-permute-done | bytes 172064 | tf_op jit(solution)/shard_map/ppermute | solution.py:567
  90.2 1.8 %collective-permute-done.6.refs_6_ = bf16[336,256]{1,0:T(8,128)(2,1)S(1)} collective-permute-done((bf16[336,256]{1,0:T(8,128)(2,1)S(1)}, bf16[336,256]{1,0:T(8,128)(2,1)S(1)}, u32[]{:S(2)}, u32[]{:S(2)}) %collective-permute-start.6) | collective-permute-done | bytes 172064 | tf_op jit(solution)/shard_map/ppermute | solution.py:567
  92.1 2.3 %shard_map.178 = (f32[512,512]{1,0:T(8,128)}, f32[512,512]{1,0:T(8,128)}, f32[80,512]{1,0:T(8,128)}, f32[1,512]{1,0:T(1,128)}) custom-call(s32[2]{0:T(128)S(1)} %pad_add_fusion.refs_0_, f32[1,512]{1,0:T(1,128)S(1)} %bitcast.33, bf16[512,512]{1,0:T(8,128)(2,1)S(1)} %copy-done, bf16[80,512]{1,0:T(8,128)(2,1)S(1)} %bitcast.29, ...), custom_call_target="tpu_custom_call" | custom-call | tf_op jit(solution)/shard_map/pallas_call | solution.py:418
  (55 shorter events, 11.1 us)
Async XLA Ops:
  2.9 8.5 %copy-start.5 = (f32[512]{0:T(512)S(1)}, f32[512]{0:T(512)}, u32[]{:S(2)}) copy-start(f32[512]{0:T(512)} %param.22) | copy-start | bytes 6148
  2.9 9.1 %copy-start.4 = (s32[1,16,32]{2,1,0:T(8,128)S(1)}, s32[1,16,32]{2,1,0:T(8,128)}, u32[]{:S(2)}) copy-start(s32[1,16,32]{2,1,0:T(8,128)} %refs_5_.3) | copy-start | bytes 6148
  2.9 9.2 %copy-start.13 = (bf16[1,80,256]{2,1,0:T(8,128)(2,1)S(1)}, bf16[1,80,256]{2,1,0:T(8,128)(2,1)}, u32[]{:S(2)}) copy-start(bf16[1,80,256]{2,1,0:T(8,128)(2,1)} %param.15) | copy-start | bytes 122884
  2.9 16.3 %all-to-all-start = ((bf16[16,32,80]{2,1,0:T(8,128)(2,1)}), bf16[16,32,80]{2,1,0:T(8,128)(2,1)S(1)}, u32[]{:S(2)}, u32[]{:S(2)}) async-start(bf16[16,32,80]{2,1,0:T(8,128)(2,1)} %get-tuple-element.32), calls=%async_computation | async-start | bytes 262144 | tf_op jit(solution)/shard_map/all_to_all | solution.py:437
  22.5 11.4 %copy-start.12 = (f32[80,256]{1,0:T(8,128)S(1)}, f32[80,256]{1,0:T(8,128)}, u32[]{:S(2)}) copy-start(f32[80,256]{1,0:T(8,128)} %refs_0_.3) | copy-start | bytes 245764
  22.5 11.4 %all-to-all-start.1 = ((bf16[16,32,80]{2,1,0:T(8,128)(2,1)}), bf16[16,32,80]{2,1,0:T(8,128)(2,1)S(1)}, u32[]{:S(2)}, u32[]{:S(2)}) async-start(bf16[16,32,80]{2,1,0:T(8,128)(2,1)} %bitcast.35), calls=%async_computation.1 | async-start | bytes 262144 | tf_op jit(solution)/shard_map/all_to_all | solution.py:42
  34.2 2.1 %copy-start.2 = (f32[80,256]{1,0:T(8,128)}, f32[80,256]{1,0:T(8,128)S(1)}, u32[]{:S(2)}) copy-start(f32[80,256]{1,0:T(8,128)S(1)} %fusion.4.refs_0_) | copy-start | bytes 245764
  34.2 2.1 %copy-start.3 = (bf16[80,256]{1,0:T(8,128)(2,1)S(1)}, bf16[80,256]{1,0:T(8,128)(2,1)}, u32[]{:S(2)}) copy-start(bf16[80,256]{1,0:T(8,128)(2,1)} %refs_3_.5) | copy-start | bytes 122884
  37.7 3.7 %copy-start.11 = (bf16[88,512]{1,0:T(8,128)(2,1)S(1)}, bf16[88,512]{1,0:T(8,128)(2,1)}, u32[]{:S(2)}) copy-start(bf16[88,512]{1,0:T(8,128)(2,1)} %get-tuple-element.38) | copy-start | bytes 270340
  37.7 16.7 %copy-start.6 = (bf16[512,512]{1,0:T(8,128)(2,1)S(1)}, bf16[512,512]{1,0:T(8,128)(2,1)}, u32[]{:S(2)}) copy-start(bf16[512,512]{1,0:T(8,128)(2,1)} %refs_3_.7) | copy-start | bytes 1572868
  37.7 29.7 %all-to-all-start.2 = ((bf16[16,80,128]{2,1,0:T(8,128)(2,1)}), bf16[16,80,128]{2,1,0:T(8,128)(2,1)S(1)}, u32[]{:S(2)}, u32[]{:S(2)}) async-start(bf16[16,80,128]{2,1,0:T(8,128)(2,1)} %shard_map.174), calls=%async_computation.2 | async-start | bytes 655360 | tf_op jit(solution)/shard_map/all_to_all | solution.py:437
  41.4 9.5 %collective-permute-start = (bf16[1,88,512]{2,1,0:T(8,128)(2,1)S(1)}, bf16[1,88,512]{2,1,0:T(8,128)(2,1)S(1)}, u32[]{:S(2)}, u32[]{:S(2)}) collective-permute-start(bf16[1,88,512]{2,1,0:T(8,128)(2,1)S(1)} %bitcast.37), channel_id=1, source_target_pairs={{0,8},{2,10},{4,12},{6,14},{8,0},{10,2},{12,4},{14,6},{16,24},{18,... | collective-permute-start | bytes 270344 | tf_op jit(solution)/shard_map/ppermute | solution.py:524
  43.3 11.0 %copy-start.1 = (bf16[512,80]{0,1:T(8,128)(2,1)S(1)}, bf16[512,80]{0,1:T(8,128)(2,1)}, u32[]{:S(2)}) copy-start(bf16[512,80]{0,1:T(8,128)(2,1)} %param.25) | copy-start | bytes 245764
  51.5 10.7 %collective-permute-start.1 = (bf16[2,88,512]{2,1,0:T(8,128)(2,1)S(1)}, bf16[2,88,512]{2,1,0:T(8,128)(2,1)S(1)}, u32[]{:S(2)}, u32[]{:S(2)}) collective-permute-start(bf16[2,88,512]{2,1,0:T(8,128)(2,1)S(1)} %pad_maximum_fusion), channel_id=1, source_target_pairs={{0,16},{2,18},{4,20},{6,22},{8,24},{10,26},{12,28},{14,30},{16,0},... | collective-permute-start | bytes 540680 | tf_op jit(solution)/shard_map/ppermute | solution.py:524
  71.3 8.4 %collective-permute-start.2 = (bf16[336,256]{1,0:T(8,128)(2,1)S(1)}, bf16[336,256]{1,0:T(8,128)(2,1)S(1)}, u32[]{:S(2)}, u32[]{:S(2)}) collective-permute-start(bf16[336,256]{1,0:T(8,128)(2,1)S(1)} %get-tuple-element.51), channel_id=1, source_target_pairs={{0,2},{2,0},{4,6},{6,4},{8,10},{10,8},{12,14},{14,12},{16,18},{18,... | collective-permute-start | bytes 516104 | tf_op jit(solution)/shard_map/ppermute | solution.py:565
  72.8 9.5 %collective-permute-start.3 = (bf16[336,256]{1,0:T(8,128)(2,1)S(1)}, bf16[336,256]{1,0:T(8,128)(2,1)S(1)}, u32[]{:S(2)}, u32[]{:S(2)}) collective-permute-start(bf16[336,256]{1,0:T(8,128)(2,1)S(1)} %get-tuple-element.52), channel_id=1, source_target_pairs={{0,4},{2,6},{4,0},{6,2},{8,12},{10,14},{12,8},{14,10},{16,20},{18,... | collective-permute-start | bytes 516104 | tf_op jit(solution)/shard_map/ppermute | solution.py:565
  74.3 8.0 %collective-permute-start.4 = (bf16[336,256]{1,0:T(8,128)(2,1)S(1)}, bf16[336,256]{1,0:T(8,128)(2,1)S(1)}, u32[]{:S(2)}, u32[]{:S(2)}) collective-permute-start(bf16[336,256]{1,0:T(8,128)(2,1)S(1)} %get-tuple-element.53), channel_id=1, source_target_pairs={{0,6},{2,4},{4,2},{6,0},{8,14},{10,12},{12,10},{14,8},{16,22},{18,... | collective-permute-start | bytes 516104 | tf_op jit(solution)/shard_map/ppermute | solution.py:565
  75.0 1.0 %copy-start.7 = (bf16[512,512]{1,0:T(8,128)(2,1)S(1)}, bf16[512,512]{1,0:T(8,128)(2,1)}, u32[]{:S(2)}) copy-start(bf16[512,512]{1,0:T(8,128)(2,1)} %refs_3_.7) | copy-start | bytes 1572868
  76.1 1.0 %copy-start.14 = (f32[256,512]{1,0:T(8,128)S(1)}, f32[256,512]{1,0:T(8,128)}, u32[]{:S(2)}) copy-start(f32[256,512]{1,0:T(8,128)} %get-tuple-element.49) | copy-start | bytes 1572868
  77.1 1.0 %copy-start = (bf16[512,512]{1,0:T(8,128)(2,1)S(1)}, bf16[512,512]{1,0:T(8,128)(2,1)}, u32[]{:S(2)}) copy-start(bf16[512,512]{1,0:T(8,128)(2,1)} %refs_2_.9) | copy-start | bytes 1572868
  78.2 1.0 %copy-start.8 = (f32[256,512]{1,0:T(8,128)S(1)}, f32[256,512]{1,0:T(8,128)}, u32[]{:S(2)}) copy-start(f32[256,512]{1,0:T(8,128)} %get-tuple-element.48) | copy-start | bytes 1572868
  82.4 7.8 %collective-permute-start.7 = (bf16[336,256]{1,0:T(8,128)(2,1)S(1)}, bf16[336,256]{1,0:T(8,128)(2,1)S(1)}, u32[]{:S(2)}, u32[]{:S(2)}) collective-permute-start(bf16[336,256]{1,0:T(8,128)(2,1)S(1)} %add_convert_fusion.refs_4_), channel_id=1, source_target_pairs={{0,6},{2,4},{4,2},{6,0},{8,14},{10,12},{12,10},{14,8},{16,22},{18,... | collective-permute-start | bytes 516104 | tf_op jit(solution)/shard_map/ppermute | solution.py:567
  83.9 8.1 %collective-permute-start.6 = (bf16[336,256]{1,0:T(8,128)(2,1)S(1)}, bf16[336,256]{1,0:T(8,128)(2,1)S(1)}, u32[]{:S(2)}, u32[]{:S(2)}) collective-permute-start(bf16[336,256]{1,0:T(8,128)(2,1)S(1)} %add_convert_fusion.refs_4_), channel_id=1, source_target_pairs={{0,4},{2,6},{4,0},{6,2},{8,12},{10,14},{12,8},{14,10},{16,20},{18,... | collective-permute-start | bytes 516104 | tf_op jit(solution)/shard_map/ppermute | solution.py:567
  85.1 6.9 %collective-permute-start.5 = (bf16[336,256]{1,0:T(8,128)(2,1)S(1)}, bf16[336,256]{1,0:T(8,128)(2,1)S(1)}, u32[]{:S(2)}, u32[]{:S(2)}) collective-permute-start(bf16[336,256]{1,0:T(8,128)(2,1)S(1)} %add_convert_fusion.refs_4_), channel_id=1, source_target_pairs={{0,2},{2,0},{4,6},{6,4},{8,10},{10,8},{12,14},{14,12},{16,18},{18,... | collective-permute-start | bytes 516104 | tf_op jit(solution)/shard_map/ppermute | solution.py:567
  (2 other events, 1.3 us)

commit v6 on v5

--- a/solution.py
+++ b/solution.py
@@ -94,11 +94,33 @@
 
 
 def encode_kernel(
-    group, ready, field_ref, noise_ref, send_ref, recv_ref, mesh_ref, out_ref, table_ref, block_ref, sems
+    group,
+    ready,
+    field_ref,
+    noise_ref,
+    send_ref,
+    recv_ref,
+    mesh_ref,
+    lift_in,
+    expand_in,
+    contract_in,
+    readout_in,
+    out_ref,
+    table_ref,
+    lift_ref,
+    expand_ref,
+    contract_ref,
+    readout_ref,
+    block_ref,
+    sems,
 ):
     grid_rows = field_ref.shape[1]
     bands, _ = send_ref.shape[1:]
     rows = bands // group
+    pairs = [(lift_in, lift_ref), (expand_in, expand_ref), (contract_in, contract_ref), (readout_in, readout_ref)]
+    weights = [pltpu.make_async_copy(a, b, sems.at[i + 1]) for i, (a, b) in enumerate(pairs)]
+    for copy in weights:
+        copy.start()
     ready(0, 1, 2, 3, 4)
     inputs = (field_ref[...] + noise_ref[0].astype(f32)).astype(bf16) * 0.5
 
@@ -118,7 +140,8 @@
     block_ref[...] = mm(inputs, pick, 1, 0).T.astype(bf16).reshape(block_ref.shape)
     copy = pltpu.make_async_copy(block_ref, out_ref, sems.at[0])
     copy.start()
-    copy.wait()
+    for copy in [copy] + weights:
+        copy.wait()
 
 
 def loss_kernel(
@@ -177,10 +200,10 @@
     cells_ref,
     table_ref,
     lift_ref,
-    scale_ref,
     expand_ref,
     contract_ref,
     readout_ref,
+    scale_ref,
     chosen_ref,
     *rest,
 ):
@@ -200,7 +223,6 @@
         bufs[at][...] = value
         copies[at].start()
 
-    ready(2)
     state, _, _, _, following, hidden = node_forward(
         cells_ref[...],
         1,
@@ -209,7 +231,7 @@
         expand_ref,
         contract_ref,
         lift_ref,
-        lambda: ready(3, 4, 5, 6),
+        lambda: ready(6),
         keep,
     )
     both_buf[:, 0:width] = following
@@ -233,38 +255,30 @@
     expand_ref,
     contract_ref,
     parcel_ref,
-    normed_out,
-    bend_out,
+    normed_ref,
+    bend_ref,
     both_out,
     table_ref,
-    normed_buf,
-    bend_buf,
     both_buf,
     sems,
 ):
     mates = table_ref.shape[0]
     width = both_buf.shape[2] // 2
     ready(*range(5))
-    pairs = [(normed_buf, normed_out), (bend_buf, bend_out), (both_buf, both_out)]
-    copies = [
-        [pltpu.make_async_copy(a.at[m], b.at[m], sems.at[i, m]) for i, (a, b) in enumerate(pairs)]
-        for m in range(mates)
-    ]
+    copies = [pltpu.make_async_copy(both_buf.at[m], both_out.at[m], sems.at[m]) for m in range(mates)]
     for m in range(mates):
         table = parcel_ref[m, channels:, 0:LANES].astype(f32)
         table_ref[m] = table
         _, _, normed, bend, following, hidden = node_forward(
             parcel_ref[m, 0:channels, :], 0, table, scale_ref, expand_ref, contract_ref, lift_ref, lambda: None
         )
-        normed_buf[m] = normed
-        bend_buf[m] = bend
+        normed_ref[m] = normed
+        bend_ref[m] = bend
         both_buf[m, :, 0:width] = following
         both_buf[m, :, width:] = hidden
-        for copy in copies[m]:
-            copy.start()
-    for line in copies:
-        for copy in line:
-            copy.wait()
+        copies[m].start()
+    for copy in copies:
+        copy.wait()
 
 
 def backward_kernel(
@@ -384,7 +398,7 @@
         copy.wait()
 
 
-def vmem_call(kernel, outs, scratch=(), sems=(), budget=24, left_in=(), left_out=(), fetched=()):
+def vmem_call(kernel, outs, scratch=(), sems=(), budget=24, left_in=(), left_out=(), fetched=(), vmem_in=(), vmem_out=()):
     vmem = pl.BlockSpec(memory_space=pltpu.VMEM)
     smem = pl.BlockSpec(memory_space=pltpu.SMEM)
     left = pl.BlockSpec(memory_space=pltpu.HBM)
@@ -417,7 +431,10 @@
 
         return pl.pallas_call(
             run,
-            out_shape=[(pltpu.HBM if i in left_out else jax.ShapeDtypeStruct)(s, d) for i, (s, d) in enumerate(outs)],
+            out_shape=[
+                (pltpu.HBM if i in left_out else pltpu.VMEM if i in vmem_out else jax.ShapeDtypeStruct)(s, d)
+                for i, (s, d) in enumerate(outs)
+            ],
             in_specs=[smem] * first + [left if i in outside else vmem for i in range(len(operands))],
             out_specs=[left if i in left_out else vmem for i in range(len(outs))],
             scratch_shapes=[pltpu.VMEM(s, d) for s, d in scratch]
@@ -427,7 +444,14 @@
             compiler_params=pltpu.CompilerParams(vmem_limit_bytes=budget * 2**20),
         )(
             *([] if scalars is None else [scalars]),
-            *[pltpu.with_memory_space_constraint(x, pltpu.HBM) if i in outside else x for i, x in enumerate(operands)],
+            *[
+                pltpu.with_memory_space_constraint(x, pltpu.HBM)
+                if i in outside
+                else pltpu.with_memory_space_constraint(x, pltpu.VMEM)
+                if i in vmem_in
+                else x
+                for i, x in enumerate(operands)
+            ],
         )
 
     return call
@@ -489,14 +513,17 @@
     cell_ids = jnp.arange(grid_rows, dtype=jnp.int32)
     cap = enc_send.shape[2]
     block = ((bands, cap, channels), bf16)
-    outgoing, table = vmem_call(
+    weights = (lattice_lift_matrix, expand_matrix, contract_matrix, readout_matrix.T)
+    outgoing, table, *near_weights = vmem_call(
         functools.partial(encode_kernel, group),
-        [block, ((TABLE_ROWS, LANES), f32)],
+        [block, ((TABLE_ROWS, LANES), f32)] + [(w.shape, w.dtype) for w in weights],
         scratch=[block],
-        sems=[(1,)],
+        sems=[(5,)],
+        left_in=range(5, 9),
         left_out=(0,),
+        vmem_out=range(2, 6),
         fetched=range(5),
-    )(None, scaled_atmosphere_field, perturbation, enc_send, enc_recv, dec_send)
+    )(None, scaled_atmosphere_field, perturbation, enc_send, enc_recv, dec_send, *weights)
     arrived = all_to_all(outgoing).reshape(slots, channels)
     half_scale = 0.5 * mixing_rescale_factor[None, :]
     kept = [((node_rows, width), bf16), ((node_rows, hid), bf16), ((node_rows, width + hid), bf16)]
@@ -507,17 +534,9 @@
         scratch=sent,
         sems=[(len(sent),)],
         left_out=range(len(sent)),
-        fetched=(2, 3, 4, 5, 6),
-    )(
-        None,
-        arrived,
-        table,
-        lattice_lift_matrix,
-        half_scale,
-        expand_matrix,
-        contract_matrix,
-        readout_matrix.T,
-    )
+        fetched=(6,),
+        vmem_in=(2, 3, 4, 5),
+    )(None, arrived, table, *near_weights, half_scale)
     parcels, mates = parcel[None], []
     while parcels.shape[0] < group:
         held = parcels.shape[0]
@@ -527,9 +546,10 @@
         mates += vmem_call(
             functools.partial(mates_kernel, channels),
             mate_kept + [((held, TABLE_ROWS, LANES), f32)],
-            scratch=mate_kept,
-            sems=[(3, held)],
-            left_out=(0, 1, 2),
+            scratch=mate_kept[2:],
+            sems=[(held,)],
+            left_out=(2,),
+            vmem_out=(0, 1),
             fetched=range(5),
         )(None, lattice_lift_matrix, half_scale, expand_matrix, contract_matrix, more)
     chain = (0.5 * mm(readout_matrix, contract_matrix, 0, 1)).astype(bf16)
@@ -559,7 +579,8 @@
         ]
         + [((group,) + shape, dtype) for shape, dtype in kept],
         sems=[(3, group)],
-        left_in=[3, 4, 5] + [6 + i for i in range(len(mates)) if i % 4 < 3],
+        left_in=[3, 4, 5] + [6 + i for i in range(len(mates)) if i % 4 == 2],
+        vmem_in=[6 + i for i in range(len(mates)) if i % 4 < 2],
     )(me, returned, chain, table, normed, bend, both, *mates)
     swaps = [[(i, i ^ p) for i in range(bands)] for p in range(1, crew)]
     others = [lax.ppermute(piece, "band", swap) for piece, swap in zip(pieces[1:], swaps)]

time: 95.2 us -> 94.5 us (level)
  no operation moved by 1% of the time
where the time goes in v6:
time: 94.5 us; the launch traced here: 93.7 us
  waiting for transfers between devices  32.5 us (34%)
  starting transfers between devices  27.7 us (29%)
  Pallas kernels  20.1 us (21%)
  local copies, waits for them, and re-layouts  4.28 us (5%)
  blocking collectives  3.91 us (4%)
  matrix products  2.43 us (3%)
  other arithmetic  1.81 us (2%)
    pallas_call x7, Pallas kernels, call(): pl.pallas_call(run, out_shape=[(pltpu.HBM if i in left_out else pltpu.VME...  20.1 us
    all_to_all x2, starting transfers between devices, all_to_all(): return lax.all_to_all(x, 'band', split_axis=0, concat_axis=0, tiled=True)  12.2 us
    ppermute x2, waiting for transfers between devices, column_body(): lax.ppermute(parcels, 'band', [(i, i ^ held * crew) for i in range(bands)])  11.8 us
    all_to_all x1, waiting for transfers between devices, exchange(): lax.all_to_all(x.reshape(band_count, rows // band_count, width), 'band',...  7.75 us
    ppermute x3, waiting for transfers between devices, column_body(): totals = [total] + [lax.ppermute(total, 'band', swap) for swap in swaps]  5.19 us
    all_to_all x2, waiting for transfers between devices, all_to_all(): return lax.all_to_all(x, 'band', split_axis=0, concat_axis=0, tiled=True)  5.14 us
    ppermute x2, starting transfers between devices, column_body(): lax.ppermute(parcels, 'band', [(i, i ^ held * crew) for i in range(bands)])  4.73 us
    unnamed x30, local copies, waits for them, and re-layouts  4.2 us
  transfers between devices with their start and end apart: 11, of which 7 were waited for; matrix products, arithmetic and copies ran while one was open for 4% of the time, Pallas kernels for 8%

profile of v6, /device:TPU:0, one launch (start us, length us, event | category | flops | bytes accessed | tf_op | source)
XLA Modules:
  0.0 93.7 jit_solution(7502952362018504016)
XLA Ops:
  0.6 2.5 %shard_map.172 = (bf16[16,32,80]{2,1,0:T(8,128)(2,1)}, f32[8,128]{1,0:T(8,128)S(1)}, bf16[80,512]{1,0:T(8,128)(2,1)S(1)}, bf16[512,512]{1,0:T(8,128)(2,1)S(1)}, ...) custom-call(f32[80,256]{1,0:T(8,128)} %refs_0_.3, bf16[1,80,256]{2,1,0:T(8,128)(2,1)} %refs_1_.1, ...), custom_call_target="tpu_custom_call" | custom-call | tf_op jit(solution)/shard_map/pallas_call | solution.py:432
  3.2 8.5 %all-to-all-start = ((bf16[16,32,80]{2,1,0:T(8,128)(2,1)}), bf16[16,32,80]{2,1,0:T(8,128)(2,1)S(1)}, u32[]{:S(2)}, u32[]{:S(2)}) async-start(bf16[16,32,80]{2,1,0:T(8,128)(2,1)} %get-tuple-element.36), calls=%async_computation | async-start | bytes 262144 | tf_op jit(solution)/shard_map/all_to_all | solution.py:461
  12.4 1.9 %all_gather.8.refs_2_ = bf16[2,80,256]{2,1,0:T(8,128)(2,1)S(1)} all-gather(bf16[1,80,256]{2,1,0:T(8,128)(2,1)S(1)} %copy-done.13), channel_id=1, replica_groups=mesh['band'=16,'member'=2] {'member'}, dimensions={0}, use_global_device_ids=true | all-gather | bytes 122880 | tf_op jit(solution)/shard_map/all_gather | solution.py:561
  14.4 5.1 %all-to-all-done = bf16[16,32,80]{2,1,0:T(8,128)(2,1)S(1)} async-done(((bf16[16,32,80]{2,1,0:T(8,128)(2,1)}), bf16[16,32,80]{2,1,0:T(8,128)(2,1)S(1)}, u32[]{:S(2)}, u32[]{:S(2)}) %all-to-all-start) | async-done | bytes 81952 | tf_op jit(solution)/shard_map/all_to_all | solution.py:461
  19.5 2.5 %shard_map.173 = (bf16[512,80]{1,0:T(8,128)(2,1)}, bf16[88,512]{1,0:T(8,128)(2,1)}, f32[256,512]{1,0:T(8,128)}, f32[256,512]{1,0:T(8,128)}, bf16[256,512]{1,0:T(...) custom-call(bf16[512,80]{1,0:T(8,128)(2,1)S(1)} %bitcast.31, ...), custom_call_target="tpu_custom_call" | custom-call | tf_op jit(solution)/shard_map/pallas_call | solution.py:432
  22.0 3.7 %all-to-all-start.1 = ((bf16[16,32,80]{2,1,0:T(8,128)(2,1)}), bf16[16,32,80]{2,1,0:T(8,128)(2,1)S(1)}, u32[]{:S(2)}, u32[]{:S(2)}) async-start(bf16[16,32,80]{2,1,0:T(8,128)(2,1)} %bitcast.35), calls=%async_computation.1 | async-start | bytes 262144 | tf_op jit(solution)/shard_map/all_to_all | solution.py:42
  25.7 7.8 %all-to-all-done.1 = bf16[16,32,80]{2,1,0:T(8,128)(2,1)S(1)} async-done(((bf16[16,32,80]{2,1,0:T(8,128)(2,1)}), bf16[16,32,80]{2,1,0:T(8,128)(2,1)S(1)}, u32[]{:S(2)}, u32[]{:S(2)}) %all-to-all-start.1) | async-done | bytes 81952 | tf_op jit(solution)/shard_map/all_to_all | solution.py:42
  33.7 2.1 %all-gather = f32[160,256]{1,0:T(8,128)S(1)} all-gather(f32[80,256]{1,0:T(8,128)S(1)} %fusion.4.refs_0_), channel_id=2, replica_groups=mesh['band'=16,'member'=2] {'member'}, dimensions={0}, use_global_device_ids=true | all-gather | bytes 245760 | tf_op jit(solution)/shard_map/all_gather | solution.py:560
  35.8 1.4 %shard_map.174 = bf16[16,80,128]{2,1,0:T(8,128)(2,1)} custom-call(f32[80,256]{1,0:T(8,128)S(1)} %fusion.4.refs_0_, f32[2,80,256]{2,1,0:T(8,128)S(1)} %bitcast.30, bf16[2,80,256]{2,1,0:T(8,128)(2,1)S(1)} %all_gather.8.refs_2_, bf16[80,256]{1,0:T(8,128)(2,1)S(1)} %copy-done.3, f32[1,256]{1,0:T(1,128)S(1)} %bitcast.34, s32[1,16,32]{2,1,0:T(8,128)S(1)} %copy-done.4), custom_call_target="tpu_custom_call" | custom-call | tf_op jit(solution)/shard_map/pallas_call | solution.py:432
  37.2 3.7 %all-to-all-start.2 = ((bf16[16,80,128]{2,1,0:T(8,128)(2,1)}), bf16[16,80,128]{2,1,0:T(8,128)(2,1)S(1)}, u32[]{:S(2)}, u32[]{:S(2)}) async-start(bf16[16,80,128]{2,1,0:T(8,128)(2,1)} %shard_map.174), calls=%async_computation.2 | async-start | bytes 655360 | tf_op jit(solution)/shard_map/all_to_all | solution.py:461
  40.9 1.9 %collective-permute-start = (bf16[1,88,512]{2,1,0:T(8,128)(2,1)S(1)}, bf16[1,88,512]{2,1,0:T(8,128)(2,1)S(1)}, u32[]{:S(2)}, u32[]{:S(2)}) collective-permute-start(bf16[1,88,512]{2,1,0:T(8,128)(2,1)S(1)} %bitcast.37), channel_id=1, source_target_pairs={{0,8},{2,10},{4,12},{6,14},{8,0},{10,2},{12,4},{14,6},{16,24},{18,... | collective-permute-start | bytes 270344 | tf_op jit(solution)/shard_map/ppermute | solution.py:543
  42.8 7.5 %collective-permute-done.refs_4_ = bf16[1,88,512]{2,1,0:T(8,128)(2,1)S(1)} collective-permute-done((bf16[1,88,512]{2,1,0:T(8,128)(2,1)S(1)}, bf16[1,88,512]{2,1,0:T(8,128)(2,1)S(1)}, u32[]{:S(2)}, u32[]{:S(2)}) %collective-permute-start) | collective-permute-done | bytes 90144 | tf_op jit(solution)/shard_map/ppermute | solution.py:543
  51.0 2.9 %collective-permute-start.1 = (bf16[2,88,512]{2,1,0:T(8,128)(2,1)S(1)}, bf16[2,88,512]{2,1,0:T(8,128)(2,1)S(1)}, u32[]{:S(2)}, u32[]{:S(2)}) collective-permute-start(bf16[2,88,512]{2,1,0:T(8,128)(2,1)S(1)} %pad_maximum_fusion), channel_id=1, source_target_pairs={{0,16},{2,18},{4,20},{6,22},{8,24},{10,26},{12,28},{14,30},{16,0},... | collective-permute-start | bytes 540680 | tf_op jit(solution)/shard_map/ppermute | solution.py:543
  54.2 3.3 %shard_map.175 = (bf16[1,256,512]{2,1,0:T(8,128)(2,1)S(1)}, bf16[1,256,512]{2,1,0:T(8,128)(2,1)S(1)}, bf16[1,256,1024]{2,1,0:T(8,128)(2,1)}, f32[1,8,128]{2,1,0:T(8,128)S(1)}) custom-call(bf16[80,512]{1,0:T(8,128)(2,1)} %refs_0_.5, f32[1,512]{1,0:T(1,128)} %bitcast.40, bf16[512,512]{1,0:T(8,128)(2,1)} %refs_2_.7, bf16[512,512]{1,0:T(8,128)(2,1)} %refs_3_.7, ...), custom_call_target="tpu_custom_call" | custom-call | tf_op jit(solution)/shard_map/pallas_call | solution.py:432
  57.5 4.3 %collective-permute-done.1.refs_4_ = bf16[2,88,512]{2,1,0:T(8,128)(2,1)S(1)} collective-permute-done((bf16[2,88,512]{2,1,0:T(8,128)(2,1)S(1)}, bf16[2,88,512]{2,1,0:T(8,128)(2,1)S(1)}, u32[]{:S(2)}, u32[]{:S(2)}) %collective-permute-start.1) | collective-permute-done | bytes 180256 | tf_op jit(solution)/shard_map/ppermute | solution.py:543
  62.4 4.4 %shard_map.176 = (bf16[2,256,512]{2,1,0:T(8,128)(2,1)S(1)}, bf16[2,256,512]{2,1,0:T(8,128)(2,1)S(1)}, bf16[2,256,1024]{2,1,0:T(8,128)(2,1)}, f32[2,8,128]{2,1,0:T(8,128)S(1)}) custom-call(bf16[80,512]{1,0:T(8,128)(2,1)} %refs_0_.5, f32[1,512]{1,0:T(1,128)} %bitcast.41, bf16[512,512]{1,0:T(8,128)(2,1)} %refs_2_.7, bf16[512,512]{1,0:T(8,128)(2,1)} %refs_3_.7, ...), custom_call_target="tpu_custom_call" | custom-call | tf_op jit(solution)/shard_map/pallas_call | solution.py:432
  66.8 3.8 %shard_map.177 = (f32[256,80]{1,0:T(8,128)S(1)}, bf16[336,256]{1,0:T(8,128)(2,1)S(1)}, bf16[336,256]{1,0:T(8,128)(2,1)S(1)}, bf16[336,256]{1,0:T(8,128)(2,1)S(1)}, bf16[336,256]{1,0:T(8,128)(2,1)S(1)}) custom-call(s32[2]{0:T(128)S(1)} %pad_add_fusion.refs_0_, bf16[16,80,128]{2,1,0:T(8,128)(2,1)S(1)} %all-to-all-done.2.refs_1_, ...), custom_call_target="tpu_custom_call" | custom-call | tf_op jit(solution)/shard_map/pallas_call | solution.py:432
  70.6 1.5 %collective-permute-start.2 = (bf16[336,256]{1,0:T(8,128)(2,1)S(1)}, bf16[336,256]{1,0:T(8,128)(2,1)S(1)}, u32[]{:S(2)}, u32[]{:S(2)}) collective-permute-start(bf16[336,256]{1,0:T(8,128)(2,1)S(1)} %get-tuple-element.59), channel_id=1, source_target_pairs={{0,2},{2,0},{4,6},{6,4},{8,10},{10,8},{12,14},{14,12},{16,18},{18,... | collective-permute-start | bytes 516104 | tf_op jit(solution)/shard_map/ppermute | solution.py:586
  72.1 1.5 %collective-permute-start.3 = (bf16[336,256]{1,0:T(8,128)(2,1)S(1)}, bf16[336,256]{1,0:T(8,128)(2,1)S(1)}, u32[]{:S(2)}, u32[]{:S(2)}) collective-permute-start(bf16[336,256]{1,0:T(8,128)(2,1)S(1)} %get-tuple-element.60), channel_id=1, source_target_pairs={{0,4},{2,6},{4,0},{6,2},{8,12},{10,14},{12,8},{14,10},{16,20},{18,... | collective-permute-start | bytes 516104 | tf_op jit(solution)/shard_map/ppermute | solution.py:586
  79.0 2.6 %collective-permute-done.3 = bf16[336,256]{1,0:T(8,128)(2,1)S(1)} collective-permute-done((bf16[336,256]{1,0:T(8,128)(2,1)S(1)}, bf16[336,256]{1,0:T(8,128)(2,1)S(1)}, u32[]{:S(2)}, u32[]{:S(2)}) %collective-permute-start.3) | collective-permute-done | bytes 172064 | tf_op jit(solution)/shard_map/ppermute | solution.py:586
  81.8 1.5 %collective-permute-start.7 = (bf16[336,256]{1,0:T(8,128)(2,1)S(1)}, bf16[336,256]{1,0:T(8,128)(2,1)S(1)}, u32[]{:S(2)}, u32[]{:S(2)}) collective-permute-start(bf16[336,256]{1,0:T(8,128)(2,1)S(1)} %add_convert_fusion.refs_4_), channel_id=1, source_target_pairs={{0,6},{2,4},{4,2},{6,0},{8,14},{10,12},{12,10},{14,8},{16,22},{18,... | collective-permute-start | bytes 516104 | tf_op jit(solution)/shard_map/ppermute | solution.py:588
  86.2 3.4 %collective-permute-done.7.refs_7_ = bf16[336,256]{1,0:T(8,128)(2,1)S(1)} collective-permute-done((bf16[336,256]{1,0:T(8,128)(2,1)S(1)}, bf16[336,256]{1,0:T(8,128)(2,1)S(1)}, u32[]{:S(2)}, u32[]{:S(2)}) %collective-permute-start.7) | collective-permute-done | bytes 172064 | tf_op jit(solution)/shard_map/ppermute | solution.py:588
  89.6 1.8 %collective-permute-done.6.refs_6_ = bf16[336,256]{1,0:T(8,128)(2,1)S(1)} collective-permute-done((bf16[336,256]{1,0:T(8,128)(2,1)S(1)}, bf16[336,256]{1,0:T(8,128)(2,1)S(1)}, u32[]{:S(2)}, u32[]{:S(2)}) %collective-permute-start.6) | collective-permute-done | bytes 172064 | tf_op jit(solution)/shard_map/ppermute | solution.py:588
  91.4 2.3 %shard_map.178 = (f32[512,512]{1,0:T(8,128)}, f32[512,512]{1,0:T(8,128)}, f32[80,512]{1,0:T(8,128)}, f32[1,512]{1,0:T(1,128)}) custom-call(s32[2]{0:T(128)S(1)} %pad_add_fusion.refs_0_, f32[1,512]{1,0:T(1,128)S(1)} %bitcast.33, bf16[512,512]{1,0:T(8,128)(2,1)S(1)} %copy-done, bf16[80,512]{1,0:T(8,128)(2,1)S(1)} %bitcast.29, ...), custom_call_target="tpu_custom_call" | custom-call | tf_op jit(solution)/shard_map/pallas_call | solution.py:432
  (55 shorter events, 11.1 us)
Async XLA Ops:
  3.2 8.5 %copy-start.5 = (f32[512]{0:T(512)S(1)}, f32[512]{0:T(512)}, u32[]{:S(2)}) copy-start(f32[512]{0:T(512)} %param.22) | copy-start | bytes 6148
  3.2 9.1 %copy-start.4 = (s32[1,16,32]{2,1,0:T(8,128)S(1)}, s32[1,16,32]{2,1,0:T(8,128)}, u32[]{:S(2)}) copy-start(s32[1,16,32]{2,1,0:T(8,128)} %refs_5_.3) | copy-start | bytes 6148
  3.2 9.2 %copy-start.13 = (bf16[1,80,256]{2,1,0:T(8,128)(2,1)S(1)}, bf16[1,80,256]{2,1,0:T(8,128)(2,1)}, u32[]{:S(2)}) copy-start(bf16[1,80,256]{2,1,0:T(8,128)(2,1)} %param.15) | copy-start | bytes 122884
  3.2 16.3 %all-to-all-start = ((bf16[16,32,80]{2,1,0:T(8,128)(2,1)}), bf16[16,32,80]{2,1,0:T(8,128)(2,1)S(1)}, u32[]{:S(2)}, u32[]{:S(2)}) async-start(bf16[16,32,80]{2,1,0:T(8,128)(2,1)} %get-tuple-element.36), calls=%async_computation | async-start | bytes 262144 | tf_op jit(solution)/shard_map/all_to_all | solution.py:461
  22.0 11.4 %copy-start.12 = (f32[80,256]{1,0:T(8,128)S(1)}, f32[80,256]{1,0:T(8,128)}, u32[]{:S(2)}) copy-start(f32[80,256]{1,0:T(8,128)} %refs_0_.3) | copy-start | bytes 245764
  22.0 11.4 %all-to-all-start.1 = ((bf16[16,32,80]{2,1,0:T(8,128)(2,1)}), bf16[16,32,80]{2,1,0:T(8,128)(2,1)S(1)}, u32[]{:S(2)}, u32[]{:S(2)}) async-start(bf16[16,32,80]{2,1,0:T(8,128)(2,1)} %bitcast.35), calls=%async_computation.1 | async-start | bytes 262144 | tf_op jit(solution)/shard_map/all_to_all | solution.py:42
  33.7 2.1 %copy-start.2 = (f32[80,256]{1,0:T(8,128)}, f32[80,256]{1,0:T(8,128)S(1)}, u32[]{:S(2)}) copy-start(f32[80,256]{1,0:T(8,128)S(1)} %fusion.4.refs_0_) | copy-start | bytes 245764
  33.7 2.1 %copy-start.3 = (bf16[80,256]{1,0:T(8,128)(2,1)S(1)}, bf16[80,256]{1,0:T(8,128)(2,1)}, u32[]{:S(2)}) copy-start(bf16[80,256]{1,0:T(8,128)(2,1)} %refs_3_.5) | copy-start | bytes 122884
  37.1 3.7 %copy-start.11 = (bf16[88,512]{1,0:T(8,128)(2,1)S(1)}, bf16[88,512]{1,0:T(8,128)(2,1)}, u32[]{:S(2)}) copy-start(bf16[88,512]{1,0:T(8,128)(2,1)} %get-tuple-element.46) | copy-start | bytes 270340
  37.2 16.7 %copy-start.6 = (bf16[512,512]{1,0:T(8,128)(2,1)S(1)}, bf16[512,512]{1,0:T(8,128)(2,1)}, u32[]{:S(2)}) copy-start(bf16[512,512]{1,0:T(8,128)(2,1)} %refs_3_.7) | copy-start | bytes 1572868
  37.2 29.6 %all-to-all-start.2 = ((bf16[16,80,128]{2,1,0:T(8,128)(2,1)}), bf16[16,80,128]{2,1,0:T(8,128)(2,1)S(1)}, u32[]{:S(2)}, u32[]{:S(2)}) async-start(bf16[16,80,128]{2,1,0:T(8,128)(2,1)} %shard_map.174), calls=%async_computation.2 | async-start | bytes 655360 | tf_op jit(solution)/shard_map/all_to_all | solution.py:461
  40.9 9.5 %collective-permute-start = (bf16[1,88,512]{2,1,0:T(8,128)(2,1)S(1)}, bf16[1,88,512]{2,1,0:T(8,128)(2,1)S(1)}, u32[]{:S(2)}, u32[]{:S(2)}) collective-permute-start(bf16[1,88,512]{2,1,0:T(8,128)(2,1)S(1)} %bitcast.37), channel_id=1, source_target_pairs={{0,8},{2,10},{4,12},{6,14},{8,0},{10,2},{12,4},{14,6},{16,24},{18,... | collective-permute-start | bytes 270344 | tf_op jit(solution)/shard_map/ppermute | solution.py:543
  42.8 11.0 %copy-start.1 = (bf16[512,80]{0,1:T(8,128)(2,1)S(1)}, bf16[512,80]{0,1:T(8,128)(2,1)}, u32[]{:S(2)}) copy-start(bf16[512,80]{0,1:T(8,128)(2,1)} %param.25) | copy-start | bytes 245764
  51.0 10.7 %collective-permute-start.1 = (bf16[2,88,512]{2,1,0:T(8,128)(2,1)S(1)}, bf16[2,88,512]{2,1,0:T(8,128)(2,1)S(1)}, u32[]{:S(2)}, u32[]{:S(2)}) collective-permute-start(bf16[2,88,512]{2,1,0:T(8,128)(2,1)S(1)} %pad_maximum_fusion), channel_id=1, source_target_pairs={{0,16},{2,18},{4,20},{6,22},{8,24},{10,26},{12,28},{14,30},{16,0},... | collective-permute-start | bytes 540680 | tf_op jit(solution)/shard_map/ppermute | solution.py:543
  70.6 8.4 %collective-permute-start.2 = (bf16[336,256]{1,0:T(8,128)(2,1)S(1)}, bf16[336,256]{1,0:T(8,128)(2,1)S(1)}, u32[]{:S(2)}, u32[]{:S(2)}) collective-permute-start(bf16[336,256]{1,0:T(8,128)(2,1)S(1)} %get-tuple-element.59), channel_id=1, source_target_pairs={{0,2},{2,0},{4,6},{6,4},{8,10},{10,8},{12,14},{14,12},{16,18},{18,... | collective-permute-start | bytes 516104 | tf_op jit(solution)/shard_map/ppermute | solution.py:586
  72.1 9.5 %collective-permute-start.3 = (bf16[336,256]{1,0:T(8,128)(2,1)S(1)}, bf16[336,256]{1,0:T(8,128)(2,1)S(1)}, u32[]{:S(2)}, u32[]{:S(2)}) collective-permute-start(bf16[336,256]{1,0:T(8,128)(2,1)S(1)} %get-tuple-element.60), channel_id=1, source_target_pairs={{0,4},{2,6},{4,0},{6,2},{8,12},{10,14},{12,8},{14,10},{16,20},{18,... | collective-permute-start | bytes 516104 | tf_op jit(solution)/shard_map/ppermute | solution.py:586
  73.6 8.1 %collective-permute-start.4 = (bf16[336,256]{1,0:T(8,128)(2,1)S(1)}, bf16[336,256]{1,0:T(8,128)(2,1)S(1)}, u32[]{:S(2)}, u32[]{:S(2)}) collective-permute-start(bf16[336,256]{1,0:T(8,128)(2,1)S(1)} %get-tuple-element.61), channel_id=1, source_target_pairs={{0,6},{2,4},{4,2},{6,0},{8,14},{10,12},{12,10},{14,8},{16,22},{18,... | collective-permute-start | bytes 516104 | tf_op jit(solution)/shard_map/ppermute | solution.py:586
  74.4 1.0 %copy-start.7 = (bf16[512,512]{1,0:T(8,128)(2,1)S(1)}, bf16[512,512]{1,0:T(8,128)(2,1)}, u32[]{:S(2)}) copy-start(bf16[512,512]{1,0:T(8,128)(2,1)} %refs_3_.7) | copy-start | bytes 1572868
  75.4 1.0 %copy-start.14 = (f32[256,512]{1,0:T(8,128)S(1)}, f32[256,512]{1,0:T(8,128)}, u32[]{:S(2)}) copy-start(f32[256,512]{1,0:T(8,128)} %get-tuple-element.57) | copy-start | bytes 1572868
  76.4 1.0 %copy-start = (bf16[512,512]{1,0:T(8,128)(2,1)S(1)}, bf16[512,512]{1,0:T(8,128)(2,1)}, u32[]{:S(2)}) copy-start(bf16[512,512]{1,0:T(8,128)(2,1)} %refs_2_.7) | copy-start | bytes 1572868
  77.5 1.0 %copy-start.8 = (f32[256,512]{1,0:T(8,128)S(1)}, f32[256,512]{1,0:T(8,128)}, u32[]{:S(2)}) copy-start(f32[256,512]{1,0:T(8,128)} %get-tuple-element.56) | copy-start | bytes 1572868
  81.8 7.8 %collective-permute-start.7 = (bf16[336,256]{1,0:T(8,128)(2,1)S(1)}, bf16[336,256]{1,0:T(8,128)(2,1)S(1)}, u32[]{:S(2)}, u32[]{:S(2)}) collective-permute-start(bf16[336,256]{1,0:T(8,128)(2,1)S(1)} %add_convert_fusion.refs_4_), channel_id=1, source_target_pairs={{0,6},{2,4},{4,2},{6,0},{8,14},{10,12},{12,10},{14,8},{16,22},{18,... | collective-permute-start | bytes 516104 | tf_op jit(solution)/shard_map/ppermute | solution.py:588
  83.3 8.1 %collective-permute-start.6 = (bf16[336,256]{1,0:T(8,128)(2,1)S(1)}, bf16[336,256]{1,0:T(8,128)(2,1)S(1)}, u32[]{:S(2)}, u32[]{:S(2)}) collective-permute-start(bf16[336,256]{1,0:T(8,128)(2,1)S(1)} %add_convert_fusion.refs_4_), channel_id=1, source_target_pairs={{0,4},{2,6},{4,0},{6,2},{8,12},{10,14},{12,8},{14,10},{16,20},{18,... | collective-permute-start | bytes 516104 | tf_op jit(solution)/shard_map/ppermute | solution.py:588
  84.5 7.0 %collective-permute-start.5 = (bf16[336,256]{1,0:T(8,128)(2,1)S(1)}, bf16[336,256]{1,0:T(8,128)(2,1)S(1)}, u32[]{:S(2)}, u32[]{:S(2)}) collective-permute-start(bf16[336,256]{1,0:T(8,128)(2,1)S(1)} %add_convert_fusion.refs_4_), channel_id=1, source_target_pairs={{0,2},{2,0},{4,6},{6,4},{8,10},{10,8},{12,14},{14,12},{16,18},{18,... | collective-permute-start | bytes 516104 | tf_op jit(solution)/shard_map/ppermute | solution.py:588
  (2 other events, 1.3 us)

commit v7 on v6

--- a/solution.py
+++ b/solution.py
@@ -144,14 +144,15 @@
         copy.wait()
 
 
-def loss_kernel(
-    group, student_ref, pred_ref, target_ref, weight_ref, inverse_ref, recv_ref, out_ref, block_ref, sems
-):
+def loss_kernel(group, student_ref, target_ref, weight_ref, inverse_ref, recv_ref, *rest):
+    other_refs, (out_ref, block_ref, sems) = rest[:-3], rest[-3:]
     grid_rows = student_ref.shape[1]
     student = student_ref[...]
     terms = jnp.zeros_like(student)
-    for j in range(pred_ref.shape[0]):
-        terms = terms + slope(student - target_ref[j].astype(f32)) - slope(student - pred_ref[j])
+    for j in range(target_ref.shape[0]):
+        terms = terms + slope(student - target_ref[j].astype(f32))
+    for other_ref in (student_ref,) + other_refs:
+        terms = terms - slope(student - other_ref[...])
     scaled = (weight_ref[...].astype(f32) * terms * inverse_ref[...]).astype(bf16)
     order, crew = column_order(recv_ref, group)
     subs = lax.broadcasted_iota(jnp.int32, (grid_rows, LANES), 0).astype(f32)
@@ -557,7 +558,9 @@
     fill_map = (cell_ids[:, None] == dec_recv[0].reshape(-1)[None, :]).astype(bf16)
     inverse = 1.0 / jnp.maximum(jnp.sum(fill_map.astype(f32), axis=1), 1.0)
     student_outputs = scaled_atmosphere_field + mm(slot_values, fill_map, 0, 1) * inverse[None, :]
-    all_pred = lax.all_gather(student_outputs, "member", axis=0)
+    members = lax.axis_size("member")
+    turns = [[(m, (m + t) % members) for m in range(members)] for t in range(1, members)]
+    others = [lax.ppermute(student_outputs, "member", turn) for turn in turns]
     all_target = lax.all_gather(target[0], "member", axis=0)
     outgoing = vmem_call(
         functools.partial(loss_kernel, group),
@@ -565,7 +568,7 @@
         scratch=[((crew, channels, LANES), bf16)],
         sems=[(group,)],
         left_out=(0,),
-    )(None, student_outputs, all_pred, all_target, weight_map, inverse[None, :], dec_recv)[0]
+    )(None, student_outputs, all_target, weight_map, inverse[None, :], dec_recv, *others)[0]
     returned = all_to_all(outgoing)
     piece_rows = 2 * (width // crew) + channels
     node_grad, *pieces = vmem_call(

time: 94.5 us -> 94.7 us (level)
  blocking collectives: 3.91 us -> 1.85 us
  waiting for transfers between devices: 32.5 us -> 34.3 us
    all_gather x1 -> x0, blocking collectives: 2.06 us -> none  [column_body(): all_pred = lax.all_gather(student_outputs, 'member', axis=0)]
    all_to_all x2, waiting for transfers between devices: 5.14 us -> 6.99 us  [all_to_all(): return lax.all_to_all(x, 'band', split_axis=0, concat_axis=0, tiled=True)]
  transfers between devices with their start and end apart: 11 -> 12, of which waited for: 7 -> 7; matrix products, arithmetic and copies ran while one was open for 4% -> 4% of each run, Pallas kernels for 8% -> 8%
where the time goes in v7:
time: 94.7 us; the launch traced here: 93.8 us
  waiting for transfers between devices  34.3 us (36%)
  starting transfers between devices  27.6 us (29%)
  Pallas kernels  20.1 us (21%)
  local copies, waits for them, and re-layouts  4.71 us (5%)
  matrix products  2.43 us (3%)
  blocking collectives  1.85 us (2%)
  other arithmetic  1.82 us (2%)
    pallas_call x7, Pallas kernels, call(): pl.pallas_call(run, out_shape=[(pltpu.HBM if i in left_out else pltpu.VME...  20.1 us
    all_to_all x2, starting transfers between devices, all_to_all(): return lax.all_to_all(x, 'band', split_axis=0, concat_axis=0, tiled=True)  12 us
    ppermute x2, waiting for transfers between devices, column_body(): lax.ppermute(parcels, 'band', [(i, i ^ held * crew) for i in range(bands)])  11.8 us
    all_to_all x1, waiting for transfers between devices, exchange(): lax.all_to_all(x.reshape(band_count, rows // band_count, width), 'band',...  7.75 us
    all_to_all x2, waiting for transfers between devices, all_to_all(): return lax.all_to_all(x, 'band', split_axis=0, concat_axis=0, tiled=True)  6.99 us
    ppermute x3, waiting for transfers between devices, column_body(): totals = [total] + [lax.ppermute(total, 'band', swap) for swap in swaps]  5.15 us
    ppermute x2, starting transfers between devices, column_body(): lax.ppermute(parcels, 'band', [(i, i ^ held * crew) for i in range(bands)])  4.74 us
    unnamed x30, local copies, waits for them, and re-layouts  4.64 us
  transfers between devices with their start and end apart: 12, of which 7 were waited for; matrix products, arithmetic and copies ran while one was open for 4% of the time, Pallas kernels for 8%

profile of v7, /device:TPU:0, one launch (start us, length us, event | category | flops | bytes accessed | tf_op | source)
XLA Modules:
  0.0 93.8 jit_solution(14120747201181552170)
XLA Ops:
  0.6 2.5 %shard_map.172 = (bf16[16,32,80]{2,1,0:T(8,128)(2,1)}, f32[8,128]{1,0:T(8,128)S(1)}, bf16[80,512]{1,0:T(8,128)(2,1)S(1)}, bf16[512,512]{1,0:T(8,128)(2,1)S(1)}, ...) custom-call(f32[80,256]{1,0:T(8,128)} %refs_0_.3, bf16[1,80,256]{2,1,0:T(8,128)(2,1)} %refs_1_.1, ...), custom_call_target="tpu_custom_call" | custom-call | tf_op jit(solution)/shard_map/pallas_call | solution.py:433
  3.2 8.4 %all-to-all-start = ((bf16[16,32,80]{2,1,0:T(8,128)(2,1)}), bf16[16,32,80]{2,1,0:T(8,128)(2,1)S(1)}, u32[]{:S(2)}, u32[]{:S(2)}) async-start(bf16[16,32,80]{2,1,0:T(8,128)(2,1)} %get-tuple-element.36), calls=%async_computation | async-start | bytes 262144 | tf_op jit(solution)/shard_map/all_to_all | solution.py:462
  12.4 7.0 %all-to-all-done = bf16[16,32,80]{2,1,0:T(8,128)(2,1)S(1)} async-done(((bf16[16,32,80]{2,1,0:T(8,128)(2,1)}), bf16[16,32,80]{2,1,0:T(8,128)(2,1)S(1)}, u32[]{:S(2)}, u32[]{:S(2)}) %all-to-all-start) | async-done | bytes 81952 | tf_op jit(solution)/shard_map/all_to_all | solution.py:462
  19.3 2.5 %shard_map.173 = (bf16[512,80]{1,0:T(8,128)(2,1)}, bf16[88,512]{1,0:T(8,128)(2,1)}, f32[256,512]{1,0:T(8,128)}, f32[256,512]{1,0:T(8,128)}, bf16[256,512]{1,0:T(...) custom-call(bf16[512,80]{1,0:T(8,128)(2,1)S(1)} %bitcast.29, ...), custom_call_target="tpu_custom_call" | custom-call | tf_op jit(solution)/shard_map/pallas_call | solution.py:433
  21.9 3.7 %all-to-all-start.1 = ((bf16[16,32,80]{2,1,0:T(8,128)(2,1)}), bf16[16,32,80]{2,1,0:T(8,128)(2,1)S(1)}, u32[]{:S(2)}, u32[]{:S(2)}) async-start(bf16[16,32,80]{2,1,0:T(8,128)(2,1)} %bitcast.33), calls=%async_computation.1 | async-start | bytes 262144 | tf_op jit(solution)/shard_map/all_to_all | solution.py:42
  25.5 7.8 %all-to-all-done.1 = bf16[16,32,80]{2,1,0:T(8,128)(2,1)S(1)} async-done(((bf16[16,32,80]{2,1,0:T(8,128)(2,1)}), bf16[16,32,80]{2,1,0:T(8,128)(2,1)S(1)}, u32[]{:S(2)}, u32[]{:S(2)}) %all-to-all-start.1) | async-done | bytes 81952 | tf_op jit(solution)/shard_map/all_to_all | solution.py:42
  34.1 1.9 %all_gather.3.refs_1_ = bf16[2,80,256]{2,1,0:T(8,128)(2,1)S(1)} all-gather(bf16[1,80,256]{2,1,0:T(8,128)(2,1)S(1)} %copy-done.13), channel_id=1, replica_groups=mesh['band'=16,'member'=2] {'member'}, dimensions={0}, use_global_device_ids=true | all-gather | bytes 122880 | tf_op jit(solution)/shard_map/all_gather | solution.py:564
  35.9 1.4 %shard_map.174 = bf16[16,80,128]{2,1,0:T(8,128)(2,1)} custom-call(f32[80,256]{1,0:T(8,128)S(1)} %fusion.4.refs_0_, bf16[2,80,256]{2,1,0:T(8,128)(2,1)S(1)} %all_gather.3.refs_1_, bf16[80,256]{1,0:T(8,128)(2,1)S(1)} %copy-done.3, f32[1,256]{1,0:T(1,128)S(1)} %bitcast.32, s32[1,16,32]{2,1,0:T(8,128)S(1)} %copy-done.4, f32[80,256]{1,0:T(8,128)S(1)} %collective-permute-done.refs_5_), custom_call_target="tpu_custom_call" | custom-call | tf_op jit(solution)/shard_map/pallas_call | solution.py:433
  37.3 3.7 %all-to-all-start.2 = ((bf16[16,80,128]{2,1,0:T(8,128)(2,1)}), bf16[16,80,128]{2,1,0:T(8,128)(2,1)S(1)}, u32[]{:S(2)}, u32[]{:S(2)}) async-start(bf16[16,80,128]{2,1,0:T(8,128)(2,1)} %shard_map.174), calls=%async_computation.2 | async-start | bytes 655360 | tf_op jit(solution)/shard_map/all_to_all | solution.py:462
  41.1 1.9 %collective-permute-start.1 = (bf16[1,88,512]{2,1,0:T(8,128)(2,1)S(1)}, bf16[1,88,512]{2,1,0:T(8,128)(2,1)S(1)}, u32[]{:S(2)}, u32[]{:S(2)}) collective-permute-start(bf16[1,88,512]{2,1,0:T(8,128)(2,1)S(1)} %bitcast.35), channel_id=1, source_target_pairs={{0,8},{2,10},{4,12},{6,14},{8,0},{10,2},{12,4},{14,6},{16,24},{18,... | collective-permute-start | bytes 270344 | tf_op jit(solution)/shard_map/ppermute | solution.py:544
  43.0 7.5 %collective-permute-done.1.refs_4_ = bf16[1,88,512]{2,1,0:T(8,128)(2,1)S(1)} collective-permute-done((bf16[1,88,512]{2,1,0:T(8,128)(2,1)S(1)}, bf16[1,88,512]{2,1,0:T(8,128)(2,1)S(1)}, u32[]{:S(2)}, u32[]{:S(2)}) %collective-permute-start.1) | collective-permute-done | bytes 90144 | tf_op jit(solution)/shard_map/ppermute | solution.py:544
  51.2 2.9 %collective-permute-start.2 = (bf16[2,88,512]{2,1,0:T(8,128)(2,1)S(1)}, bf16[2,88,512]{2,1,0:T(8,128)(2,1)S(1)}, u32[]{:S(2)}, u32[]{:S(2)}) collective-permute-start(bf16[2,88,512]{2,1,0:T(8,128)(2,1)S(1)} %pad_maximum_fusion), channel_id=1, source_target_pairs={{0,16},{2,18},{4,20},{6,22},{8,24},{10,26},{12,28},{14,30},{16,0},... | collective-permute-start | bytes 540680 | tf_op jit(solution)/shard_map/ppermute | solution.py:544
  54.4 3.3 %shard_map.175 = (bf16[1,256,512]{2,1,0:T(8,128)(2,1)S(1)}, bf16[1,256,512]{2,1,0:T(8,128)(2,1)S(1)}, bf16[1,256,1024]{2,1,0:T(8,128)(2,1)}, f32[1,8,128]{2,1,0:T(8,128)S(1)}) custom-call(bf16[80,512]{1,0:T(8,128)(2,1)} %refs_0_.5, f32[1,512]{1,0:T(1,128)} %bitcast.38, bf16[512,512]{1,0:T(8,128)(2,1)} %refs_2_.9, bf16[512,512]{1,0:T(8,128)(2,1)} %refs_3_.5, ...), custom_call_target="tpu_custom_call" | custom-call | tf_op jit(solution)/shard_map/pallas_call | solution.py:433
  57.7 4.2 %collective-permute-done.2.refs_4_ = bf16[2,88,512]{2,1,0:T(8,128)(2,1)S(1)} collective-permute-done((bf16[2,88,512]{2,1,0:T(8,128)(2,1)S(1)}, bf16[2,88,512]{2,1,0:T(8,128)(2,1)S(1)}, u32[]{:S(2)}, u32[]{:S(2)}) %collective-permute-start.2) | collective-permute-done | bytes 180256 | tf_op jit(solution)/shard_map/ppermute | solution.py:544
  62.6 4.4 %shard_map.176 = (bf16[2,256,512]{2,1,0:T(8,128)(2,1)S(1)}, bf16[2,256,512]{2,1,0:T(8,128)(2,1)S(1)}, bf16[2,256,1024]{2,1,0:T(8,128)(2,1)}, f32[2,8,128]{2,1,0:T(8,128)S(1)}) custom-call(bf16[80,512]{1,0:T(8,128)(2,1)} %refs_0_.5, f32[1,512]{1,0:T(1,128)} %bitcast.39, bf16[512,512]{1,0:T(8,128)(2,1)} %refs_2_.9, bf16[512,512]{1,0:T(8,128)(2,1)} %refs_3_.5, ...), custom_call_target="tpu_custom_call" | custom-call | tf_op jit(solution)/shard_map/pallas_call | solution.py:433
  67.0 3.8 %shard_map.177 = (f32[256,80]{1,0:T(8,128)S(1)}, bf16[336,256]{1,0:T(8,128)(2,1)S(1)}, bf16[336,256]{1,0:T(8,128)(2,1)S(1)}, bf16[336,256]{1,0:T(8,128)(2,1)S(1)}, bf16[336,256]{1,0:T(8,128)(2,1)S(1)}) custom-call(s32[2]{0:T(128)S(1)} %pad_add_fusion.refs_0_, bf16[16,80,128]{2,1,0:T(8,128)(2,1)S(1)} %all-to-all-done.2.refs_1_, ...), custom_call_target="tpu_custom_call" | custom-call | tf_op jit(solution)/shard_map/pallas_call | solution.py:433
  70.8 1.5 %collective-permute-start.3 = (bf16[336,256]{1,0:T(8,128)(2,1)S(1)}, bf16[336,256]{1,0:T(8,128)(2,1)S(1)}, u32[]{:S(2)}, u32[]{:S(2)}) collective-permute-start(bf16[336,256]{1,0:T(8,128)(2,1)S(1)} %get-tuple-element.59), channel_id=1, source_target_pairs={{0,2},{2,0},{4,6},{6,4},{8,10},{10,8},{12,14},{14,12},{16,18},{18,... | collective-permute-start | bytes 516104 | tf_op jit(solution)/shard_map/ppermute | solution.py:589
  72.3 1.5 %collective-permute-start.4 = (bf16[336,256]{1,0:T(8,128)(2,1)S(1)}, bf16[336,256]{1,0:T(8,128)(2,1)S(1)}, u32[]{:S(2)}, u32[]{:S(2)}) collective-permute-start(bf16[336,256]{1,0:T(8,128)(2,1)S(1)} %get-tuple-element.60), channel_id=1, source_target_pairs={{0,4},{2,6},{4,0},{6,2},{8,12},{10,14},{12,8},{14,10},{16,20},{18,... | collective-permute-start | bytes 516104 | tf_op jit(solution)/shard_map/ppermute | solution.py:589
  79.2 2.6 %collective-permute-done.4 = bf16[336,256]{1,0:T(8,128)(2,1)S(1)} collective-permute-done((bf16[336,256]{1,0:T(8,128)(2,1)S(1)}, bf16[336,256]{1,0:T(8,128)(2,1)S(1)}, u32[]{:S(2)}, u32[]{:S(2)}) %collective-permute-start.4) | collective-permute-done | bytes 172064 | tf_op jit(solution)/shard_map/ppermute | solution.py:589
  82.0 1.5 %collective-permute-start.8 = (bf16[336,256]{1,0:T(8,128)(2,1)S(1)}, bf16[336,256]{1,0:T(8,128)(2,1)S(1)}, u32[]{:S(2)}, u32[]{:S(2)}) collective-permute-start(bf16[336,256]{1,0:T(8,128)(2,1)S(1)} %add_convert_fusion.refs_4_), channel_id=1, source_target_pairs={{0,6},{2,4},{4,2},{6,0},{8,14},{10,12},{12,10},{14,8},{16,22},{18,... | collective-permute-start | bytes 516104 | tf_op jit(solution)/shard_map/ppermute | solution.py:591
  83.5 1.2 %collective-permute-start.7 = (bf16[336,256]{1,0:T(8,128)(2,1)S(1)}, bf16[336,256]{1,0:T(8,128)(2,1)S(1)}, u32[]{:S(2)}, u32[]{:S(2)}) collective-permute-start(bf16[336,256]{1,0:T(8,128)(2,1)S(1)} %add_convert_fusion.refs_4_), channel_id=1, source_target_pairs={{0,4},{2,6},{4,0},{6,2},{8,12},{10,14},{12,8},{14,10},{16,20},{18,... | collective-permute-start | bytes 516104 | tf_op jit(solution)/shard_map/ppermute | solution.py:591
  86.4 3.3 %collective-permute-done.8.refs_7_ = bf16[336,256]{1,0:T(8,128)(2,1)S(1)} collective-permute-done((bf16[336,256]{1,0:T(8,128)(2,1)S(1)}, bf16[336,256]{1,0:T(8,128)(2,1)S(1)}, u32[]{:S(2)}, u32[]{:S(2)}) %collective-permute-start.8) | collective-permute-done | bytes 172064 | tf_op jit(solution)/shard_map/ppermute | solution.py:591
  89.7 1.8 %collective-permute-done.7.refs_6_ = bf16[336,256]{1,0:T(8,128)(2,1)S(1)} collective-permute-done((bf16[336,256]{1,0:T(8,128)(2,1)S(1)}, bf16[336,256]{1,0:T(8,128)(2,1)S(1)}, u32[]{:S(2)}, u32[]{:S(2)}) %collective-permute-start.7) | collective-permute-done | bytes 172064 | tf_op jit(solution)/shard_map/ppermute | solution.py:591
  91.6 2.3 %shard_map.178 = (f32[512,512]{1,0:T(8,128)}, f32[512,512]{1,0:T(8,128)}, f32[80,512]{1,0:T(8,128)}, f32[1,512]{1,0:T(1,128)}) custom-call(s32[2]{0:T(128)S(1)} %pad_add_fusion.refs_0_, f32[1,512]{1,0:T(1,128)S(1)} %bitcast.31, bf16[512,512]{1,0:T(8,128)(2,1)S(1)} %copy-done, bf16[80,512]{1,0:T(8,128)(2,1)S(1)} %bitcast.28, ...), custom_call_target="tpu_custom_call" | custom-call | tf_op jit(solution)/shard_map/pallas_call | solution.py:433
  (56 shorter events, 10.5 us)
Async XLA Ops:
  3.2 8.4 %copy-start.5 = (f32[512]{0:T(512)S(1)}, f32[512]{0:T(512)}, u32[]{:S(2)}) copy-start(f32[512]{0:T(512)} %param.22) | copy-start | bytes 6148
  3.2 9.0 %copy-start.4 = (s32[1,16,32]{2,1,0:T(8,128)S(1)}, s32[1,16,32]{2,1,0:T(8,128)}, u32[]{:S(2)}) copy-start(s32[1,16,32]{2,1,0:T(8,128)} %refs_4_.3) | copy-start | bytes 6148
  3.2 16.2 %all-to-all-start = ((bf16[16,32,80]{2,1,0:T(8,128)(2,1)}), bf16[16,32,80]{2,1,0:T(8,128)(2,1)S(1)}, u32[]{:S(2)}, u32[]{:S(2)}) async-start(bf16[16,32,80]{2,1,0:T(8,128)(2,1)} %get-tuple-element.36), calls=%async_computation | async-start | bytes 262144 | tf_op jit(solution)/shard_map/all_to_all | solution.py:462
  21.9 11.4 %copy-start.12 = (f32[80,256]{1,0:T(8,128)S(1)}, f32[80,256]{1,0:T(8,128)}, u32[]{:S(2)}) copy-start(f32[80,256]{1,0:T(8,128)} %refs_0_.3) | copy-start | bytes 245764
  21.9 11.4 %all-to-all-start.1 = ((bf16[16,32,80]{2,1,0:T(8,128)(2,1)}), bf16[16,32,80]{2,1,0:T(8,128)(2,1)S(1)}, u32[]{:S(2)}, u32[]{:S(2)}) async-start(bf16[16,32,80]{2,1,0:T(8,128)(2,1)} %bitcast.33), calls=%async_computation.1 | async-start | bytes 262144 | tf_op jit(solution)/shard_map/all_to_all | solution.py:42
  33.5 3.8 %copy-start.2 = (f32[80,256]{1,0:T(8,128)}, f32[80,256]{1,0:T(8,128)S(1)}, u32[]{:S(2)}) copy-start(f32[80,256]{1,0:T(8,128)S(1)} %fusion.4.refs_0_) | copy-start | bytes 245764
  33.5 2.4 %copy-start.3 = (bf16[80,256]{1,0:T(8,128)(2,1)S(1)}, bf16[80,256]{1,0:T(8,128)(2,1)}, u32[]{:S(2)}) copy-start(bf16[80,256]{1,0:T(8,128)(2,1)} %refs_2_.6) | copy-start | bytes 122884
  33.6 2.4 %collective-permute-start = (f32[80,256]{1,0:T(8,128)S(1)}, f32[80,256]{1,0:T(8,128)S(1)}, u32[]{:S(2)}, u32[]{:S(2)}) collective-permute-start(f32[80,256]{1,0:T(8,128)S(1)} %fusion.4.refs_0_), channel_id=1, source_target_pairs={{0,1},{1,0},{2,3},{3,2},{4,5},{5,4},{6,7},{7,6},{8,9},{9,8},{10,11... | collective-permute-start | bytes 245768 | tf_op jit(solution)/shard_map/ppermute | solution.py:563
  37.3 3.7 %copy-start.11 = (bf16[88,512]{1,0:T(8,128)(2,1)S(1)}, bf16[88,512]{1,0:T(8,128)(2,1)}, u32[]{:S(2)}) copy-start(bf16[88,512]{1,0:T(8,128)(2,1)} %get-tuple-element.46) | copy-start | bytes 270340
  37.3 16.7 %copy-start.6 = (bf16[512,512]{1,0:T(8,128)(2,1)S(1)}, bf16[512,512]{1,0:T(8,128)(2,1)}, u32[]{:S(2)}) copy-start(bf16[512,512]{1,0:T(8,128)(2,1)} %refs_3_.5) | copy-start | bytes 1572868
  37.3 29.6 %all-to-all-start.2 = ((bf16[16,80,128]{2,1,0:T(8,128)(2,1)}), bf16[16,80,128]{2,1,0:T(8,128)(2,1)S(1)}, u32[]{:S(2)}, u32[]{:S(2)}) async-start(bf16[16,80,128]{2,1,0:T(8,128)(2,1)} %shard_map.174), calls=%async_computation.2 | async-start | bytes 655360 | tf_op jit(solution)/shard_map/all_to_all | solution.py:462
  41.1 9.5 %collective-permute-start.1 = (bf16[1,88,512]{2,1,0:T(8,128)(2,1)S(1)}, bf16[1,88,512]{2,1,0:T(8,128)(2,1)S(1)}, u32[]{:S(2)}, u32[]{:S(2)}) collective-permute-start(bf16[1,88,512]{2,1,0:T(8,128)(2,1)S(1)} %bitcast.35), channel_id=1, source_target_pairs={{0,8},{2,10},{4,12},{6,14},{8,0},{10,2},{12,4},{14,6},{16,24},{18,... | collective-permute-start | bytes 270344 | tf_op jit(solution)/shard_map/ppermute | solution.py:544
  43.0 11.1 %copy-start.1 = (bf16[512,80]{0,1:T(8,128)(2,1)S(1)}, bf16[512,80]{0,1:T(8,128)(2,1)}, u32[]{:S(2)}) copy-start(bf16[512,80]{0,1:T(8,128)(2,1)} %param.25) | copy-start | bytes 245764
  51.2 10.7 %collective-permute-start.2 = (bf16[2,88,512]{2,1,0:T(8,128)(2,1)S(1)}, bf16[2,88,512]{2,1,0:T(8,128)(2,1)S(1)}, u32[]{:S(2)}, u32[]{:S(2)}) collective-permute-start(bf16[2,88,512]{2,1,0:T(8,128)(2,1)S(1)} %pad_maximum_fusion), channel_id=1, source_target_pairs={{0,16},{2,18},{4,20},{6,22},{8,24},{10,26},{12,28},{14,30},{16,0},... | collective-permute-start | bytes 540680 | tf_op jit(solution)/shard_map/ppermute | solution.py:544
  70.8 8.4 %collective-permute-start.3 = (bf16[336,256]{1,0:T(8,128)(2,1)S(1)}, bf16[336,256]{1,0:T(8,128)(2,1)S(1)}, u32[]{:S(2)}, u32[]{:S(2)}) collective-permute-start(bf16[336,256]{1,0:T(8,128)(2,1)S(1)} %get-tuple-element.59), channel_id=1, source_target_pairs={{0,2},{2,0},{4,6},{6,4},{8,10},{10,8},{12,14},{14,12},{16,18},{18,... | collective-permute-start | bytes 516104 | tf_op jit(solution)/shard_map/ppermute | solution.py:589
  72.3 9.5 %collective-permute-start.4 = (bf16[336,256]{1,0:T(8,128)(2,1)S(1)}, bf16[336,256]{1,0:T(8,128)(2,1)S(1)}, u32[]{:S(2)}, u32[]{:S(2)}) collective-permute-start(bf16[336,256]{1,0:T(8,128)(2,1)S(1)} %get-tuple-element.60), channel_id=1, source_target_pairs={{0,4},{2,6},{4,0},{6,2},{8,12},{10,14},{12,8},{14,10},{16,20},{18,... | collective-permute-start | bytes 516104 | tf_op jit(solution)/shard_map/ppermute | solution.py:589
  73.8 8.1 %collective-permute-start.5 = (bf16[336,256]{1,0:T(8,128)(2,1)S(1)}, bf16[336,256]{1,0:T(8,128)(2,1)S(1)}, u32[]{:S(2)}, u32[]{:S(2)}) collective-permute-start(bf16[336,256]{1,0:T(8,128)(2,1)S(1)} %get-tuple-element.61), channel_id=1, source_target_pairs={{0,6},{2,4},{4,2},{6,0},{8,14},{10,12},{12,10},{14,8},{16,22},{18,... | collective-permute-start | bytes 516104 | tf_op jit(solution)/shard_map/ppermute | solution.py:589
  74.6 1.0 %copy-start.7 = (bf16[512,512]{1,0:T(8,128)(2,1)S(1)}, bf16[512,512]{1,0:T(8,128)(2,1)}, u32[]{:S(2)}) copy-start(bf16[512,512]{1,0:T(8,128)(2,1)} %refs_3_.5) | copy-start | bytes 1572868
  75.6 1.0 %copy-start.14 = (f32[256,512]{1,0:T(8,128)S(1)}, f32[256,512]{1,0:T(8,128)}, u32[]{:S(2)}) copy-start(f32[256,512]{1,0:T(8,128)} %get-tuple-element.57) | copy-start | bytes 1572868
  76.6 1.0 %copy-start = (bf16[512,512]{1,0:T(8,128)(2,1)S(1)}, bf16[512,512]{1,0:T(8,128)(2,1)}, u32[]{:S(2)}) copy-start(bf16[512,512]{1,0:T(8,128)(2,1)} %refs_2_.9) | copy-start | bytes 1572868
  77.7 1.0 %copy-start.8 = (f32[256,512]{1,0:T(8,128)S(1)}, f32[256,512]{1,0:T(8,128)}, u32[]{:S(2)}) copy-start(f32[256,512]{1,0:T(8,128)} %get-tuple-element.56) | copy-start | bytes 1572868
  82.0 7.8 %collective-permute-start.8 = (bf16[336,256]{1,0:T(8,128)(2,1)S(1)}, bf16[336,256]{1,0:T(8,128)(2,1)S(1)}, u32[]{:S(2)}, u32[]{:S(2)}) collective-permute-start(bf16[336,256]{1,0:T(8,128)(2,1)S(1)} %add_convert_fusion.refs_4_), channel_id=1, source_target_pairs={{0,6},{2,4},{4,2},{6,0},{8,14},{10,12},{12,10},{14,8},{16,22},{18,... | collective-permute-start | bytes 516104 | tf_op jit(solution)/shard_map/ppermute | solution.py:591
  83.5 8.1 %collective-permute-start.7 = (bf16[336,256]{1,0:T(8,128)(2,1)S(1)}, bf16[336,256]{1,0:T(8,128)(2,1)S(1)}, u32[]{:S(2)}, u32[]{:S(2)}) collective-permute-start(bf16[336,256]{1,0:T(8,128)(2,1)S(1)} %add_convert_fusion.refs_4_), channel_id=1, source_target_pairs={{0,4},{2,6},{4,0},{6,2},{8,12},{10,14},{12,8},{14,10},{16,20},{18,... | collective-permute-start | bytes 516104 | tf_op jit(solution)/shard_map/ppermute | solution.py:591
  84.6 6.9 %collective-permute-start.6 = (bf16[336,256]{1,0:T(8,128)(2,1)S(1)}, bf16[336,256]{1,0:T(8,128)(2,1)S(1)}, u32[]{:S(2)}, u32[]{:S(2)}) collective-permute-start(bf16[336,256]{1,0:T(8,128)(2,1)S(1)} %add_convert_fusion.refs_4_), channel_id=1, source_target_pairs={{0,2},{2,0},{4,6},{6,4},{8,10},{10,8},{12,14},{14,12},{16,18},{18,... | collective-permute-start | bytes 516104 | tf_op jit(solution)/shard_map/ppermute | solution.py:591
  (3 other events, 2.1 us)

commit v8 on v7

--- a/solution.py
+++ b/solution.py
@@ -286,7 +286,6 @@
     group,
     channels,
     mate_count,
-    me_ref,
     grad_ref,
     chain_ref,
     table_ref,
@@ -301,7 +300,9 @@
     slots = value_ref.shape[1]
     node_rows = normed_ref.shape[0]
     cap = slots // bands
-    z, xy = me_ref[0], me_ref[1]
+    crew = grad_ref.shape[0] // group
+    band = lax.axis_index("band")
+    z, xy = band // crew, band % crew
     subs = lax.broadcasted_iota(jnp.int32, (node_rows, LANES), 0).astype(f32)
     held = [(table_ref[...], bend_ref, normed_ref, both_ref)]
     for at in range(0, mate_count, 4):
@@ -325,7 +326,7 @@
         value_ref[:, pl.ds(pl.multiple_of(b * cap, cap), cap), :] = values.reshape(group, cap, channels)
         return carry
 
-    lax.fori_loop(0, bands, turn, 0, unroll=4)
+    lax.fori_loop(0, bands, turn, 0, unroll=True)
     parts = slots // LANES
     for s in range(group):
         table = held[s][0]
@@ -358,7 +359,7 @@
         piece_ref[2 * rows :, :] = small_ref[:, pl.ds(pl.multiple_of(to * lanes, lanes), lanes)].astype(bf16)
 
 
-def finish_kernel(factor, me_ref, scale_ref, expand_ref, readout_ref, *rest):
+def finish_kernel(factor, scale_ref, expand_ref, readout_ref, *rest):
     count = len(rest) - 11
     piece_refs = rest[:count]
     up_out, down_out, dec_out, gain_out, small_ref, up_ref, down_ref, dec_ref, gain_ref, sems, last_sems = rest[count:]
@@ -366,7 +367,8 @@
     half = up_ref.shape[1] // 2
     lanes = small_ref.shape[1] // count
     width = up_ref.shape[0]
-    places = [pl.ds(pl.multiple_of((me_ref[1] ^ p) * rows, rows), rows) for p in range(count)]
+    xy = lax.axis_index("band") % count
+    places = [pl.ds(pl.multiple_of((xy ^ p) * rows, rows), rows) for p in range(count)]
     up_copies = [pltpu.make_async_copy(up_ref.at[at], up_out.at[at], sems.at[0, p]) for p, at in enumerate(places)]
     down_copies = [
         pltpu.make_async_copy(down_ref.at[at], down_out.at[at], sems.at[1, p])
@@ -376,7 +378,7 @@
         up_ref[places[p], 0:half] = piece_ref[0:rows, :].astype(f32) * factor
         up_ref[places[p], half:] = piece_ref[rows : 2 * rows, :].astype(f32) * factor
         up_copies[p].start()
-        at = pl.ds(pl.multiple_of((me_ref[1] ^ p) * lanes, lanes), lanes)
+        at = pl.ds(pl.multiple_of((xy ^ p) * lanes, lanes), lanes)
         small_ref[:, at] = piece_ref[2 * rows :, :].astype(f32) * factor
     dec_ref[...] = small_ref[:, 0:width]
     last_copies = [
@@ -509,8 +511,6 @@
     width, hid = expand_matrix.shape
     slots = bands * enc_send.shape[2]
     crew = bands // group
-    band = lax.axis_index("band").astype(jnp.int32)
-    me = jnp.stack([band // crew, band % crew])
     cell_ids = jnp.arange(grid_rows, dtype=jnp.int32)
     cap = enc_send.shape[2]
     block = ((bands, cap, channels), bf16)
@@ -584,7 +584,7 @@
         sems=[(3, group)],
         left_in=[3, 4, 5] + [6 + i for i in range(len(mates)) if i % 4 == 2],
         vmem_in=[6 + i for i in range(len(mates)) if i % 4 < 2],
-    )(me, returned, chain, table, normed, bend, both, *mates)
+    )(None, returned, chain, table, normed, bend, both, *mates)
     swaps = [[(i, i ^ p) for i in range(bands)] for p in range(1, crew)]
     others = [lax.ppermute(piece, "band", swap) for piece, swap in zip(pieces[1:], swaps)]
     total = sum(x.astype(f32) for x in [pieces[0]] + others).astype(bf16)
@@ -606,7 +606,7 @@
         scratch=[((channels, width + hid), f32)] + whole,
         sems=[(2, crew), (2,)],
         left_out=range(4),
-    )(me, mixing_rescale_factor[None, :], expand_matrix, readout_matrix.T, *totals)
+    )(None, mixing_rescale_factor[None, :], expand_matrix, readout_matrix.T, *totals)
     return (
         student_outputs[None],
         state_grad[None],

time: 94.7 us -> 93.6 us (0.988)
  Pallas kernels: 20.1 us -> 19.1 us
    pallas_call x7, Pallas kernels: 20.1 us -> 19.1 us  [call(): pl.pallas_call(run, out_shape=[(pltpu.HBM if i in left_out else pltpu.VME...]
where the time goes in v8:
time: 93.6 us; the launch traced here: 92.8 us
  waiting for transfers between devices  34.4 us (37%)
  starting transfers between devices  27.6 us (29%)
  Pallas kernels  19.1 us (20%)
  local copies, waits for them, and re-layouts  4.71 us (5%)
  matrix products  2.44 us (3%)
  blocking collectives  1.85 us (2%)
  other arithmetic  1.74 us (2%)
    pallas_call x7, Pallas kernels, call(): pl.pallas_call(run, out_shape=[(pltpu.HBM if i in left_out else pltpu.VME...  19.1 us
    all_to_all x2, starting transfers between devices, all_to_all(): return lax.all_to_all(x, 'band', split_axis=0, concat_axis=0, tiled=True)  12 us
    ppermute x2, waiting for transfers between devices, column_body(): lax.ppermute(parcels, 'band', [(i, i ^ held * crew) for i in range(bands)])  11.8 us
    all_to_all x1, waiting for transfers between devices, exchange(): lax.all_to_all(x.reshape(band_count, rows // band_count, width), 'band',...  7.75 us
    all_to_all x2, waiting for transfers between devices, all_to_all(): return lax.all_to_all(x, 'band', split_axis=0, concat_axis=0, tiled=True)  6.99 us
    ppermute x3, waiting for transfers between devices, column_body(): totals = [total] + [lax.ppermute(total, 'band', swap) for swap in swaps]  5.15 us
    ppermute x2, starting transfers between devices, column_body(): lax.ppermute(parcels, 'band', [(i, i ^ held * crew) for i in range(bands)])  4.76 us
    unnamed x30, local copies, waits for them, and re-layouts  4.63 us
  transfers between devices with their start and end apart: 12, of which 7 were waited for; matrix products, arithmetic and copies ran while one was open for 4% of the time, Pallas kernels for 8%

profile of v8, /device:TPU:0, one launch (start us, length us, event | category | flops | bytes accessed | tf_op | source)
XLA Modules:
  0.0 92.8 jit_solution(7782613464814127904)
XLA Ops:
  0.6 2.5 %shard_map.172 = (bf16[16,32,80]{2,1,0:T(8,128)(2,1)}, f32[8,128]{1,0:T(8,128)S(1)}, bf16[80,512]{1,0:T(8,128)(2,1)S(1)}, bf16[512,512]{1,0:T(8,128)(2,1)S(1)}, ...) custom-call(f32[80,256]{1,0:T(8,128)} %refs_0_.3, bf16[1,80,256]{2,1,0:T(8,128)(2,1)} %refs_1_.2, ...), custom_call_target="tpu_custom_call" | custom-call | tf_op jit(solution)/shard_map/pallas_call | solution.py:435
  3.2 8.4 %all-to-all-start = ((bf16[16,32,80]{2,1,0:T(8,128)(2,1)}), bf16[16,32,80]{2,1,0:T(8,128)(2,1)S(1)}, u32[]{:S(2)}, u32[]{:S(2)}) async-start(bf16[16,32,80]{2,1,0:T(8,128)(2,1)} %get-tuple-element.36), calls=%async_computation | async-start | bytes 262144 | tf_op jit(solution)/shard_map/all_to_all | solution.py:464
  12.4 7.0 %all-to-all-done = bf16[16,32,80]{2,1,0:T(8,128)(2,1)S(1)} async-done(((bf16[16,32,80]{2,1,0:T(8,128)(2,1)}), bf16[16,32,80]{2,1,0:T(8,128)(2,1)S(1)}, u32[]{:S(2)}, u32[]{:S(2)}) %all-to-all-start) | async-done | bytes 81952 | tf_op jit(solution)/shard_map/all_to_all | solution.py:464
  19.3 2.5 %shard_map.173 = (bf16[512,80]{1,0:T(8,128)(2,1)}, bf16[88,512]{1,0:T(8,128)(2,1)}, f32[256,512]{1,0:T(8,128)}, f32[256,512]{1,0:T(8,128)}, bf16[256,512]{1,0:T(...) custom-call(bf16[512,80]{1,0:T(8,128)(2,1)S(1)} %bitcast.27, ...), custom_call_target="tpu_custom_call" | custom-call | tf_op jit(solution)/shard_map/pallas_call | solution.py:435
  21.9 3.7 %all-to-all-start.1 = ((bf16[16,32,80]{2,1,0:T(8,128)(2,1)}), bf16[16,32,80]{2,1,0:T(8,128)(2,1)S(1)}, u32[]{:S(2)}, u32[]{:S(2)}) async-start(bf16[16,32,80]{2,1,0:T(8,128)(2,1)} %bitcast.31), calls=%async_computation.1 | async-start | bytes 262144 | tf_op jit(solution)/shard_map/all_to_all | solution.py:42
  25.5 7.8 %all-to-all-done.1 = bf16[16,32,80]{2,1,0:T(8,128)(2,1)S(1)} async-done(((bf16[16,32,80]{2,1,0:T(8,128)(2,1)}), bf16[16,32,80]{2,1,0:T(8,128)(2,1)S(1)}, u32[]{:S(2)}, u32[]{:S(2)}) %all-to-all-start.1) | async-done | bytes 81952 | tf_op jit(solution)/shard_map/all_to_all | solution.py:42
  34.1 1.9 %all_gather.3.refs_1_ = bf16[2,80,256]{2,1,0:T(8,128)(2,1)S(1)} all-gather(bf16[1,80,256]{2,1,0:T(8,128)(2,1)S(1)} %copy-done.13), channel_id=1, replica_groups=mesh['band'=16,'member'=2] {'member'}, dimensions={0}, use_global_device_ids=true | all-gather | bytes 122880 | tf_op jit(solution)/shard_map/all_gather | solution.py:564
  35.9 1.4 %shard_map.174 = bf16[16,80,128]{2,1,0:T(8,128)(2,1)} custom-call(f32[80,256]{1,0:T(8,128)S(1)} %fusion.4.refs_0_, bf16[2,80,256]{2,1,0:T(8,128)(2,1)S(1)} %all_gather.3.refs_1_, bf16[80,256]{1,0:T(8,128)(2,1)S(1)} %copy-done.3, f32[1,256]{1,0:T(1,128)S(1)} %bitcast.30, s32[1,16,32]{2,1,0:T(8,128)S(1)} %copy-done.4, f32[80,256]{1,0:T(8,128)S(1)} %collective-permute-done.refs_5_), custom_call_target="tpu_custom_call" | custom-call | tf_op jit(solution)/shard_map/pallas_call | solution.py:435
  37.3 3.7 %all-to-all-start.2 = ((bf16[16,80,128]{2,1,0:T(8,128)(2,1)}), bf16[16,80,128]{2,1,0:T(8,128)(2,1)S(1)}, u32[]{:S(2)}, u32[]{:S(2)}) async-start(bf16[16,80,128]{2,1,0:T(8,128)(2,1)} %shard_map.174), calls=%async_computation.2 | async-start | bytes 655360 | tf_op jit(solution)/shard_map/all_to_all | solution.py:464
  41.1 1.9 %collective-permute-start.1 = (bf16[1,88,512]{2,1,0:T(8,128)(2,1)S(1)}, bf16[1,88,512]{2,1,0:T(8,128)(2,1)S(1)}, u32[]{:S(2)}, u32[]{:S(2)}) collective-permute-start(bf16[1,88,512]{2,1,0:T(8,128)(2,1)S(1)} %bitcast.33), channel_id=1, source_target_pairs={{0,8},{2,10},{4,12},{6,14},{8,0},{10,2},{12,4},{14,6},{16,24},{18,... | collective-permute-start | bytes 270344 | tf_op jit(solution)/shard_map/ppermute | solution.py:544
  43.0 7.6 %collective-permute-done.1.refs_4_ = bf16[1,88,512]{2,1,0:T(8,128)(2,1)S(1)} collective-permute-done((bf16[1,88,512]{2,1,0:T(8,128)(2,1)S(1)}, bf16[1,88,512]{2,1,0:T(8,128)(2,1)S(1)}, u32[]{:S(2)}, u32[]{:S(2)}) %collective-permute-start.1) | collective-permute-done | bytes 90144 | tf_op jit(solution)/shard_map/ppermute | solution.py:544
  51.2 2.9 %collective-permute-start.2 = (bf16[2,88,512]{2,1,0:T(8,128)(2,1)S(1)}, bf16[2,88,512]{2,1,0:T(8,128)(2,1)S(1)}, u32[]{:S(2)}, u32[]{:S(2)}) collective-permute-start(bf16[2,88,512]{2,1,0:T(8,128)(2,1)S(1)} %pad_maximum_fusion), channel_id=1, source_target_pairs={{0,16},{2,18},{4,20},{6,22},{8,24},{10,26},{12,28},{14,30},{16,0},... | collective-permute-start | bytes 540680 | tf_op jit(solution)/shard_map/ppermute | solution.py:544
  54.4 3.3 %shard_map.175 = (bf16[1,256,512]{2,1,0:T(8,128)(2,1)S(1)}, bf16[1,256,512]{2,1,0:T(8,128)(2,1)S(1)}, bf16[1,256,1024]{2,1,0:T(8,128)(2,1)}, f32[1,8,128]{2,1,0:T(8,128)S(1)}) custom-call(bf16[80,512]{1,0:T(8,128)(2,1)} %refs_0_.5, f32[1,512]{1,0:T(1,128)} %bitcast.36, bf16[512,512]{1,0:T(8,128)(2,1)} %refs_1_.3, bf16[512,512]{1,0:T(8,128)(2,1)} %refs_3_.5, ...), custom_call_target="tpu_custom_call" | custom-call | tf_op jit(solution)/shard_map/pallas_call | solution.py:435
  57.7 4.2 %collective-permute-done.2.refs_4_ = bf16[2,88,512]{2,1,0:T(8,128)(2,1)S(1)} collective-permute-done((bf16[2,88,512]{2,1,0:T(8,128)(2,1)S(1)}, bf16[2,88,512]{2,1,0:T(8,128)(2,1)S(1)}, u32[]{:S(2)}, u32[]{:S(2)}) %collective-permute-start.2) | collective-permute-done | bytes 180256 | tf_op jit(solution)/shard_map/ppermute | solution.py:544
  62.6 4.4 %shard_map.176 = (bf16[2,256,512]{2,1,0:T(8,128)(2,1)S(1)}, bf16[2,256,512]{2,1,0:T(8,128)(2,1)S(1)}, bf16[2,256,1024]{2,1,0:T(8,128)(2,1)}, f32[2,8,128]{2,1,0:T(8,128)S(1)}) custom-call(bf16[80,512]{1,0:T(8,128)(2,1)} %refs_0_.5, f32[1,512]{1,0:T(1,128)} %bitcast.37, bf16[512,512]{1,0:T(8,128)(2,1)} %refs_1_.3, bf16[512,512]{1,0:T(8,128)(2,1)} %refs_3_.5, ...), custom_call_target="tpu_custom_call" | custom-call | tf_op jit(solution)/shard_map/pallas_call | solution.py:435
  67.0 3.2 %shard_map.177 = (f32[256,80]{1,0:T(8,128)S(1)}, bf16[336,256]{1,0:T(8,128)(2,1)S(1)}, bf16[336,256]{1,0:T(8,128)(2,1)S(1)}, bf16[336,256]{1,0:T(8,128)(2,1)S(1)}, bf16[336,256]{1,0:T(8,128)(2,1)S(1)}) custom-call(bf16[16,80,128]{2,1,0:T(8,128)(2,1)S(1)} %all-to-all-done.2.refs_0_, bf16[80,512]{1,0:T(8,128)(2,1)S(1)} %fusion.3.refs_1_, ...), custom_call_target="tpu_custom_call" | custom-call | tf_op jit(solution)/shard_map/pallas_call | solution.py:435
  70.3 1.5 %collective-permute-start.3 = (bf16[336,256]{1,0:T(8,128)(2,1)S(1)}, bf16[336,256]{1,0:T(8,128)(2,1)S(1)}, u32[]{:S(2)}, u32[]{:S(2)}) collective-permute-start(bf16[336,256]{1,0:T(8,128)(2,1)S(1)} %get-tuple-element.59), channel_id=1, source_target_pairs={{0,2},{2,0},{4,6},{6,4},{8,10},{10,8},{12,14},{14,12},{16,18},{18,... | collective-permute-start | bytes 516104 | tf_op jit(solution)/shard_map/ppermute | solution.py:589
  71.8 1.5 %collective-permute-start.4 = (bf16[336,256]{1,0:T(8,128)(2,1)S(1)}, bf16[336,256]{1,0:T(8,128)(2,1)S(1)}, u32[]{:S(2)}, u32[]{:S(2)}) collective-permute-start(bf16[336,256]{1,0:T(8,128)(2,1)S(1)} %get-tuple-element.60), channel_id=1, source_target_pairs={{0,4},{2,6},{4,0},{6,2},{8,12},{10,14},{12,8},{14,10},{16,20},{18,... | collective-permute-start | bytes 516104 | tf_op jit(solution)/shard_map/ppermute | solution.py:589
  78.7 2.6 %collective-permute-done.4 = bf16[336,256]{1,0:T(8,128)(2,1)S(1)} collective-permute-done((bf16[336,256]{1,0:T(8,128)(2,1)S(1)}, bf16[336,256]{1,0:T(8,128)(2,1)S(1)}, u32[]{:S(2)}, u32[]{:S(2)}) %collective-permute-start.4) | collective-permute-done | bytes 172064 | tf_op jit(solution)/shard_map/ppermute | solution.py:589
  81.4 1.5 %collective-permute-start.8 = (bf16[336,256]{1,0:T(8,128)(2,1)S(1)}, bf16[336,256]{1,0:T(8,128)(2,1)S(1)}, u32[]{:S(2)}, u32[]{:S(2)}) collective-permute-start(bf16[336,256]{1,0:T(8,128)(2,1)S(1)} %add_convert_fusion.refs_3_), channel_id=1, source_target_pairs={{0,6},{2,4},{4,2},{6,0},{8,14},{10,12},{12,10},{14,8},{16,22},{18,... | collective-permute-start | bytes 516104 | tf_op jit(solution)/shard_map/ppermute | solution.py:591
  82.9 1.2 %collective-permute-start.7 = (bf16[336,256]{1,0:T(8,128)(2,1)S(1)}, bf16[336,256]{1,0:T(8,128)(2,1)S(1)}, u32[]{:S(2)}, u32[]{:S(2)}) collective-permute-start(bf16[336,256]{1,0:T(8,128)(2,1)S(1)} %add_convert_fusion.refs_3_), channel_id=1, source_target_pairs={{0,4},{2,6},{4,0},{6,2},{8,12},{10,14},{12,8},{14,10},{16,20},{18,... | collective-permute-start | bytes 516104 | tf_op jit(solution)/shard_map/ppermute | solution.py:591
  85.9 3.3 %collective-permute-done.8.refs_6_ = bf16[336,256]{1,0:T(8,128)(2,1)S(1)} collective-permute-done((bf16[336,256]{1,0:T(8,128)(2,1)S(1)}, bf16[336,256]{1,0:T(8,128)(2,1)S(1)}, u32[]{:S(2)}, u32[]{:S(2)}) %collective-permute-start.8) | collective-permute-done | bytes 172064 | tf_op jit(solution)/shard_map/ppermute | solution.py:591
  89.2 1.8 %collective-permute-done.7.refs_5_ = bf16[336,256]{1,0:T(8,128)(2,1)S(1)} collective-permute-done((bf16[336,256]{1,0:T(8,128)(2,1)S(1)}, bf16[336,256]{1,0:T(8,128)(2,1)S(1)}, u32[]{:S(2)}, u32[]{:S(2)}) %collective-permute-start.7) | collective-permute-done | bytes 172064 | tf_op jit(solution)/shard_map/ppermute | solution.py:591
  91.0 1.7 %shard_map.178 = (f32[512,512]{1,0:T(8,128)}, f32[512,512]{1,0:T(8,128)}, f32[80,512]{1,0:T(8,128)}, f32[1,512]{1,0:T(1,128)}) custom-call(f32[1,512]{1,0:T(1,128)S(1)} %bitcast.29, bf16[512,512]{1,0:T(8,128)(2,1)S(1)} %copy-done, bf16[80,512]{1,0:T(8,128)(2,1)S(1)} %bitcast.26, bf16[336,256]{1,0:T(8,128)(2,1)S(1)} %add_convert_fusion.refs_3_, ...), custom_call_target="tpu_custom_call" | custom-call | tf_op jit(solution)/shard_map/pallas_call | solution.py:435
  (55 shorter events, 10.4 us)
Async XLA Ops:
  3.2 8.4 %copy-start.5 = (f32[512]{0:T(512)S(1)}, f32[512]{0:T(512)}, u32[]{:S(2)}) copy-start(f32[512]{0:T(512)} %param.22) | copy-start | bytes 6148
  3.2 9.0 %copy-start.4 = (s32[1,16,32]{2,1,0:T(8,128)S(1)}, s32[1,16,32]{2,1,0:T(8,128)}, u32[]{:S(2)}) copy-start(s32[1,16,32]{2,1,0:T(8,128)} %refs_4_.3) | copy-start | bytes 6148
  3.2 16.2 %all-to-all-start = ((bf16[16,32,80]{2,1,0:T(8,128)(2,1)}), bf16[16,32,80]{2,1,0:T(8,128)(2,1)S(1)}, u32[]{:S(2)}, u32[]{:S(2)}) async-start(bf16[16,32,80]{2,1,0:T(8,128)(2,1)} %get-tuple-element.36), calls=%async_computation | async-start | bytes 262144 | tf_op jit(solution)/shard_map/all_to_all | solution.py:464
  21.9 11.4 %copy-start.12 = (f32[80,256]{1,0:T(8,128)S(1)}, f32[80,256]{1,0:T(8,128)}, u32[]{:S(2)}) copy-start(f32[80,256]{1,0:T(8,128)} %refs_0_.3) | copy-start | bytes 245764
  21.9 11.4 %all-to-all-start.1 = ((bf16[16,32,80]{2,1,0:T(8,128)(2,1)}), bf16[16,32,80]{2,1,0:T(8,128)(2,1)S(1)}, u32[]{:S(2)}, u32[]{:S(2)}) async-start(bf16[16,32,80]{2,1,0:T(8,128)(2,1)} %bitcast.31), calls=%async_computation.1 | async-start | bytes 262144 | tf_op jit(solution)/shard_map/all_to_all | solution.py:42
  33.5 3.8 %copy-start.2 = (f32[80,256]{1,0:T(8,128)}, f32[80,256]{1,0:T(8,128)S(1)}, u32[]{:S(2)}) copy-start(f32[80,256]{1,0:T(8,128)S(1)} %fusion.4.refs_0_) | copy-start | bytes 245764
  33.5 2.4 %copy-start.3 = (bf16[80,256]{1,0:T(8,128)(2,1)S(1)}, bf16[80,256]{1,0:T(8,128)(2,1)}, u32[]{:S(2)}) copy-start(bf16[80,256]{1,0:T(8,128)(2,1)} %refs_2_.5) | copy-start | bytes 122884
  33.6 2.4 %collective-permute-start = (f32[80,256]{1,0:T(8,128)S(1)}, f32[80,256]{1,0:T(8,128)S(1)}, u32[]{:S(2)}, u32[]{:S(2)}) collective-permute-start(f32[80,256]{1,0:T(8,128)S(1)} %fusion.4.refs_0_), channel_id=1, source_target_pairs={{0,1},{1,0},{2,3},{3,2},{4,5},{5,4},{6,7},{7,6},{8,9},{9,8},{10,11... | collective-permute-start | bytes 245768 | tf_op jit(solution)/shard_map/ppermute | solution.py:563
  37.3 3.7 %copy-start.11 = (bf16[88,512]{1,0:T(8,128)(2,1)S(1)}, bf16[88,512]{1,0:T(8,128)(2,1)}, u32[]{:S(2)}) copy-start(bf16[88,512]{1,0:T(8,128)(2,1)} %get-tuple-element.46) | copy-start | bytes 270340
  37.3 16.7 %copy-start.6 = (bf16[512,512]{1,0:T(8,128)(2,1)S(1)}, bf16[512,512]{1,0:T(8,128)(2,1)}, u32[]{:S(2)}) copy-start(bf16[512,512]{1,0:T(8,128)(2,1)} %refs_3_.5) | copy-start | bytes 1572868
  37.3 29.6 %all-to-all-start.2 = ((bf16[16,80,128]{2,1,0:T(8,128)(2,1)}), bf16[16,80,128]{2,1,0:T(8,128)(2,1)S(1)}, u32[]{:S(2)}, u32[]{:S(2)}) async-start(bf16[16,80,128]{2,1,0:T(8,128)(2,1)} %shard_map.174), calls=%async_computation.2 | async-start | bytes 655360 | tf_op jit(solution)/shard_map/all_to_all | solution.py:464
  41.0 13.0 %copy-start.1 = (bf16[512,80]{0,1:T(8,128)(2,1)S(1)}, bf16[512,80]{0,1:T(8,128)(2,1)}, u32[]{:S(2)}) copy-start(bf16[512,80]{0,1:T(8,128)(2,1)} %param.25) | copy-start | bytes 245764
  41.1 9.5 %collective-permute-start.1 = (bf16[1,88,512]{2,1,0:T(8,128)(2,1)S(1)}, bf16[1,88,512]{2,1,0:T(8,128)(2,1)S(1)}, u32[]{:S(2)}, u32[]{:S(2)}) collective-permute-start(bf16[1,88,512]{2,1,0:T(8,128)(2,1)S(1)} %bitcast.33), channel_id=1, source_target_pairs={{0,8},{2,10},{4,12},{6,14},{8,0},{10,2},{12,4},{14,6},{16,24},{18,... | collective-permute-start | bytes 270344 | tf_op jit(solution)/shard_map/ppermute | solution.py:544
  51.2 10.7 %collective-permute-start.2 = (bf16[2,88,512]{2,1,0:T(8,128)(2,1)S(1)}, bf16[2,88,512]{2,1,0:T(8,128)(2,1)S(1)}, u32[]{:S(2)}, u32[]{:S(2)}) collective-permute-start(bf16[2,88,512]{2,1,0:T(8,128)(2,1)S(1)} %pad_maximum_fusion), channel_id=1, source_target_pairs={{0,16},{2,18},{4,20},{6,22},{8,24},{10,26},{12,28},{14,30},{16,0},... | collective-permute-start | bytes 540680 | tf_op jit(solution)/shard_map/ppermute | solution.py:544
  70.3 8.4 %collective-permute-start.3 = (bf16[336,256]{1,0:T(8,128)(2,1)S(1)}, bf16[336,256]{1,0:T(8,128)(2,1)S(1)}, u32[]{:S(2)}, u32[]{:S(2)}) collective-permute-start(bf16[336,256]{1,0:T(8,128)(2,1)S(1)} %get-tuple-element.59), channel_id=1, source_target_pairs={{0,2},{2,0},{4,6},{6,4},{8,10},{10,8},{12,14},{14,12},{16,18},{18,... | collective-permute-start | bytes 516104 | tf_op jit(solution)/shard_map/ppermute | solution.py:589
  71.8 9.5 %collective-permute-start.4 = (bf16[336,256]{1,0:T(8,128)(2,1)S(1)}, bf16[336,256]{1,0:T(8,128)(2,1)S(1)}, u32[]{:S(2)}, u32[]{:S(2)}) collective-permute-start(bf16[336,256]{1,0:T(8,128)(2,1)S(1)} %get-tuple-element.60), channel_id=1, source_target_pairs={{0,4},{2,6},{4,0},{6,2},{8,12},{10,14},{12,8},{14,10},{16,20},{18,... | collective-permute-start | bytes 516104 | tf_op jit(solution)/shard_map/ppermute | solution.py:589
  73.3 8.1 %collective-permute-start.5 = (bf16[336,256]{1,0:T(8,128)(2,1)S(1)}, bf16[336,256]{1,0:T(8,128)(2,1)S(1)}, u32[]{:S(2)}, u32[]{:S(2)}) collective-permute-start(bf16[336,256]{1,0:T(8,128)(2,1)S(1)} %get-tuple-element.61), channel_id=1, source_target_pairs={{0,6},{2,4},{4,2},{6,0},{8,14},{10,12},{12,10},{14,8},{16,22},{18,... | collective-permute-start | bytes 516104 | tf_op jit(solution)/shard_map/ppermute | solution.py:589
  74.0 1.0 %copy-start.7 = (bf16[512,512]{1,0:T(8,128)(2,1)S(1)}, bf16[512,512]{1,0:T(8,128)(2,1)}, u32[]{:S(2)}) copy-start(bf16[512,512]{1,0:T(8,128)(2,1)} %refs_3_.5) | copy-start | bytes 1572868
  75.1 1.0 %copy-start.14 = (f32[256,512]{1,0:T(8,128)S(1)}, f32[256,512]{1,0:T(8,128)}, u32[]{:S(2)}) copy-start(f32[256,512]{1,0:T(8,128)} %get-tuple-element.57) | copy-start | bytes 1572868
  76.1 1.0 %copy-start = (bf16[512,512]{1,0:T(8,128)(2,1)S(1)}, bf16[512,512]{1,0:T(8,128)(2,1)}, u32[]{:S(2)}) copy-start(bf16[512,512]{1,0:T(8,128)(2,1)} %refs_1_.3) | copy-start | bytes 1572868
  77.1 1.0 %copy-start.8 = (f32[256,512]{1,0:T(8,128)S(1)}, f32[256,512]{1,0:T(8,128)}, u32[]{:S(2)}) copy-start(f32[256,512]{1,0:T(8,128)} %get-tuple-element.56) | copy-start | bytes 1572868
  81.4 7.8 %collective-permute-start.8 = (bf16[336,256]{1,0:T(8,128)(2,1)S(1)}, bf16[336,256]{1,0:T(8,128)(2,1)S(1)}, u32[]{:S(2)}, u32[]{:S(2)}) collective-permute-start(bf16[336,256]{1,0:T(8,128)(2,1)S(1)} %add_convert_fusion.refs_3_), channel_id=1, source_target_pairs={{0,6},{2,4},{4,2},{6,0},{8,14},{10,12},{12,10},{14,8},{16,22},{18,... | collective-permute-start | bytes 516104 | tf_op jit(solution)/shard_map/ppermute | solution.py:591
  82.9 8.1 %collective-permute-start.7 = (bf16[336,256]{1,0:T(8,128)(2,1)S(1)}, bf16[336,256]{1,0:T(8,128)(2,1)S(1)}, u32[]{:S(2)}, u32[]{:S(2)}) collective-permute-start(bf16[336,256]{1,0:T(8,128)(2,1)S(1)} %add_convert_fusion.refs_3_), channel_id=1, source_target_pairs={{0,4},{2,6},{4,0},{6,2},{8,12},{10,14},{12,8},{14,10},{16,20},{18,... | collective-permute-start | bytes 516104 | tf_op jit(solution)/shard_map/ppermute | solution.py:591
  84.1 6.9 %collective-permute-start.6 = (bf16[336,256]{1,0:T(8,128)(2,1)S(1)}, bf16[336,256]{1,0:T(8,128)(2,1)S(1)}, u32[]{:S(2)}, u32[]{:S(2)}) collective-permute-start(bf16[336,256]{1,0:T(8,128)(2,1)S(1)} %add_convert_fusion.refs_3_), channel_id=1, source_target_pairs={{0,2},{2,0},{4,6},{6,4},{8,10},{10,8},{12,14},{14,12},{16,18},{18,... | collective-permute-start | bytes 516104 | tf_op jit(solution)/shard_map/ppermute | solution.py:591
  (3 other events, 2.1 us)

commit v9 on v8

--- a/solution.py
+++ b/solution.py
@@ -101,12 +101,14 @@
     send_ref,
     recv_ref,
     mesh_ref,
+    fill_ref,
     lift_in,
     expand_in,
     contract_in,
     readout_in,
     out_ref,
     table_ref,
+    order_ref,
     lift_ref,
     expand_ref,
     contract_ref,
@@ -121,7 +123,7 @@
     weights = [pltpu.make_async_copy(a, b, sems.at[i + 1]) for i, (a, b) in enumerate(pairs)]
     for copy in weights:
         copy.start()
-    ready(0, 1, 2, 3, 4)
+    ready(0, 1, 2, 3, 4, 5)
     inputs = (field_ref[...] + noise_ref[0].astype(f32)).astype(bf16) * 0.5
 
     def in_rows(ref, first):
@@ -140,11 +142,12 @@
     block_ref[...] = mm(inputs, pick, 1, 0).T.astype(bf16).reshape(block_ref.shape)
     copy = pltpu.make_async_copy(block_ref, out_ref, sems.at[0])
     copy.start()
+    order_ref[...] = column_order(fill_ref, group)[0]
     for copy in [copy] + weights:
         copy.wait()
 
 
-def loss_kernel(group, student_ref, target_ref, weight_ref, inverse_ref, recv_ref, *rest):
+def loss_kernel(group, student_ref, target_ref, weight_ref, inverse_ref, order_ref, *rest):
     other_refs, (out_ref, block_ref, sems) = rest[:-3], rest[-3:]
     grid_rows = student_ref.shape[1]
     student = student_ref[...]
@@ -154,7 +157,7 @@
     for other_ref in (student_ref,) + other_refs:
         terms = terms - slope(student - other_ref[...])
     scaled = (weight_ref[...].astype(f32) * terms * inverse_ref[...]).astype(bf16)
-    order, crew = column_order(recv_ref, group)
+    order, crew = order_ref[...], block_ref.shape[0]
     subs = lax.broadcasted_iota(jnp.int32, (grid_rows, LANES), 0).astype(f32)
     for c in range(crew):
         block_ref[c] = mm(scaled, one_hot(subs, order[c : c + 1, :]), 1, 0).astype(bf16)
@@ -515,16 +518,16 @@
     cap = enc_send.shape[2]
     block = ((bands, cap, channels), bf16)
     weights = (lattice_lift_matrix, expand_matrix, contract_matrix, readout_matrix.T)
-    outgoing, table, *near_weights = vmem_call(
+    outgoing, table, column_slots, *near_weights = vmem_call(
         functools.partial(encode_kernel, group),
-        [block, ((TABLE_ROWS, LANES), f32)] + [(w.shape, w.dtype) for w in weights],
+        [block, ((TABLE_ROWS, LANES), f32), ((8, LANES), f32)] + [(w.shape, w.dtype) for w in weights],
         scratch=[block],
         sems=[(5,)],
-        left_in=range(5, 9),
+        left_in=range(6, 10),
         left_out=(0,),
-        vmem_out=range(2, 6),
-        fetched=range(5),
-    )(None, scaled_atmosphere_field, perturbation, enc_send, enc_recv, dec_send, *weights)
+        vmem_out=range(3, 7),
+        fetched=range(6),
+    )(None, scaled_atmosphere_field, perturbation, enc_send, enc_recv, dec_send, dec_recv, *weights)
     arrived = all_to_all(outgoing).reshape(slots, channels)
     half_scale = 0.5 * mixing_rescale_factor[None, :]
     kept = [((node_rows, width), bf16), ((node_rows, hid), bf16), ((node_rows, width + hid), bf16)]
@@ -568,7 +571,7 @@
         scratch=[((crew, channels, LANES), bf16)],
         sems=[(group,)],
         left_out=(0,),
-    )(None, student_outputs, all_target, weight_map, inverse[None, :], dec_recv, *others)[0]
+    )(None, student_outputs, all_target, weight_map, inverse[None, :], column_slots, *others)[0]
     returned = all_to_all(outgoing)
     piece_rows = 2 * (width // crew) + channels
     node_grad, *pieces = vmem_call(

time: 93.6 us -> 93.4 us (level)
  no operation moved by 1% of the time
where the time goes in v9:
time: 93.4 us; the launch traced here: 92.5 us
  waiting for transfers between devices  34.4 us (37%)
  starting transfers between devices  27.6 us (30%)
  Pallas kernels  18.8 us (20%)
  local copies, waits for them, and re-layouts  4.72 us (5%)
  matrix products  2.43 us (3%)
  blocking collectives  1.85 us (2%)
  other arithmetic  1.74 us (2%)
    pallas_call x7, Pallas kernels, call(): pl.pallas_call(run, out_shape=[(pltpu.HBM if i in left_out else pltpu.VME...  18.8 us
    all_to_all x2, starting transfers between devices, all_to_all(): return lax.all_to_all(x, 'band', split_axis=0, concat_axis=0, tiled=True)  12 us
    ppermute x2, waiting for transfers between devices, column_body(): lax.ppermute(parcels, 'band', [(i, i ^ held * crew) for i in range(bands)])  11.9 us
    all_to_all x1, waiting for transfers between devices, exchange(): lax.all_to_all(x.reshape(band_count, rows // band_count, width), 'band',...  7.75 us
    all_to_all x2, waiting for transfers between devices, all_to_all(): return lax.all_to_all(x, 'band', split_axis=0, concat_axis=0, tiled=True)  6.99 us
    ppermute x3, waiting for transfers between devices, column_body(): totals = [total] + [lax.ppermute(total, 'band', swap) for swap in swaps]  5.15 us
    ppermute x2, starting transfers between devices, column_body(): lax.ppermute(parcels, 'band', [(i, i ^ held * crew) for i in range(bands)])  4.76 us
    unnamed x30, local copies, waits for them, and re-layouts  4.64 us
  transfers between devices with their start and end apart: 12, of which 7 were waited for; matrix products, arithmetic and copies ran while one was open for 4% of the time, Pallas kernels for 8%

profile of v9, /device:TPU:0, one launch (start us, length us, event | category | flops | bytes accessed | tf_op | source)
XLA Modules:
  0.0 92.5 jit_solution(7539136185764997772)
XLA Ops:
  0.6 2.6 %shard_map.172 = (bf16[16,32,80]{2,1,0:T(8,128)(2,1)}, f32[8,128]{1,0:T(8,128)S(1)}, f32[8,128]{1,0:T(8,128)S(1)}, bf16[80,512]{1,0:T(8,128)(2,1)S(1)}, bf16[512...) custom-call(f32[80,256]{1,0:T(8,128)} %refs_0_.3, bf16[1,80,256]{2,1,0:T(8,128)(2,1)} %refs_1_.2, ...), custom_call_target="tpu_custom_call" | custom-call | tf_op jit(solution)/shard_map/pallas_call | solution.py:438
  3.3 8.4 %all-to-all-start = ((bf16[16,32,80]{2,1,0:T(8,128)(2,1)}), bf16[16,32,80]{2,1,0:T(8,128)(2,1)S(1)}, u32[]{:S(2)}, u32[]{:S(2)}) async-start(bf16[16,32,80]{2,1,0:T(8,128)(2,1)} %get-tuple-element.37), calls=%async_computation | async-start | bytes 262144 | tf_op jit(solution)/shard_map/all_to_all | solution.py:467
  12.4 7.0 %all-to-all-done = bf16[16,32,80]{2,1,0:T(8,128)(2,1)S(1)} async-done(((bf16[16,32,80]{2,1,0:T(8,128)(2,1)}), bf16[16,32,80]{2,1,0:T(8,128)(2,1)S(1)}, u32[]{:S(2)}, u32[]{:S(2)}) %all-to-all-start) | async-done | bytes 81952 | tf_op jit(solution)/shard_map/all_to_all | solution.py:467
  19.4 2.5 %shard_map.173 = (bf16[512,80]{1,0:T(8,128)(2,1)}, bf16[88,512]{1,0:T(8,128)(2,1)}, f32[256,512]{1,0:T(8,128)}, f32[256,512]{1,0:T(8,128)}, bf16[256,512]{1,0:T(...) custom-call(bf16[512,80]{1,0:T(8,128)(2,1)S(1)} %bitcast.27, ...), custom_call_target="tpu_custom_call" | custom-call | tf_op jit(solution)/shard_map/pallas_call | solution.py:438
  21.9 3.7 %all-to-all-start.1 = ((bf16[16,32,80]{2,1,0:T(8,128)(2,1)}), bf16[16,32,80]{2,1,0:T(8,128)(2,1)S(1)}, u32[]{:S(2)}, u32[]{:S(2)}) async-start(bf16[16,32,80]{2,1,0:T(8,128)(2,1)} %bitcast.31), calls=%async_computation.1 | async-start | bytes 262144 | tf_op jit(solution)/shard_map/all_to_all | solution.py:42
  25.6 7.8 %all-to-all-done.1 = bf16[16,32,80]{2,1,0:T(8,128)(2,1)S(1)} async-done(((bf16[16,32,80]{2,1,0:T(8,128)(2,1)}), bf16[16,32,80]{2,1,0:T(8,128)(2,1)S(1)}, u32[]{:S(2)}, u32[]{:S(2)}) %all-to-all-start.1) | async-done | bytes 81952 | tf_op jit(solution)/shard_map/all_to_all | solution.py:42
  34.1 1.9 %all_gather.3.refs_1_ = bf16[2,80,256]{2,1,0:T(8,128)(2,1)S(1)} all-gather(bf16[1,80,256]{2,1,0:T(8,128)(2,1)S(1)} %copy-done.12), channel_id=1, replica_groups=mesh['band'=16,'member'=2] {'member'}, dimensions={0}, use_global_device_ids=true | all-gather | bytes 122880 | tf_op jit(solution)/shard_map/all_gather | solution.py:567
  36.0 1.1 %shard_map.174 = bf16[16,80,128]{2,1,0:T(8,128)(2,1)} custom-call(f32[80,256]{1,0:T(8,128)S(1)} %fusion.4.refs_0_, bf16[2,80,256]{2,1,0:T(8,128)(2,1)S(1)} %all_gather.3.refs_1_, bf16[80,256]{1,0:T(8,128)(2,1)S(1)} %copy-done.3, f32[1,256]{1,0:T(1,128)S(1)} %bitcast.30, f32[8,128]{1,0:T(8,128)S(1)} %get-tuple-element.44.refs_4_, ...), custom_call_target="tpu_custom_call" | custom-call | tf_op jit(solution)/shard_map/pallas_call | solution.py:438
  37.1 3.7 %all-to-all-start.2 = ((bf16[16,80,128]{2,1,0:T(8,128)(2,1)}), bf16[16,80,128]{2,1,0:T(8,128)(2,1)S(1)}, u32[]{:S(2)}, u32[]{:S(2)}) async-start(bf16[16,80,128]{2,1,0:T(8,128)(2,1)} %shard_map.174), calls=%async_computation.2 | async-start | bytes 655360 | tf_op jit(solution)/shard_map/all_to_all | solution.py:467
  40.8 1.9 %collective-permute-start.1 = (bf16[1,88,512]{2,1,0:T(8,128)(2,1)S(1)}, bf16[1,88,512]{2,1,0:T(8,128)(2,1)S(1)}, u32[]{:S(2)}, u32[]{:S(2)}) collective-permute-start(bf16[1,88,512]{2,1,0:T(8,128)(2,1)S(1)} %bitcast.33), channel_id=1, source_target_pairs={{0,8},{2,10},{4,12},{6,14},{8,0},{10,2},{12,4},{14,6},{16,24},{18,... | collective-permute-start | bytes 270344 | tf_op jit(solution)/shard_map/ppermute | solution.py:547
  42.7 7.6 %collective-permute-done.1.refs_4_ = bf16[1,88,512]{2,1,0:T(8,128)(2,1)S(1)} collective-permute-done((bf16[1,88,512]{2,1,0:T(8,128)(2,1)S(1)}, bf16[1,88,512]{2,1,0:T(8,128)(2,1)S(1)}, u32[]{:S(2)}, u32[]{:S(2)}) %collective-permute-start.1) | collective-permute-done | bytes 90144 | tf_op jit(solution)/shard_map/ppermute | solution.py:547
  50.9 2.9 %collective-permute-start.2 = (bf16[2,88,512]{2,1,0:T(8,128)(2,1)S(1)}, bf16[2,88,512]{2,1,0:T(8,128)(2,1)S(1)}, u32[]{:S(2)}, u32[]{:S(2)}) collective-permute-start(bf16[2,88,512]{2,1,0:T(8,128)(2,1)S(1)} %pad_maximum_fusion), channel_id=1, source_target_pairs={{0,16},{2,18},{4,20},{6,22},{8,24},{10,26},{12,28},{14,30},{16,0},... | collective-permute-start | bytes 540680 | tf_op jit(solution)/shard_map/ppermute | solution.py:547
  54.1 3.3 %shard_map.175 = (bf16[1,256,512]{2,1,0:T(8,128)(2,1)S(1)}, bf16[1,256,512]{2,1,0:T(8,128)(2,1)S(1)}, bf16[1,256,1024]{2,1,0:T(8,128)(2,1)}, f32[1,8,128]{2,1,0:T(8,128)S(1)}) custom-call(bf16[80,512]{1,0:T(8,128)(2,1)} %refs_0_.5, f32[1,512]{1,0:T(1,128)} %bitcast.36, bf16[512,512]{1,0:T(8,128)(2,1)} %refs_1_.3, bf16[512,512]{1,0:T(8,128)(2,1)} %refs_3_.5, ...), custom_call_target="tpu_custom_call" | custom-call | tf_op jit(solution)/shard_map/pallas_call | solution.py:438
  57.5 4.2 %collective-permute-done.2.refs_4_ = bf16[2,88,512]{2,1,0:T(8,128)(2,1)S(1)} collective-permute-done((bf16[2,88,512]{2,1,0:T(8,128)(2,1)S(1)}, bf16[2,88,512]{2,1,0:T(8,128)(2,1)S(1)}, u32[]{:S(2)}, u32[]{:S(2)}) %collective-permute-start.2) | collective-permute-done | bytes 180256 | tf_op jit(solution)/shard_map/ppermute | solution.py:547
  62.4 4.4 %shard_map.176 = (bf16[2,256,512]{2,1,0:T(8,128)(2,1)S(1)}, bf16[2,256,512]{2,1,0:T(8,128)(2,1)S(1)}, bf16[2,256,1024]{2,1,0:T(8,128)(2,1)}, f32[2,8,128]{2,1,0:T(8,128)S(1)}) custom-call(bf16[80,512]{1,0:T(8,128)(2,1)} %refs_0_.5, f32[1,512]{1,0:T(1,128)} %bitcast.37, bf16[512,512]{1,0:T(8,128)(2,1)} %refs_1_.3, bf16[512,512]{1,0:T(8,128)(2,1)} %refs_3_.5, ...), custom_call_target="tpu_custom_call" | custom-call | tf_op jit(solution)/shard_map/pallas_call | solution.py:438
  66.8 3.3 %shard_map.177 = (f32[256,80]{1,0:T(8,128)S(1)}, bf16[336,256]{1,0:T(8,128)(2,1)S(1)}, bf16[336,256]{1,0:T(8,128)(2,1)S(1)}, bf16[336,256]{1,0:T(8,128)(2,1)S(1)}, bf16[336,256]{1,0:T(8,128)(2,1)S(1)}) custom-call(bf16[16,80,128]{2,1,0:T(8,128)(2,1)S(1)} %all-to-all-done.2.refs_0_, bf16[80,512]{1,0:T(8,128)(2,1)S(1)} %fusion.3.refs_1_, ...), custom_call_target="tpu_custom_call" | custom-call | tf_op jit(solution)/shard_map/pallas_call | solution.py:438
  70.0 1.5 %collective-permute-start.3 = (bf16[336,256]{1,0:T(8,128)(2,1)S(1)}, bf16[336,256]{1,0:T(8,128)(2,1)S(1)}, u32[]{:S(2)}, u32[]{:S(2)}) collective-permute-start(bf16[336,256]{1,0:T(8,128)(2,1)S(1)} %get-tuple-element.61), channel_id=1, source_target_pairs={{0,2},{2,0},{4,6},{6,4},{8,10},{10,8},{12,14},{14,12},{16,18},{18,... | collective-permute-start | bytes 516104 | tf_op jit(solution)/shard_map/ppermute | solution.py:592
  71.6 1.5 %collective-permute-start.4 = (bf16[336,256]{1,0:T(8,128)(2,1)S(1)}, bf16[336,256]{1,0:T(8,128)(2,1)S(1)}, u32[]{:S(2)}, u32[]{:S(2)}) collective-permute-start(bf16[336,256]{1,0:T(8,128)(2,1)S(1)} %get-tuple-element.62), channel_id=1, source_target_pairs={{0,4},{2,6},{4,0},{6,2},{8,12},{10,14},{12,8},{14,10},{16,20},{18,... | collective-permute-start | bytes 516104 | tf_op jit(solution)/shard_map/ppermute | solution.py:592
  78.4 2.7 %collective-permute-done.4 = bf16[336,256]{1,0:T(8,128)(2,1)S(1)} collective-permute-done((bf16[336,256]{1,0:T(8,128)(2,1)S(1)}, bf16[336,256]{1,0:T(8,128)(2,1)S(1)}, u32[]{:S(2)}, u32[]{:S(2)}) %collective-permute-start.4) | collective-permute-done | bytes 172064 | tf_op jit(solution)/shard_map/ppermute | solution.py:592
  81.2 1.5 %collective-permute-start.8 = (bf16[336,256]{1,0:T(8,128)(2,1)S(1)}, bf16[336,256]{1,0:T(8,128)(2,1)S(1)}, u32[]{:S(2)}, u32[]{:S(2)}) collective-permute-start(bf16[336,256]{1,0:T(8,128)(2,1)S(1)} %add_convert_fusion.refs_3_), channel_id=1, source_target_pairs={{0,6},{2,4},{4,2},{6,0},{8,14},{10,12},{12,10},{14,8},{16,22},{18,... | collective-permute-start | bytes 516104 | tf_op jit(solution)/shard_map/ppermute | solution.py:594
  82.7 1.2 %collective-permute-start.7 = (bf16[336,256]{1,0:T(8,128)(2,1)S(1)}, bf16[336,256]{1,0:T(8,128)(2,1)S(1)}, u32[]{:S(2)}, u32[]{:S(2)}) collective-permute-start(bf16[336,256]{1,0:T(8,128)(2,1)S(1)} %add_convert_fusion.refs_3_), channel_id=1, source_target_pairs={{0,4},{2,6},{4,0},{6,2},{8,12},{10,14},{12,8},{14,10},{16,20},{18,... | collective-permute-start | bytes 516104 | tf_op jit(solution)/shard_map/ppermute | solution.py:594
  85.6 3.3 %collective-permute-done.8.refs_6_ = bf16[336,256]{1,0:T(8,128)(2,1)S(1)} collective-permute-done((bf16[336,256]{1,0:T(8,128)(2,1)S(1)}, bf16[336,256]{1,0:T(8,128)(2,1)S(1)}, u32[]{:S(2)}, u32[]{:S(2)}) %collective-permute-start.8) | collective-permute-done | bytes 172064 | tf_op jit(solution)/shard_map/ppermute | solution.py:594
  88.9 1.8 %collective-permute-done.7.refs_5_ = bf16[336,256]{1,0:T(8,128)(2,1)S(1)} collective-permute-done((bf16[336,256]{1,0:T(8,128)(2,1)S(1)}, bf16[336,256]{1,0:T(8,128)(2,1)S(1)}, u32[]{:S(2)}, u32[]{:S(2)}) %collective-permute-start.7) | collective-permute-done | bytes 172064 | tf_op jit(solution)/shard_map/ppermute | solution.py:594
  90.8 1.7 %shard_map.178 = (f32[512,512]{1,0:T(8,128)}, f32[512,512]{1,0:T(8,128)}, f32[80,512]{1,0:T(8,128)}, f32[1,512]{1,0:T(1,128)}) custom-call(f32[1,512]{1,0:T(1,128)S(1)} %bitcast.29, bf16[512,512]{1,0:T(8,128)(2,1)S(1)} %copy-done, bf16[80,512]{1,0:T(8,128)(2,1)S(1)} %bitcast.26, bf16[336,256]{1,0:T(8,128)(2,1)S(1)} %add_convert_fusion.refs_3_, ...), custom_call_target="tpu_custom_call" | custom-call | tf_op jit(solution)/shard_map/pallas_call | solution.py:438
  (55 shorter events, 10.4 us)
Async XLA Ops:
  3.2 8.4 %copy-start.4 = (f32[512]{0:T(512)S(1)}, f32[512]{0:T(512)}, u32[]{:S(2)}) copy-start(f32[512]{0:T(512)} %param.22) | copy-start | bytes 6148
  3.3 9.0 %copy-start.13 = (s32[1,16,32]{2,1,0:T(8,128)S(1)}, s32[1,16,32]{2,1,0:T(8,128)}, u32[]{:S(2)}) copy-start(s32[1,16,32]{2,1,0:T(8,128)} %refs_5_.1) | copy-start | bytes 6148
  3.3 16.2 %all-to-all-start = ((bf16[16,32,80]{2,1,0:T(8,128)(2,1)}), bf16[16,32,80]{2,1,0:T(8,128)(2,1)S(1)}, u32[]{:S(2)}, u32[]{:S(2)}) async-start(bf16[16,32,80]{2,1,0:T(8,128)(2,1)} %get-tuple-element.37), calls=%async_computation | async-start | bytes 262144 | tf_op jit(solution)/shard_map/all_to_all | solution.py:467
  21.9 11.4 %copy-start.11 = (f32[80,256]{1,0:T(8,128)S(1)}, f32[80,256]{1,0:T(8,128)}, u32[]{:S(2)}) copy-start(f32[80,256]{1,0:T(8,128)} %refs_0_.3) | copy-start | bytes 245764
  21.9 11.4 %all-to-all-start.1 = ((bf16[16,32,80]{2,1,0:T(8,128)(2,1)}), bf16[16,32,80]{2,1,0:T(8,128)(2,1)S(1)}, u32[]{:S(2)}, u32[]{:S(2)}) async-start(bf16[16,32,80]{2,1,0:T(8,128)(2,1)} %bitcast.31), calls=%async_computation.1 | async-start | bytes 262144 | tf_op jit(solution)/shard_map/all_to_all | solution.py:42
  33.6 3.5 %copy-start.2 = (f32[80,256]{1,0:T(8,128)}, f32[80,256]{1,0:T(8,128)S(1)}, u32[]{:S(2)}) copy-start(f32[80,256]{1,0:T(8,128)S(1)} %fusion.4.refs_0_) | copy-start | bytes 245764
  33.6 2.4 %copy-start.3 = (bf16[80,256]{1,0:T(8,128)(2,1)S(1)}, bf16[80,256]{1,0:T(8,128)(2,1)}, u32[]{:S(2)}) copy-start(bf16[80,256]{1,0:T(8,128)(2,1)} %refs_2_.5) | copy-start | bytes 122884
  33.6 2.4 %collective-permute-start = (f32[80,256]{1,0:T(8,128)S(1)}, f32[80,256]{1,0:T(8,128)S(1)}, u32[]{:S(2)}, u32[]{:S(2)}) collective-permute-start(f32[80,256]{1,0:T(8,128)S(1)} %fusion.4.refs_0_), channel_id=1, source_target_pairs={{0,1},{1,0},{2,3},{3,2},{4,5},{5,4},{6,7},{7,6},{8,9},{9,8},{10,11... | collective-permute-start | bytes 245768 | tf_op jit(solution)/shard_map/ppermute | solution.py:566
  37.1 3.7 %copy-start.10 = (bf16[88,512]{1,0:T(8,128)(2,1)S(1)}, bf16[88,512]{1,0:T(8,128)(2,1)}, u32[]{:S(2)}) copy-start(bf16[88,512]{1,0:T(8,128)(2,1)} %get-tuple-element.48) | copy-start | bytes 270340
  37.1 16.7 %copy-start.5 = (bf16[512,512]{1,0:T(8,128)(2,1)S(1)}, bf16[512,512]{1,0:T(8,128)(2,1)}, u32[]{:S(2)}) copy-start(bf16[512,512]{1,0:T(8,128)(2,1)} %refs_3_.5) | copy-start | bytes 1572868
  37.1 29.7 %all-to-all-start.2 = ((bf16[16,80,128]{2,1,0:T(8,128)(2,1)}), bf16[16,80,128]{2,1,0:T(8,128)(2,1)S(1)}, u32[]{:S(2)}, u32[]{:S(2)}) async-start(bf16[16,80,128]{2,1,0:T(8,128)(2,1)} %shard_map.174), calls=%async_computation.2 | async-start | bytes 655360 | tf_op jit(solution)/shard_map/all_to_all | solution.py:467
  40.8 13.0 %copy-start.1 = (bf16[512,80]{0,1:T(8,128)(2,1)S(1)}, bf16[512,80]{0,1:T(8,128)(2,1)}, u32[]{:S(2)}) copy-start(bf16[512,80]{0,1:T(8,128)(2,1)} %param.25) | copy-start | bytes 245764
  40.8 9.5 %collective-permute-start.1 = (bf16[1,88,512]{2,1,0:T(8,128)(2,1)S(1)}, bf16[1,88,512]{2,1,0:T(8,128)(2,1)S(1)}, u32[]{:S(2)}, u32[]{:S(2)}) collective-permute-start(bf16[1,88,512]{2,1,0:T(8,128)(2,1)S(1)} %bitcast.33), channel_id=1, source_target_pairs={{0,8},{2,10},{4,12},{6,14},{8,0},{10,2},{12,4},{14,6},{16,24},{18,... | collective-permute-start | bytes 270344 | tf_op jit(solution)/shard_map/ppermute | solution.py:547
  50.9 10.8 %collective-permute-start.2 = (bf16[2,88,512]{2,1,0:T(8,128)(2,1)S(1)}, bf16[2,88,512]{2,1,0:T(8,128)(2,1)S(1)}, u32[]{:S(2)}, u32[]{:S(2)}) collective-permute-start(bf16[2,88,512]{2,1,0:T(8,128)(2,1)S(1)} %pad_maximum_fusion), channel_id=1, source_target_pairs={{0,16},{2,18},{4,20},{6,22},{8,24},{10,26},{12,28},{14,30},{16,0},... | collective-permute-start | bytes 540680 | tf_op jit(solution)/shard_map/ppermute | solution.py:547
  70.0 8.4 %collective-permute-start.3 = (bf16[336,256]{1,0:T(8,128)(2,1)S(1)}, bf16[336,256]{1,0:T(8,128)(2,1)S(1)}, u32[]{:S(2)}, u32[]{:S(2)}) collective-permute-start(bf16[336,256]{1,0:T(8,128)(2,1)S(1)} %get-tuple-element.61), channel_id=1, source_target_pairs={{0,2},{2,0},{4,6},{6,4},{8,10},{10,8},{12,14},{14,12},{16,18},{18,... | collective-permute-start | bytes 516104 | tf_op jit(solution)/shard_map/ppermute | solution.py:592
  71.6 9.5 %collective-permute-start.4 = (bf16[336,256]{1,0:T(8,128)(2,1)S(1)}, bf16[336,256]{1,0:T(8,128)(2,1)S(1)}, u32[]{:S(2)}, u32[]{:S(2)}) collective-permute-start(bf16[336,256]{1,0:T(8,128)(2,1)S(1)} %get-tuple-element.62), channel_id=1, source_target_pairs={{0,4},{2,6},{4,0},{6,2},{8,12},{10,14},{12,8},{14,10},{16,20},{18,... | collective-permute-start | bytes 516104 | tf_op jit(solution)/shard_map/ppermute | solution.py:592
  73.0 8.1 %collective-permute-start.5 = (bf16[336,256]{1,0:T(8,128)(2,1)S(1)}, bf16[336,256]{1,0:T(8,128)(2,1)S(1)}, u32[]{:S(2)}, u32[]{:S(2)}) collective-permute-start(bf16[336,256]{1,0:T(8,128)(2,1)S(1)} %get-tuple-element.63), channel_id=1, source_target_pairs={{0,6},{2,4},{4,2},{6,0},{8,14},{10,12},{12,10},{14,8},{16,22},{18,... | collective-permute-start | bytes 516104 | tf_op jit(solution)/shard_map/ppermute | solution.py:592
  73.8 1.0 %copy-start.6 = (bf16[512,512]{1,0:T(8,128)(2,1)S(1)}, bf16[512,512]{1,0:T(8,128)(2,1)}, u32[]{:S(2)}) copy-start(bf16[512,512]{1,0:T(8,128)(2,1)} %refs_3_.5) | copy-start | bytes 1572868
  74.8 1.0 %copy-start.14 = (f32[256,512]{1,0:T(8,128)S(1)}, f32[256,512]{1,0:T(8,128)}, u32[]{:S(2)}) copy-start(f32[256,512]{1,0:T(8,128)} %get-tuple-element.59) | copy-start | bytes 1572868
  75.9 1.0 %copy-start = (bf16[512,512]{1,0:T(8,128)(2,1)S(1)}, bf16[512,512]{1,0:T(8,128)(2,1)}, u32[]{:S(2)}) copy-start(bf16[512,512]{1,0:T(8,128)(2,1)} %refs_1_.3) | copy-start | bytes 1572868
  76.9 1.0 %copy-start.7 = (f32[256,512]{1,0:T(8,128)S(1)}, f32[256,512]{1,0:T(8,128)}, u32[]{:S(2)}) copy-start(f32[256,512]{1,0:T(8,128)} %get-tuple-element.58) | copy-start | bytes 1572868
  81.2 7.8 %collective-permute-start.8 = (bf16[336,256]{1,0:T(8,128)(2,1)S(1)}, bf16[336,256]{1,0:T(8,128)(2,1)S(1)}, u32[]{:S(2)}, u32[]{:S(2)}) collective-permute-start(bf16[336,256]{1,0:T(8,128)(2,1)S(1)} %add_convert_fusion.refs_3_), channel_id=1, source_target_pairs={{0,6},{2,4},{4,2},{6,0},{8,14},{10,12},{12,10},{14,8},{16,22},{18,... | collective-permute-start | bytes 516104 | tf_op jit(solution)/shard_map/ppermute | solution.py:594
  82.7 8.1 %collective-permute-start.7 = (bf16[336,256]{1,0:T(8,128)(2,1)S(1)}, bf16[336,256]{1,0:T(8,128)(2,1)S(1)}, u32[]{:S(2)}, u32[]{:S(2)}) collective-permute-start(bf16[336,256]{1,0:T(8,128)(2,1)S(1)} %add_convert_fusion.refs_3_), channel_id=1, source_target_pairs={{0,4},{2,6},{4,0},{6,2},{8,12},{10,14},{12,8},{14,10},{16,20},{18,... | collective-permute-start | bytes 516104 | tf_op jit(solution)/shard_map/ppermute | solution.py:594
  83.9 6.9 %collective-permute-start.6 = (bf16[336,256]{1,0:T(8,128)(2,1)S(1)}, bf16[336,256]{1,0:T(8,128)(2,1)S(1)}, u32[]{:S(2)}, u32[]{:S(2)}) collective-permute-start(bf16[336,256]{1,0:T(8,128)(2,1)S(1)} %add_convert_fusion.refs_3_), channel_id=1, source_target_pairs={{0,2},{2,0},{4,6},{6,4},{8,10},{10,8},{12,14},{14,12},{16,18},{18,... | collective-permute-start | bytes 516104 | tf_op jit(solution)/shard_map/ppermute | solution.py:594
  (3 other events, 2.1 us)
